TPU v7x, 32 devices: a whole 2x2x4 slice. The times are simulated.
32 devices in a mesh: gx: 4 (over x, core), gy: 8 (over z, y).
Axes of the slice: x: 2, y: 2, z: 4, core: 2. Of those that a mesh axis runs over, the one named last changes fastest.
Arguments:
- thickness: float32 [1536, 3072], P('gx', 'gy'), may hold values from 0.5 to 3
- bed_uplift: float32 [1536, 3072], P('gx', 'gy'), may hold values from -6 to 6
- flux_x: float32 [1536, 3072], P('gx', 'gy'), may hold values from -6 to 6
- flux_y: float32 [1536, 3072], P('gx', 'gy'), may hold values from -6 to 6
- mass_balance: float32 [1536, 3072], P('gx', 'gy'), may hold values from -3 to 3
- ice_mask: int32 [1536, 3072], P('gx', 'gy'), may hold values from 0 to 2
Outputs:
- thickness_new: float32 [1536, 3072], P('gx', 'gy')
- bed_new: float32 [1536, 3072], P('gx', 'gy')
All inputs are finite; a program needn't handle non-finite values.
Results may differ from a plain program's by a relative error of at most 0.000092.
Values sent between devices are 32-bit elements; how exact they have to be, the bound alone decides.
No kernel may reach another device: no remote copies, remote signals or barrier semaphores. Data moves between devices by JAX's collectives and lax.ppermute only.
A program may use at most 64 MiB of HBM per device.

v0:
```python
import math

import jax
import jax.numpy as jnp
import numpy as np
from jax import lax
from jax.sharding import PartitionSpec as P

time_step = 0.5
viscous = 4.0
buoyant = 0.01
flexural = 50.0
lanes = 128
highest = lax.Precision.HIGHEST


class Plan:
    def __init__(self, mesh, length_x, length_y):
        self.gx, self.gy = mesh.shape["gx"], mesh.shape["gy"]
        self.devices = self.gx * self.gy
        self.length_x, self.length_y = length_x, length_y
        self.radix = length_x // lanes
        self.here = self.radix // self.gx
        self.groups = self.radix // 2
        self.cols = length_y // self.devices
        self.m_parts = min(self.devices, lanes)
        self.g_parts = self.devices // self.m_parts
        self.deep = lanes // self.m_parts
        self.own_groups = self.groups // self.g_parts
        self.rows = 2 * self.deep

    def slot_matrix(self):
        n2 = np.arange(lanes)[None, :]
        m = np.arange(lanes)[:, None]
        theta = 2 * np.pi * (m * n2 % lanes) / lanes
        cos, sin = np.cos(theta), np.sin(theta)
        general = np.stack([np.concatenate([cos, sin], 1), np.concatenate([-sin, cos], 1)])
        half = lanes // 2
        turned = 2 * np.pi * ((2 * (m - half) + 1) * n2 % (2 * lanes)) / (2 * lanes)
        low = np.arange(lanes)[:, None] < half
        real = np.concatenate([np.where(low, cos, 0), np.where(low, 0, np.cos(turned))], 1)
        imag = np.concatenate([np.where(low, -sin, 0), np.where(low, 0, -np.sin(turned))], 1)
        imag[0, :lanes] = np.where(np.arange(lanes) % 2 == 0, 1.0, -1.0)
        first = np.stack([real, imag])
        return np.stack([self._by_part(general), self._by_part(first)]).astype(np.float32)

    def _by_part(self, table):
        split = table.reshape(2, self.m_parts, self.deep, 2 * lanes)
        return split.transpose(1, 0, 2, 3).reshape(2 * lanes, 2 * lanes)

    def slot_inverse(self):
        m = np.arange(lanes)[:, None]
        n2 = np.arange(lanes)[None, :]
        theta = 2 * np.pi * (m * n2 % lanes) / lanes
        cos, sin = np.cos(theta), np.sin(theta)
        general = 2 * np.stack([np.concatenate([cos, sin], 1), np.concatenate([-sin, cos], 1)])
        half = lanes // 2
        turned = 2 * np.pi * ((2 * (m - half) + 1) * n2 % (2 * lanes)) / (2 * lanes)
        low = m < half
        real = 2 * np.concatenate([np.where(low, cos, 0), np.where(low, 0, np.cos(turned))], 1)
        imag = 2 * np.concatenate([np.where(low, -sin, 0), np.where(low, 0, -np.sin(turned))], 1)
        real[0, :lanes] = 1.0
        imag[0, :lanes] = np.where(np.arange(lanes) % 2 == 0, 1.0, -1.0)
        first = np.stack([real, imag])
        return (np.stack([self._by_part(general), self._by_part(first)]) / self.length_x).astype(np.float32)

    def slot_twiddle(self):
        angle = 2 * np.pi * np.arange(self.groups)[:, None] * np.arange(lanes)[None, :] / self.length_x
        return np.stack([np.cos(angle), np.sin(angle)]).astype(np.float32)

    def source_matrix(self):
        count, deep = self.devices, self.deep
        index = np.arange(count)
        theta = 2 * np.pi * (index[:, None] * index[None, :] % count) / count
        cos, sin = np.cos(theta), np.sin(theta)
        out = np.zeros((count, 2, deep, 2, count, deep))
        for q in range(deep):
            out[:, 0, q, 0, :, q] = cos
            out[:, 1, q, 0, :, q] = sin
            out[:, 0, q, 1, :, q] = -sin
            out[:, 1, q, 1, :, q] = cos
        return out.reshape(count * 2 * deep, 2 * count * deep).astype(np.float32)

    def line_matrix(self):
        index = np.arange(self.cols)
        theta = 2 * np.pi * (index[:, None] * index[None, :] % self.cols) / self.cols
        cos, sin = np.cos(theta), np.sin(theta)
        return np.block([[cos, sin], [-sin, cos]]).astype(np.float32)

    def line_twiddle(self):
        angle = 2 * np.pi * np.arange(self.cols)[:, None] * np.arange(self.devices)[None, :] / self.length_y
        angle = np.repeat(angle, self.deep, axis=1)
        return np.stack([np.cos(angle), np.sin(angle)]).astype(np.float32)


def weighted(terms):
    groups = {}
    for coefficient, value in terms:
        size = round(abs(coefficient), 12)
        if size == 0.0:
            continue
        groups.setdefault(size, []).append((coefficient > 0, value))
    total = None
    for size, members in groups.items():
        members.sort(key=lambda member: not member[0])
        positive, part = members[0]
        for sign, value in members[1:]:
            part = part + value if sign == positive else part - value
        if size != 1.0:
            part = part * np.float32(size)
        if total is None:
            total = part if positive else -part
        else:
            total = total + part if positive else total - part
    return total


def radix_forward(values):
    count = len(values)
    half = count // 2
    even = [values[j] + values[count - j] for j in range(1, half)]
    odd = [values[j] - values[count - j] for j in range(1, half)]
    real, imag = [], []
    for g in range(half + 1):
        terms = [(1.0, values[0]), ((-1.0) ** g, values[half])]
        terms += [(math.cos(2 * math.pi * g * (j + 1) / count), even[j]) for j in range(half - 1)]
        real.append(weighted(terms))
        if 0 < g < half:
            imag.append(weighted([(-math.sin(2 * math.pi * g * (j + 1) / count), odd[j]) for j in range(half - 1)]))
    return real, imag


def radix_inverse(first, middle, real, imag):
    half = len(real) + 1
    count = 2 * half
    out = [None] * count
    for j in range(half + 1):
        terms = [(1.0, first), ((-1.0) ** j, middle)]
        terms += [(math.cos(2 * math.pi * g * j / count), real[g - 1]) for g in range(1, half)]
        together = weighted(terms)
        if j in (0, half):
            out[j] = together
            continue
        apart = weighted([(math.sin(2 * math.pi * g * j / count), imag[g - 1]) for g in range(1, half)])
        out[j] = together - apart
        out[count - j] = together + apart
    return out


def mul(a, b):
    return jnp.matmul(a, b, precision=highest)


def exchange_gx(value):
    count = lax.axis_size("gx")
    own = lax.axis_index("gx")
    if count > 8:
        return lax.all_to_all(value, "gx", split_axis=0, concat_axis=0, tiled=True)
    pieces = [lax.dynamic_index_in_dim(value, own, 0, False)]
    for step in range(1, count):
        piece = lax.dynamic_index_in_dim(value, own ^ step, 0, False)
        pieces.append(lax.ppermute(piece, "gx", [(k, k ^ step) for k in range(count)]))
    stacked = jnp.stack(pieces)
    return jnp.stack([lax.dynamic_index_in_dim(stacked, own ^ k, 0, False) for k in range(count)])


def exchange_all(value):
    return lax.all_to_all(value, ("gy", "gx"), split_axis=0, concat_axis=0, tiled=True)


def passed_along(value, axis, steps):
    count = lax.axis_size(axis)
    leading, last = (max(0, -steps), min(count, count - steps))
    return lax.ppermute(value, axis, [(source, source + steps) for source in range(leading, last)])


def forward_x(plan, lines):
    table = plan.slot_matrix()
    cos, sin = plan.slot_twiddle()
    real, imag = radix_forward([lines[:, n] for n in range(plan.radix)])
    blocks = [jnp.concatenate([real[0], real[plan.groups]], -1)]
    for g in range(1, plan.groups):
        re, im = real[g], imag[g - 1]
        blocks.append(jnp.concatenate([re * cos[g] + im * sin[g], im * cos[g] - re * sin[g]], -1))
    first = jnp.einsum("ok,fck->ofc", table[1], blocks[0], precision=highest)
    row = first[plan.deep, 0]
    first = first.at[plan.deep, 0].set(first[0, 1]).at[0, 1].set(row)
    rest = jnp.einsum("ok,gfck->ogfc", table[0], jnp.stack(blocks[1:]), precision=highest)
    spectrum = jnp.concatenate([first[:, None], rest], 1)
    spectrum = spectrum.reshape(plan.m_parts, plan.rows, plan.g_parts, -1)
    return spectrum.transpose(2, 0, 1, 3).reshape(plan.devices, plan.rows, -1)


def spectral_kernels(square):
    kappa = jnp.sqrt(square)
    damping = viscous * kappa
    across = 1.0 / (damping + buoyant + flexural * kappa**4)
    return damping, across


def wave_square(index, length):
    signed = jnp.where(2 * index >= length, index - length, index)
    wave = signed.astype(jnp.float32) * (2.0 * math.pi / length)
    return wave * wave


def middle_y(plan, received, position):
    deep, count, cols = plan.deep, plan.devices, plan.cols
    width = count * deep
    flat = received.reshape(count * plan.rows, -1).T
    mixed = mul(flat, plan.source_matrix())
    mixed = mixed.reshape(plan.own_groups, 2, cols, 2, width)
    cos, sin = plan.line_twiddle()
    re, im = mixed[:, :, :, 0], mixed[:, :, :, 1]
    turned = jnp.concatenate([re * cos + im * sin, im * cos - re * sin], 2)
    spectra = jnp.einsum("wk,gfkl->gfwl", plan.line_matrix(), turned, precision=highest)
    lane = lax.broadcasted_iota(jnp.int32, (1, width), 1)
    q, t = lane % deep, lane // deep
    w = lax.broadcasted_iota(jnp.int32, (cols, 1), 0)
    ky = wave_square(t + count * w, plan.length_y)
    m = (position % plan.m_parts) * deep + q
    base = (position // plan.m_parts) * plan.own_groups
    special = (position == 0) & (q == 0)
    results = []
    for group in range(plan.own_groups):
        g = base + group
        half = lanes // 2
        first = jnp.where(m < half, plan.radix * m, plan.radix // 2 + plan.radix * (m - half))
        index = jnp.where(g == 0, first, g + plan.radix * m)
        damping, across = spectral_kernels(wave_square(index, plan.length_x) + ky)
        u, v = spectra[group, 0], spectra[group, 1]
        ur, ui, vr, vi = u[:cols], u[cols:], v[:cols], v[cols:]
        out_r, out_i = across * (damping * ur - vr), across * (damping * ui - vi)
        if group == 0:
            out_r = jnp.where(special, across * (damping * ur - ui), out_r)
            out_i = jnp.where(special, across * (damping * ui + ur), out_i)
            damping, across = spectral_kernels(np.float32(math.pi) ** 2 + ky)
            extra = jnp.concatenate([across * (damping * vr - vi), across * (damping * vi + vr)], 0)
        results.append(jnp.concatenate([out_r, out_i], 0))
    results.append(extra)
    back = jnp.einsum("kw,gkl->gwl", plan.line_matrix() * np.float32(1.0 / plan.length_y), jnp.stack(results), precision=highest)
    re, im = back[:, :cols], back[:, cols:]
    turned = jnp.concatenate([re * cos - im * sin, im * cos + re * sin], 2)
    lines = jnp.einsum("gcl,sl->gcs", turned, plan.source_matrix(), precision=highest)
    place = lax.broadcasted_iota(jnp.int32, (1, count * plan.rows), 1)
    moved = (position == 0) & (place % plan.rows == deep)
    fixed = jnp.where(moved, jnp.roll(lines[-1], deep, axis=1), lines[0])
    lines = jnp.concatenate([fixed[None], lines[1:-1]], 0)
    return lines.reshape(plan.own_groups * cols, count * plan.rows).T.reshape(count, plan.rows, -1)


def inverse_x(plan, received):
    cols = plan.cols
    table = plan.slot_inverse()
    cos, sin = plan.slot_twiddle()
    split = received.reshape(plan.g_parts, 2 * lanes, plan.own_groups, cols)
    split = split.transpose(0, 2, 3, 1).reshape(plan.groups, cols, 2 * lanes)
    first = mul(split[0], table[1])
    rest = mul(split[1:], table[0])
    real, imag = [], []
    for g in range(1, plan.groups):
        re, im = rest[g - 1, :, :lanes], rest[g - 1, :, lanes:]
        real.append(re * cos[g] - im * sin[g])
        imag.append(im * cos[g] + re * sin[g])
    return radix_inverse(first[:, :lanes], first[:, lanes:], real, imag)


def to_lines(plan, field):
    split = field.reshape(plan.here, lanes, plan.gx, plan.cols)
    return split.transpose(2, 0, 3, 1)


def build(plan):
    def local(thickness, bed_uplift, flux_x, flux_y, mass_balance, ice_mask):
        lower_face = passed_along(flux_x[-1:, :], "gx", 1)
        left_face = passed_along(flux_y[:, -1:], "gy", 1)
        flux_below = jnp.concatenate([lower_face, flux_x[:-1, :]], axis=0)
        flux_left = jnp.concatenate([left_face, flux_y[:, :-1]], axis=1)
        divergence = flux_x - flux_below + flux_y - flux_left
        trial = thickness + time_step * (mass_balance - divergence)
        thickness_new = jnp.where(ice_mask == 2, 0.0, jnp.maximum(trial, 0.0))
        load = jnp.where(ice_mask == 0, thickness_new - thickness, 0.0)
        fields = jnp.stack([to_lines(plan, bed_uplift), to_lines(plan, load)], 1)
        lines = exchange_gx(fields)
        lines = lines.transpose(1, 0, 2, 3, 4).reshape(2, plan.radix, plan.cols, lanes)
        received = exchange_all(forward_x(plan, lines))
        position = lax.axis_index("gy") * plan.gx + lax.axis_index("gx")
        back = exchange_all(middle_y(plan, received, position))
        bed = inverse_x(plan, back)
        bed = jnp.stack(bed).reshape(plan.gx, plan.here, plan.cols, lanes)
        bed = exchange_gx(bed)
        bed_new = bed.transpose(1, 3, 0, 2).reshape(plan.here * lanes, plan.gx * plan.cols)
        return thickness_new, bed_new

    return local


def solution(mesh):
    spec = P("gx", "gy")

    def step(*args):
        length_x, length_y = args[0].shape
        plan = Plan(mesh, length_x, length_y)
        body = jax.shard_map(build(plan), mesh=mesh, in_specs=(spec,) * 6, out_specs=(spec, spec), check_vma=False)
        return body(*args)

    return step
```

profile of v0, /device:TPU:0, one launch (start us, length us, event | category | flops | bytes accessed | tf_op | source)
XLA Modules:
  0.0 132.6 jit_solution(13359822511079748274)
XLA Ops:
  0.7 1.2 slice.359
  1.8 4.9 %collective-permute-start.1 = (f32[384,1]{1,0:T(8,128)S(1)}, f32[384,1]{1,0:T(8,128)S(1)}, u32[]{:S(2)}, u32[]{:S(2)}) collective-permute-start(f32[384,1]{1,0:T(8,128)S(1)} %slice.359), channel_id=1, source_target_pairs={{0,1},{1,2},{2,3},{3,4},{4,5},{5,6},{6,7},{8,9},{9,10},{10,11},{11... | collective-permute-start | bytes 4616 | tf_op jit(solution)/shard_map/ppermute | solution.py:174
  6.7 0.7 slice.357
  7.5 1.4 %collective-permute-start = (f32[1,384]{1,0:T(1,128)S(1)}, f32[1,384]{1,0:T(1,128)S(1)}, u32[]{:S(2)}, u32[]{:S(2)}) collective-permute-start(f32[1,384]{1,0:T(1,128)S(1)} %slice.357), channel_id=1, source_target_pairs={{0,8},{8,16},{16,24},{1,9},{9,17},{17,25},{2,10},{10,18},{18,26},{... | collective-permute-start | bytes 4616 | tf_op jit(solution)/shard_map/ppermute | solution.py:174
  8.9 1.5 %reshape.399 = f32[3,128,4,96]{3,2,1,0:T(4,128)S(1)} reshape(f32[384,384]{1,0:T(8,128)} %param.61) | data formatting | bytes 1179648 | tf_op jit(solution)/shard_map/reshape | solution.py:269
  10.5 0.4 collective-permute-done.1
  10.9 2.4 %subtract_select_fusion = (f32[384,384]{1,0:T(8,128)S(1)}, f32[384,384]{1,0:T(8,128)}) fusion(f32[384,384]{1,0:T(8,128)S(1)} %copy-done.2, s32[384,384]{1,0:T(8,128)} %param.65, f32[384,384]{1,0:T(8,128)} %param.64, f32[384,383]{1,0:T(8,128)S(1)} %bitcast.668, f32[384,1]{1,0:T(8,128)S(1)} %collective-permute-done.1, f32[384,384]{1,0:T(8,128)S(1)} %copy-done, ...), kind=kLoop, calls=%fused_computation.35 | loop fusion | flops 2064384 | bytes 5308416 | tf_op jit(solution)/shard_map/jit(_where)/select_n | solution.py:282
  13.3 0.5 reshape.400
  13.8 2.1 %fusion.16 = (f32[1,2,3,96,128]{3,0,4,2,1:T(1,128)S(1)}, f32[1,2,3,96,128]{3,0,4,2,1:T(1,128)S(1)}, f32[1,2,3,96,128]{3,0,4,2,1:T(1,128)S(1)}, f32[1,2,3,96,128]{3,0,4,2,1:T(1,128)S(1)}) fusion(s32[]{:T(128)S(6)} %select_n.305, f32[4,1,3,96,128]{3,0,4,2,1:T(4,128)S(1)} %bitcast.669, f32[4,1,3,96,128]{3,0,4,2,1:T(4,128)S(1)} %bitcast.670, s32[]{:T(128)S(6)} %select_n.306, ...), kind=kLoop, calls=%fused_computation.39 | loop fusion | flops 294912 | bytes 2359312 | tf_op jit(solution)/shard_map/stack | solution.py:283
  15.9 0.8 collective-permute-start.4
  16.7 2.3 %collective-permute-start.2 = (f32[2,3,96,128]{2,3,1,0:T(8,128)S(1)}, f32[2,3,96,128]{2,3,1,0:T(8,128)S(1)}, u32[]{:S(2)}, u32[]{:S(2)}) collective-permute-start(f32[2,3,96,128]{2,3,1,0:T(8,128)S(1)} %bitcast.682), channel_id=1, source_target_pairs={{0,8},{8,0},{16,24},{24,16},{1,9},{9,1},{17,25},{25,17},{2,10},{10... | collective-permute-start | bytes 884744 | tf_op jit(solution)/shard_map/ppermute | solution.py:162
  19.3 0.6 fusion.130
  19.9 5.6 %collective-permute-done.4 = f32[2,3,96,128]{2,3,1,0:T(8,128)S(1)} collective-permute-done((f32[2,3,96,128]{2,3,1,0:T(8,128)S(1)}, f32[2,3,96,128]{2,3,1,0:T(8,128)S(1)}, u32[]{:S(2)}, u32[]{:S(2)}) %collective-permute-start.4) | collective-permute-done | bytes 294944 | tf_op jit(solution)/shard_map/ppermute | solution.py:162
  25.5 10.3 %collective-permute-done.3 = f32[2,3,96,128]{2,3,1,0:T(8,128)S(1)} collective-permute-done((f32[2,3,96,128]{2,3,1,0:T(8,128)S(1)}, f32[2,3,96,128]{2,3,1,0:T(8,128)S(1)}, u32[]{:S(2)}, u32[]{:S(2)}) %collective-permute-start.3) | collective-permute-done | bytes 294944 | tf_op jit(solution)/shard_map/ppermute | solution.py:162
  35.8 1.8 %pad_maximum_fusion = f32[4,2,3,96,128]{3,0,4,2,1:T(4,128)S(1)} fusion(f32[1,2,3,96,128]{3,0,4,2,1:T(1,128)S(1)} %bitcast.678, f32[1,2,3,96,128]{3,0,4,2,1:T(1,128)S(1)} %bitcast.680, f32[1,2,3,96,128]{3,0,4,2,1:T(1,128)S(1)} %bitcast.679, f32[1,2,3,96,128]{3,0,4,2,1:T(1,128)S(1)} %get-tuple-element.86), kind=kLoop, calls=%fused_computation.8 | loop fusion | flops 884736 | bytes 2359296 | tf_op jit(solution)/shard_map/stack | solution.py:163
  37.6 1.7 %constant_dynamic-slice_fusion.11 = (f32[1,2,3,96,128]{3,0,4,2,1:T(1,128)S(1)}, f32[1,2,3,96,128]{3,0,4,2,1:T(1,128)S(1)}, f32[1,2,3,96,128]{3,0,4,2,1:T(1,128)S(1)}, f32[1,2,3,96,128]{3,0,4,2,1:T(1,128)S(1)}) fusion(f32[4,2,3,96,128]{3,0,4,2,1:T(4,128)S(1)} %pad_maximum_fusion, s32[]{:T(128)S(6)} %select_n.305, s32[]{:T(128)S(6)} %select_n.308, ...), kind=kLoop, calls=%fused_computation.303 | loop fusion | bytes 2359312 | tf_op jit(solution)/shard_map/jit(dynamic_index_in_dim)/dynamic_slice | solution.py:164
  39.3 1.8 %maximum_bitcast_fusion = f32[2,4,3,96,128]{3,1,4,2,0:T(4,128)S(1)} fusion(f32[1,2,3,96,128]{3,0,4,2,1:T(1,128)S(1)} %get-tuple-element.83, f32[1,2,3,96,128]{3,0,4,2,1:T(1,128)S(1)} %get-tuple-element.84, f32[1,2,3,96,128]{3,0,4,2,1:T(1,128)S(1)} %get-tuple-element.85, f32[1,2,3,96,128]{3,0,4,2,1:T(1,128)S(1)} %get-tuple-element.82), kind=kLoop, calls=%fused_computation.9 | loop fusion | flops 884736 | bytes 2359296 | tf_op jit(solution)/shard_map/transpose | solution.py:285
  41.1 0.7 copy.64
  41.9 0.5 copy-done.15
  42.7 0.4 copy-done.21
  43.6 0.4 fusion.19
  44.1 0.3 scatter.6
  44.6 0.7 copy-done.6
  45.3 1.0 fusion.131
  46.3 1.7 %scatter.9 = f32[256,1,2,96]{0,3,2,1:T(8,128)S(1)} dynamic-update-slice(f32[256,1,2,96]{0,3,2,1:T(8,128)S(1)} %scatter.6, f32[1,1,1,96]{0,3,2,1:T(8,128)S(1)} %get-tuple-element.129, s32[]{:T(128)} %bitcast.23, s32[]{:T(128)} %constant.244.clone.1, s32[]{:T(128)} %bitcast.24, s32[]{:T(128)} %constant.244.clone.1) | dynamic-update-slice | bytes 772 | tf_op jit(solution)/shard_map/scatter | solution.py:187
  48.1 1.1 copy.67
  49.2 2.6 %reshape_transpose_reshape.3 = f32[32,8,1152]{2,1,0:T(8,128)} reshape(f32[256,6,2,96]{3,2,1,0:T(2,128)S(1)} %copy.67) | data formatting | bytes 2359296 | tf_op jit(solution)/shard_map/reshape;transpose;reshape | solution.py:191
  51.8 5.9 %all-to-all-start = ((f32[32,8,1152]{2,1,0:T(8,128)}), f32[32,8,1152]{2,1,0:T(8,128)S(1)}, u32[]{:S(2)}, u32[]{:S(2)}) async-start(f32[32,8,1152]{2,1,0:T(8,128)} %reshape_transpose_reshape.3), calls=%async_computation | async-start | bytes 2359296 | tf_op jit(solution)/shard_map/all_to_all | solution.py:168
  57.9 28.8 %all-to-all-done = f32[32,8,1152]{2,1,0:T(8,128)S(1)} async-done(((f32[32,8,1152]{2,1,0:T(8,128)}), f32[32,8,1152]{2,1,0:T(8,128)S(1)}, u32[]{:S(2)}, u32[]{:S(2)}) %all-to-all-start) | async-done | bytes 1179680 | tf_op jit(solution)/shard_map/all_to_all | solution.py:168
  86.7 0.4 copy.68
  87.2 1.1 fusion.132
  88.5 0.8 copy-done.10
  89.2 1.2 convolution_bitcast_fusion
  91.1 0.4 copy-done.9
  91.5 0.8 convolution_bitcast_fusion.1
  92.5 0.7 fusion.3
  93.8 21.4 %all_to_all.10 = f32[32,8,576]{2,1,0:T(8,128)S(1)} all-to-all(f32[32,8,576]{2,1,0:T(8,128)S(1)} %bitcast.671), channel_id=1, replica_groups=mesh['gx'=4,'gy'=8] {'gy','gx'}, dimensions={0} | all-to-all | bytes 1179648 | tf_op jit(solution)/shard_map/all_to_all | solution.py:168
  115.2 0.4 reshape.407
  115.6 0.3 copy.71
  116.1 0.6 fusion.14
  117.8 1.6 %collective-permute-start.6 = (f32[3,96,128]{1,2,0:T(8,128)S(1)}, f32[3,96,128]{1,2,0:T(8,128)S(1)}, u32[]{:S(2)}, u32[]{:S(2)}) collective-permute-start(f32[3,96,128]{1,2,0:T(8,128)S(1)} %bitcast.688), channel_id=1, source_target_pairs={{0,16},{8,24},{16,0},{24,8},{1,17},{9,25},{17,1},{25,9},{2,18},{10... | collective-permute-start | bytes 442376 | tf_op jit(solution)/shard_map/ppermute | solution.py:162
  119.5 0.3 collective-permute-start.7
  120.0 5.7 %collective-permute-done.6 = f32[3,96,128]{1,2,0:T(8,128)S(1)} collective-permute-done((f32[3,96,128]{1,2,0:T(8,128)S(1)}, f32[3,96,128]{1,2,0:T(8,128)S(1)}, u32[]{:S(2)}, u32[]{:S(2)}) %collective-permute-start.6) | collective-permute-done | bytes 147488 | tf_op jit(solution)/shard_map/ppermute | solution.py:162
  125.7 3.1 %collective-permute-done.7 = f32[3,96,128]{1,2,0:T(8,128)S(1)} collective-permute-done((f32[3,96,128]{1,2,0:T(8,128)S(1)}, f32[3,96,128]{1,2,0:T(8,128)S(1)}, u32[]{:S(2)}, u32[]{:S(2)}) %collective-permute-start.7) | collective-permute-done | bytes 147488 | tf_op jit(solution)/shard_map/ppermute | solution.py:162
  128.8 0.9 pad_maximum_fusion.2
  129.7 0.9 constant_dynamic-slice_fusion.3
  130.6 0.9 maximum_bitcast_fusion.1
  131.4 1.2 reshape.409
  (113 shorter events, 4.4 us)
Async XLA Ops:
  0.6 10.3 %copy-start = (f32[384,384]{1,0:T(8,128)S(1)}, f32[384,384]{1,0:T(8,128)}, u32[]{:S(2)}) copy-start(f32[384,384]{1,0:T(8,128)} %param.63) | copy-start | bytes 1769476
  0.6 10.2 %copy-start.1 = (f32[384,384]{1,0:T(8,128)S(1)}, f32[384,384]{1,0:T(8,128)}, u32[]{:S(2)}) copy-start(f32[384,384]{1,0:T(8,128)} %param.62) | copy-start | bytes 1769476
  0.7 10.2 %copy-start.2 = (f32[384,384]{1,0:T(8,128)S(1)}, f32[384,384]{1,0:T(8,128)}, u32[]{:S(2)}) copy-start(f32[384,384]{1,0:T(8,128)} %param.60) | copy-start | bytes 1769476
  1.8 9.0 %collective-permute-start.1 = (f32[384,1]{1,0:T(8,128)S(1)}, f32[384,1]{1,0:T(8,128)S(1)}, u32[]{:S(2)}, u32[]{:S(2)}) collective-permute-start(f32[384,1]{1,0:T(8,128)S(1)} %slice.359), channel_id=1, source_target_pairs={{0,1},{1,2},{2,3},{3,4},{4,5},{5,6},{6,7},{8,9},{9,10},{10,11},{11... | collective-permute-start | bytes 4616 | tf_op jit(solution)/shard_map/ppermute | solution.py:174
  7.5 3.4 %collective-permute-start = (f32[1,384]{1,0:T(1,128)S(1)}, f32[1,384]{1,0:T(1,128)S(1)}, u32[]{:S(2)}, u32[]{:S(2)}) collective-permute-start(f32[1,384]{1,0:T(1,128)S(1)} %slice.357), channel_id=1, source_target_pairs={{0,8},{8,16},{16,24},{1,9},{9,17},{17,25},{2,10},{10,18},{18,26},{... | collective-permute-start | bytes 4616 | tf_op jit(solution)/shard_map/ppermute | solution.py:174
  15.9 9.6 %collective-permute-start.4 = (f32[2,3,96,128]{2,3,1,0:T(8,128)S(1)}, f32[2,3,96,128]{2,3,1,0:T(8,128)S(1)}, u32[]{:S(2)}, u32[]{:S(2)}) collective-permute-start(f32[2,3,96,128]{2,3,1,0:T(8,128)S(1)} %bitcast.683), channel_id=1, source_target_pairs={{0,24},{8,16},{16,8},{24,0},{1,25},{9,17},{17,9},{25,1},{2,26},{10... | collective-permute-start | bytes 884744 | tf_op jit(solution)/shard_map/ppermute | solution.py:162
  16.7 8.8 %collective-permute-start.2 = (f32[2,3,96,128]{2,3,1,0:T(8,128)S(1)}, f32[2,3,96,128]{2,3,1,0:T(8,128)S(1)}, u32[]{:S(2)}, u32[]{:S(2)}) collective-permute-start(f32[2,3,96,128]{2,3,1,0:T(8,128)S(1)} %bitcast.682), channel_id=1, source_target_pairs={{0,8},{8,0},{16,24},{24,16},{1,9},{9,1},{17,25},{25,17},{2,10},{10... | collective-permute-start | bytes 884744 | tf_op jit(solution)/shard_map/ppermute | solution.py:162
  19.0 16.8 %collective-permute-start.3 = (f32[2,3,96,128]{2,3,1,0:T(8,128)S(1)}, f32[2,3,96,128]{2,3,1,0:T(8,128)S(1)}, u32[]{:S(2)}, u32[]{:S(2)}) collective-permute-start(f32[2,3,96,128]{2,3,1,0:T(8,128)S(1)} %bitcast.681), channel_id=1, source_target_pairs={{0,16},{8,24},{16,0},{24,8},{1,17},{9,25},{17,1},{25,9},{2,18},{10... | collective-permute-start | bytes 884744 | tf_op jit(solution)/shard_map/ppermute | solution.py:162
  41.8 0.7 copy-start.15
  41.8 0.7 copy-start.16
  41.9 0.7 copy-start.13
  41.9 0.7 copy-start.14
  41.9 0.7 copy-start.17
  41.9 0.7 copy-start.18
  42.4 0.7 copy-start.21
  42.4 0.7 copy-start.22
  42.4 0.7 copy-start.25
  42.4 0.7 copy-start.26
  42.6 1.0 copy-start.8
  43.1 1.3 copy-start.19
  43.1 1.3 copy-start.20
  43.1 1.3 copy-start.23
  43.2 1.3 copy-start.24
  44.3 1.0 copy-start.6
  51.8 34.9 %all-to-all-start = ((f32[32,8,1152]{2,1,0:T(8,128)}), f32[32,8,1152]{2,1,0:T(8,128)S(1)}, u32[]{:S(2)}, u32[]{:S(2)}) async-start(f32[32,8,1152]{2,1,0:T(8,128)} %reshape_transpose_reshape.3), calls=%async_computation | async-start | bytes 2359296 | tf_op jit(solution)/shard_map/all_to_all | solution.py:168
  57.7 29.4 %copy-start.5 = (f32[2,128,256,1,1]{2,1,0,4,3:T(8,128)S(1)}, f32[2,128,256,1,1]{2,1,0,4,3:T(8,128)}, u32[]{:S(2)}) copy-start(f32[2,128,256,1,1]{2,1,0,4,3:T(8,128)} %constant.296) | copy-start | bytes 786436
  87.1 1.2 copy-start.11
  87.1 1.2 copy-start.12
  88.3 0.9 copy-start.10
  90.6 0.9 copy-start.9
  91.5 0.9 copy-start.4
  115.2 1.0 copy-start.3
  115.6 1.1 copy-start.7
  117.6 2.4 %collective-permute-start.5 = (f32[3,96,128]{1,2,0:T(8,128)S(1)}, f32[3,96,128]{1,2,0:T(8,128)S(1)}, u32[]{:S(2)}, u32[]{:S(2)}) collective-permute-start(f32[3,96,128]{1,2,0:T(8,128)S(1)} %bitcast.687), channel_id=1, source_target_pairs={{0,8},{8,0},{16,24},{24,16},{1,9},{9,1},{17,25},{25,17},{2,10},{10... | collective-permute-start | bytes 442376 | tf_op jit(solution)/shard_map/ppermute | solution.py:162
  117.8 7.8 %collective-permute-start.6 = (f32[3,96,128]{1,2,0:T(8,128)S(1)}, f32[3,96,128]{1,2,0:T(8,128)S(1)}, u32[]{:S(2)}, u32[]{:S(2)}) collective-permute-start(f32[3,96,128]{1,2,0:T(8,128)S(1)} %bitcast.688), channel_id=1, source_target_pairs={{0,16},{8,24},{16,0},{24,8},{1,17},{9,25},{17,1},{25,9},{2,18},{10... | collective-permute-start | bytes 442376 | tf_op jit(solution)/shard_map/ppermute | solution.py:162
  119.5 9.3 %collective-permute-start.7 = (f32[3,96,128]{1,2,0:T(8,128)S(1)}, f32[3,96,128]{1,2,0:T(8,128)S(1)}, u32[]{:S(2)}, u32[]{:S(2)}) collective-permute-start(f32[3,96,128]{1,2,0:T(8,128)S(1)} %bitcast.689), channel_id=1, source_target_pairs={{0,24},{8,16},{16,8},{24,0},{1,25},{9,17},{17,9},{25,1},{2,26},{10... | collective-permute-start | bytes 442376 | tf_op jit(solution)/shard_map/ppermute | solution.py:162
where the time goes:
time: 133 us
  waiting for transfers between devices  53.9 us (41%)
  blocking collectives  21.4 us (16%)
  local copies, waits for them, and re-layouts  20.2 us (15%)
  starting transfers between devices  17.7 us (13%)
  other arithmetic  11.8 us (9%)
  matrix products  6.1 us (5%)
  between operations  1.53 us (1%)
    all_to_all x1, waiting for transfers between devices, exchange_all(): lax.all_to_all(value, ('gy', 'gx'), split_axis=0, concat_axis=0, tiled=True)  28.8 us
    ppermute x6, waiting for transfers between devices, exchange_gx(): lax.ppermute(piece, 'gx', [(k, k ^ step) for k in range(count)])  24.7 us
    all_to_all x1, blocking collectives, exchange_all(): lax.all_to_all(value, ('gy', 'gx'), split_axis=0, concat_axis=0, tiled=True)  21.4 us
    ppermute x2, starting transfers between devices, passed_along(): lax.ppermute(value, axis, [(source, source + steps) for source in range(l...  6.36 us
    all_to_all x1, starting transfers between devices, exchange_all(): lax.all_to_all(value, ('gy', 'gx'), split_axis=0, concat_axis=0, tiled=True)  5.89 us
    ppermute x6, starting transfers between devices, exchange_gx(): lax.ppermute(piece, 'gx', [(k, k ^ step) for k in range(count)])  5.46 us
    unnamed x55, local copies, waits for them, and re-layouts  3.56 us
  transfers between devices with their start and end apart: 9, of which 6 were waited for; matrix products, arithmetic and copies ran while one was open for 2% of the time, Pallas kernels for 0%

commit v1 on v0

--- a/solution.py
+++ b/solution.py
@@ -4,6 +4,8 @@
 import jax.numpy as jnp
 import numpy as np
 from jax import lax
+from jax.experimental import pallas as pl
+from jax.experimental.pallas import tpu as pltpu
 from jax.sharding import PartitionSpec as P
 
 time_step = 0.5
@@ -270,7 +272,333 @@
     return split.transpose(2, 0, 3, 1)
 
 
+def halves(value):
+    high = value.astype(jnp.bfloat16)
+    return high, (value - high.astype(jnp.float32)).astype(jnp.bfloat16)
+
+
+def table_halves(table):
+    high = table.astype(jnp.bfloat16)
+    return np.stack([high, (table - high.astype(np.float32)).astype(jnp.bfloat16)])
+
+
+def product(left, right, turned=False):
+    dims = (((1,), (1 if turned else 0,)), ((), ()))
+
+    def one(a, b):
+        return lax.dot_general(a, b, dims, preferred_element_type=jnp.float32)
+
+    return one(left[0], right[0]) + (one(left[0], right[1]) + one(left[1], right[0]))
+
+
+def call(body, outs, scratch, scalars, *operands):
+    scalar = pl.BlockSpec(memory_space=pltpu.SMEM)
+    whole = pl.BlockSpec(memory_space=pltpu.VMEM)
+    shapes = [jax.ShapeDtypeStruct(shape, jnp.float32) for shape in outs]
+    run = pl.pallas_call(
+        body,
+        out_shape=shapes,
+        in_specs=[scalar] * len(scalars) + [whole] * len(operands),
+        out_specs=[whole] * len(outs),
+        scratch_shapes=scratch,
+        compiler_params=pltpu.CompilerParams(vmem_limit_bytes=48 << 20),
+    )
+    return run(*scalars, *operands)
+
+
+def lines_out(plan, own, block, here, out_ref):
+    turned = block.T
+    for part in range(plan.gx):
+        out_ref[own ^ part, here] = turned[part * plan.cols : (part + 1) * plan.cols]
+
+
+def uplift_kernel(plan, own_ref, uplift_ref, flux_x_ref, flux_y_ref, out_ref, face_x_ref, face_y_ref):
+    own = own_ref[0]
+    size = flux_x_ref.shape[0]
+    face_x_ref[...] = flux_x_ref[7:8, :]
+    face_y_ref[...] = flux_y_ref[...].T[lanes - 1 : lanes, :]
+    for here in range(plan.here):
+        lines_out(plan, own, uplift_ref[here * lanes : (here + 1) * lanes, :], here, out_ref)
+
+
+def send_uplift(plan, own, bed_uplift, flux_x, flux_y):
+    rows, cols = bed_uplift.shape
+    run = pl.pallas_call(
+        lambda *refs: uplift_kernel(plan, *refs),
+        grid=(1,),
+        out_shape=[
+            jax.ShapeDtypeStruct((plan.gx, plan.here, plan.cols, lanes), jnp.float32),
+            jax.ShapeDtypeStruct((1, cols), jnp.float32),
+            jax.ShapeDtypeStruct((1, rows), jnp.float32),
+        ],
+        in_specs=[
+            pl.BlockSpec(memory_space=pltpu.SMEM),
+            pl.BlockSpec((rows, cols), lambda i: (0, 0)),
+            pl.BlockSpec((8, cols), lambda i: (rows // 8 - 1, 0)),
+            pl.BlockSpec((rows, lanes), lambda i: (0, cols // lanes - 1)),
+        ],
+    )
+    return run(own, bed_uplift, flux_x, flux_y)
+
+
+def load_kernel(plan, own_ref, thick_ref, fx_ref, fy_ref, mb_ref, mask_ref, face_x_ref, face_y_ref, out_ref, line_ref):
+    own = own_ref[0]
+    for here in range(plan.here):
+        rows = slice(here * lanes, (here + 1) * lanes)
+        fx, fy = fx_ref[rows, :], fy_ref[rows, :]
+        row = lax.broadcasted_iota(jnp.int32, fx.shape, 0)
+        col = lax.broadcasted_iota(jnp.int32, fx.shape, 1)
+        above = face_x_ref[...] if here == 0 else fx_ref[here * lanes - 1 : here * lanes, :]
+        below = jnp.where(row == 0, jnp.broadcast_to(above, fx.shape), pltpu.roll(fx, 1, 0))
+        side = jnp.broadcast_to(face_y_ref[:, rows], (lanes, lanes)).T
+        left = jnp.where(col == 0, jnp.concatenate([side] * (fx.shape[1] // lanes), 1), pltpu.roll(fy, 1, 1))
+        divergence = fx - below + fy - left
+        thick, mask = thick_ref[rows, :], mask_ref[rows, :]
+        trial = thick + time_step * (mb_ref[rows, :] - divergence)
+        new = jnp.where(mask == 2, 0.0, jnp.maximum(trial, 0.0))
+        out_ref[rows, :] = new
+        lines_out(plan, own, jnp.where(mask == 0, new - thick, 0.0), here, line_ref)
+
+
+def forward_kernel(plan, own_ref, *refs):
+    pieces, (twiddle_ref, table_ref, out_ref, line_ref, high_ref, low_ref) = refs[:-6], refs[-6:]
+    own = own_ref[0]
+    cols, radix, groups, here = plan.cols, plan.radix, plan.groups, plan.here
+    step_rows = 16
+    for field in range(2):
+        for step in range(plan.gx):
+            piece = pieces[field * plan.gx + step]
+            for a in range(here):
+                line_ref[(own ^ step) * here + a] = piece[a]
+
+        def chunk(index, carry, field=field):
+            row = pl.multiple_of(index * step_rows, step_rows)
+            real, imag = radix_forward([line_ref[n, pl.ds(row, step_rows), :] for n in range(radix)])
+            for g in range(groups):
+                if g == 0:
+                    first, second = real[0], real[groups]
+                else:
+                    cos, sin = twiddle_ref[0, g : g + 1, :], twiddle_ref[1, g : g + 1, :]
+                    first = real[g] * cos + imag[g - 1] * sin
+                    second = imag[g - 1] * cos - real[g] * sin
+                high, low = halves(jnp.concatenate([first, second], 1))
+                place = pl.ds((2 * g + field) * cols + row, step_rows)
+                high_ref[place, :] = high
+                low_ref[place, :] = low
+            return carry
+
+        lax.fori_loop(0, cols // step_rows, chunk, 0)
+
+    general = (table_ref[0, 0], table_ref[0, 1])
+    special = (table_ref[1, 0], table_ref[1, 1])
+    edge = 2 * cols
+    starts = []
+    for start in range(0, 2 * groups * cols, lanes):
+        rows = slice(start, start + lanes)
+        data = (high_ref[rows, :], low_ref[rows, :])
+        if start + lanes <= edge:
+            out = product(special, data, True)
+        else:
+            out = product(general, data, True)
+            if start < edge:
+                lane = lax.broadcasted_iota(jnp.int32, out.shape, 1)
+                out = jnp.where(lane < edge - start, product(special, data, True), out)
+        out_ref[:, :, start : start + lanes] = out.reshape(plan.devices, plan.rows, lanes)
+    size = 2 * lanes
+    block = out_ref[0, :, :size]
+    row = lax.broadcasted_iota(jnp.int32, block.shape, 0)
+    lane = lax.broadcasted_iota(jnp.int32, block.shape, 1)
+    swapped = pltpu.roll(block, plan.deep, 0)
+    to_left, to_right = pltpu.roll(swapped, size - cols, 1), pltpu.roll(swapped, cols, 1)
+    block = jnp.where((row == plan.deep) & (lane < cols), to_left, block)
+    block = jnp.where((row == 0) & (lane >= cols) & (lane < 2 * cols), to_right, block)
+    out_ref[0, :, :size] = block
+
+
+def middle_kernel(plan, position_ref, in_ref, t1_ref, t2_ref, t2i_ref, t1i_ref, twiddle_ref, out_ref, high_ref, low_ref, back_high, back_low, turn_ref):
+    position = position_ref[0]
+    cols, groups, deep, count = plan.cols, plan.groups, plan.deep, plan.devices
+    width, size = lanes, 2 * lanes
+    for start in range(0, 2 * groups * cols, lanes):
+        block = in_ref[:, :, start : start + lanes].reshape(size, lanes).T
+        high_ref[start : start + lanes, :], low_ref[start : start + lanes, :] = halves(block)
+    t1 = (t1_ref[0], t1_ref[1])
+    t2 = (t2_ref[0], t2_ref[1])
+    t2i = (t2i_ref[0], t2i_ref[1])
+    t1i = (t1i_ref[0], t1i_ref[1])
+    cos, sin = twiddle_ref[0], twiddle_ref[1]
+    lane = lax.broadcasted_iota(jnp.int32, (1, width), 1)
+    q, t = lane % deep, lane // deep
+    w = lax.broadcasted_iota(jnp.int32, (cols, width), 0)
+    ky = wave_square(t + count * w, plan.length_y)
+    m = position * deep + q
+    special = jnp.broadcast_to((position == 0) & (q == 0), (cols, width))
+    results = []
+    for g in range(groups):
+        rows = slice(2 * g * cols, 2 * (g + 1) * cols)
+        mixed = product((high_ref[rows, :], low_ref[rows, :]), t1)
+        sides = []
+        for field in range(2):
+            part = mixed[field * cols : (field + 1) * cols]
+            re, im = part[:, :width], part[:, width:]
+            sides.append(jnp.concatenate([re * cos + im * sin, im * cos - re * sin], 0))
+        spectra = product(t2, halves(jnp.concatenate(sides, 1)))
+        ur, vr = spectra[:cols, :width], spectra[:cols, width:]
+        ui, vi = spectra[cols:, :width], spectra[cols:, width:]
+        half = lanes // 2
+        if g == 0:
+            index = jnp.where(m < half, plan.radix * m, plan.radix // 2 + plan.radix * (m - half))
+        else:
+            index = g + plan.radix * m
+        damping, across = spectral_kernels(wave_square(index, plan.length_x) + ky)
+        out_r, out_i = across * (damping * ur - vr), across * (damping * ui - vi)
+        if g == 0:
+            out_r = jnp.where(special, across * (damping * ur - ui), out_r)
+            out_i = jnp.where(special, across * (damping * ui + ur), out_i)
+            damping, across = spectral_kernels(np.float32(math.pi) ** 2 + ky)
+            extra = jnp.concatenate([across * (damping * vr - vi), across * (damping * vi + vr)], 0)
+        results.append(jnp.concatenate([out_r, out_i], 0))
+    results.append(extra)
+    for g in range(0, groups + 1, 2):
+        pair = results[g : g + 2]
+        back = product(t2i, halves(jnp.concatenate(pair, 1)))
+        for k in range(len(pair)):
+            re, im = back[:cols, k * width : (k + 1) * width], back[cols:, k * width : (k + 1) * width]
+            turned = jnp.concatenate([re * cos - im * sin, im * cos + re * sin], 1)
+            place = slice((g + k) * cols, (g + k + 1) * cols)
+            back_high[place, :], back_low[place, :] = halves(turned)
+    last = slice(groups * cols, (groups + 1) * cols)
+    extra = product((back_high[last, :], back_low[last, :]), t1i)
+    place = lax.broadcasted_iota(jnp.int32, (cols, size), 1)
+    moved = (position == 0) & (place % plan.rows == deep)
+    for g in range(groups):
+        rows = slice(g * cols, (g + 1) * cols)
+        lines = product((back_high[rows, :], back_low[rows, :]), t1i)
+        if g == 0:
+            lines = jnp.where(moved, pltpu.roll(extra, deep, 1), lines)
+        turn_ref[rows, :] = lines
+    for start in range(0, groups * cols, lanes):
+        block = turn_ref[start : start + lanes, :].T
+        keep = min(lanes, groups * cols - start)
+        out_ref[:, :, start : start + keep] = block.reshape(count, plan.rows, lanes)[:, :, :keep]
+
+
+def inverse_kernel(plan, own_ref, in_ref, twiddle_ref, table_ref, out_ref, turn_ref, mid_ref):
+    own = own_ref[0]
+    cols, groups, here = plan.cols, plan.groups, plan.here
+    size = 2 * lanes
+    total = groups * cols
+    for start in range(0, total, lanes):
+        keep = min(lanes, total - start)
+        block = in_ref[:, :, start : start + keep].reshape(size, keep)
+        turn_ref[start : start + keep, :] = block.T
+    for g in range(groups):
+        rows = slice(g * cols, (g + 1) * cols)
+        kind = 1 if g == 0 else 0
+        mid_ref[rows, :] = product(halves(turn_ref[rows, :]), (table_ref[kind, 0], table_ref[kind, 1]))
+    step_rows = 16
+
+    def chunk(index, carry):
+        row = pl.multiple_of(index * step_rows, step_rows)
+        real, imag = [], []
+        for g in range(1, groups):
+            place = pl.ds(g * cols + row, step_rows)
+            re, im = mid_ref[place, :lanes], mid_ref[place, lanes:]
+            cos, sin = twiddle_ref[0, g : g + 1, :], twiddle_ref[1, g : g + 1, :]
+            real.append(re * cos - im * sin)
+            imag.append(im * cos + re * sin)
+        place = pl.ds(row, step_rows)
+        values = radix_inverse(mid_ref[place, :lanes], mid_ref[place, lanes:], real, imag)
+        for n, value in enumerate(values):
+            out_ref[own ^ (n // here), n % here, place, :] = value
+        return carry
+
+    lax.fori_loop(0, cols // step_rows, chunk, 0)
+
+
+def final_kernel(plan, own_ref, *refs):
+    pieces, (out_ref, line_ref) = refs[:-2], refs[-2:]
+    own = own_ref[0]
+    for step in range(plan.gx):
+        start = pl.multiple_of((own ^ step) * plan.cols, 8)
+        for a in range(plan.here):
+            line_ref[a, pl.ds(start, plan.cols), :] = pieces[step][a]
+    for a in range(plan.here):
+        out_ref[a * lanes : (a + 1) * lanes, :] = line_ref[a].T
+
+
+def swap_gx(plan, pieces):
+    got = [pieces[0]]
+    for step in range(1, plan.gx):
+        got.append(lax.ppermute(pieces[step], "gx", [(k, k ^ step) for k in range(plan.gx)]))
+    return got
+
+
+def build_kernels(plan):
+    vmem, f32, bf16 = pltpu.VMEM, jnp.float32, jnp.bfloat16
+    size, cols, groups = 2 * lanes, plan.cols, plan.groups
+    piece_shape = (plan.gx, plan.here, cols, lanes)
+
+    def local(thickness, bed_uplift, flux_x, flux_y, mass_balance, ice_mask):
+        own = lax.axis_index("gx").reshape(1)
+        position = (lax.axis_index("gy") * plan.gx + lax.axis_index("gx")).reshape(1)
+        uplift, face_x, face_y = send_uplift(plan, own, bed_uplift, flux_x, flux_y)
+        lower_face = passed_along(face_x, "gx", 1)
+        left_face = passed_along(face_y, "gy", 1)
+        lines_u = swap_gx(plan, uplift)
+        thickness_new, load = call(
+            lambda *refs: load_kernel(plan, *refs),
+            [thickness.shape, piece_shape],
+            [],
+            [own],
+            *(thickness, flux_x, flux_y, mass_balance, ice_mask, lower_face, left_face),
+        )
+        lines_v = swap_gx(plan, load)
+        twiddle = plan.slot_twiddle()
+        forward = np.stack([table_halves(table) for table in plan.slot_matrix()])
+        (spectrum,) = call(
+            lambda *refs: forward_kernel(plan, *refs),
+            [(plan.devices, plan.rows, 2 * groups * cols)],
+            [vmem((plan.radix, cols, lanes), f32)] + [vmem((2 * groups * cols, size), bf16)] * 2,
+            [own],
+            *(lines_u + lines_v + [twiddle, forward]),
+        )
+        received = exchange_all(spectrum)
+        source, line = plan.source_matrix(), plan.line_matrix()
+        scale = np.float32(1.0 / plan.length_y)
+        tables = [table_halves(table) for table in (source, line, line.T * scale, source.T)]
+        (middle,) = call(
+            lambda *refs: middle_kernel(plan, *refs),
+            [(plan.devices, plan.rows, groups * cols)],
+            [vmem((2 * groups * cols, size), bf16)] * 2 + [vmem(((groups + 1) * cols, size), bf16)] * 2 + [vmem(((groups + 1) * cols, size), f32)],
+            [position],
+            *([received] + tables + [plan.line_twiddle()]),
+        )
+        back = exchange_all(middle)
+        inverse = np.stack([table_halves(table) for table in plan.slot_inverse()])
+        (bed,) = call(
+            lambda *refs: inverse_kernel(plan, *refs),
+            [piece_shape],
+            [vmem((groups * cols, size), f32)] * 2,
+            [own],
+            *(back, twiddle, inverse),
+        )
+        (bed_new,) = call(
+            lambda *refs: final_kernel(plan, *refs),
+            [thickness.shape],
+            [vmem((plan.here, plan.gx * cols, lanes), f32)],
+            [own],
+            *swap_gx(plan, bed),
+        )
+        return thickness_new, bed_new
+
+    return local
+
+
 def build(plan):
+    if plan.devices * plan.rows == 2 * lanes and plan.cols % 16 == 0 and plan.radix <= 16 and plan.gx in (2, 4, 8):
+        return build_kernels(plan)
+
     def local(thickness, bed_uplift, flux_x, flux_y, mass_balance, ice_mask):
         lower_face = passed_along(flux_x[-1:, :], "gx", 1)
         left_face = passed_along(flux_y[:, -1:], "gy", 1)

time: 133 us -> 98 us (0.74)
  local copies, waits for them, and re-layouts: 20.2 us -> 1.3 us
  other arithmetic: 11.8 us -> 0 us
  Pallas kernels: 0 us -> 10.9 us
  waiting for transfers between devices: 53.9 us -> 44.2 us
  matrix products: 6.1 us -> 0 us
  starting transfers between devices: 17.7 us -> 19.1 us
    pallas_call x0 -> x6, Pallas kernels: none -> 10.9 us  [the longest x5 8.56 us: call(): return run(*scalars, *operands)]
    ppermute x6 -> x9, waiting for transfers between devices: 24.7 us -> 15.1 us  [swap_gx(): lax.ppermute(pieces[step], 'gx', [(k, k ^ step) for k in range(plan.gx)])]
    dot_general x8 -> x0, matrix products: 6.1 us -> none  [the longest x3 1.94 us: mul(): return jnp.matmul(a, b, precision=highest)]
    another operation x6 -> x0, other arithmetic: 4.79 us -> none  [the longest x2 2.63 us: exchange_gx(): stacked = jnp.stack(pieces)]
    reshape x6 -> x0, local copies, waits for them, and re-layouts: 4.11 us -> none  [the longest x2 1.99 us: to_lines(): split = field.reshape(plan.here, lanes, plan.gx, plan.cols)]
    unnamed x55 -> x26, local copies, waits for them, and re-layouts: 3.56 us -> 0.06 us
    another operation x3 -> x0, local copies, waits for them, and re-layouts: 3.22 us -> none  [the longest x1 2.63 us: forward_x(): return spectrum.transpose(2, 0, 1, 3).reshape(plan.devices, plan.rows, -1)]
    ppermute x6 -> x9, starting transfers between devices: 5.46 us -> 8.55 us  [swap_gx(): lax.ppermute(pieces[step], 'gx', [(k, k ^ step) for k in range(plan.gx)])]
  transfers between devices with their start and end apart: 9 -> 12, of which waited for: 6 -> 5; matrix products, arithmetic and copies ran while one was open for 2% -> 1% of each run, Pallas kernels for 0% -> 1%
where the time goes in v1:
time: 98 us; the launch traced here: 97.8 us
  waiting for transfers between devices  44.2 us (45%)
  blocking collectives  21.4 us (22%)
  starting transfers between devices  19.1 us (19%)
  Pallas kernels  10.9 us (11%)
  local copies, waits for them, and re-layouts  1.3 us (1%)
    all_to_all x1, waiting for transfers between devices, exchange_all(): lax.all_to_all(value, ('gy', 'gx'), split_axis=0, concat_axis=0, tiled=True)  29 us
    all_to_all x1, blocking collectives, exchange_all(): lax.all_to_all(value, ('gy', 'gx'), split_axis=0, concat_axis=0, tiled=True)  21.4 us
    ppermute x9, waiting for transfers between devices, swap_gx(): lax.ppermute(pieces[step], 'gx', [(k, k ^ step) for k in range(plan.gx)])  15.1 us
    pallas_call x5, Pallas kernels, call(): return run(*scalars, *operands)  8.56 us
    ppermute x9, starting transfers between devices, swap_gx(): lax.ppermute(pieces[step], 'gx', [(k, k ^ step) for k in range(plan.gx)])  8.55 us
    ppermute x2, starting transfers between devices, passed_along(): lax.ppermute(value, axis, [(source, source + steps) for source in range(l...  6.63 us
    all_to_all x1, starting transfers between devices, exchange_all(): lax.all_to_all(value, ('gy', 'gx'), split_axis=0, concat_axis=0, tiled=True)  3.98 us
    pallas_call x1, Pallas kernels, send_uplift(): return run(own, bed_uplift, flux_x, flux_y)  2.36 us
  transfers between devices with their start and end apart: 12, of which 5 were waited for; matrix products, arithmetic and copies ran while one was open for 1% of the time, Pallas kernels for 1%

profile of v1, /device:TPU:0, one launch (start us, length us, event | category | flops | bytes accessed | tf_op | source)
XLA Modules:
  0.0 97.8 jit_solution(7518496851259903951)
XLA Ops:
  0.6 0.0 copy-start
  0.6 0.0 copy-start.1
  0.7 0.0 copy-start.2
  0.7 0.0 copy-start.3
  0.7 0.0 copy-start.4
  0.7 2.4 %shard_map.149 = (f32[4,3,96,128]{3,2,1,0:T(8,128)}, f32[1,384]{1,0:T(1,128)}, f32[1,384]{1,0:T(1,128)}) custom-call(s32[1]{0:T(128)} %bitcast.refs_0_, f32[384,384]{1,0:T(8,128)} %refs_1_.2, f32[384,384]{1,0:T(8,128)} %refs_2_.5, f32[384,384]{1,0:T(8,128)} %refs_3_.5), custom_call_target="tpu_custom_call" | custom-call | tf_op jit(solution)/shard_map/pallas_call | solution.py:341
  3.0 2.4 %collective-permute-start = (f32[1,384]{1,0:T(1,128)}, f32[1,384]{1,0:T(1,128)S(1)}, u32[]{:S(2)}, u32[]{:S(2)}) collective-permute-start(f32[1,384]{1,0:T(1,128)} %get-tuple-element.7), channel_id=1, source_target_pairs={{0,8},{8,16},{16,24},{1,9},{9,17},{17,25},{2,10},{10,18},{18,26},{... | collective-permute-start | bytes 4616 | tf_op jit(solution)/shard_map/ppermute | solution.py:176
  5.4 4.2 %collective-permute-start.1 = (f32[1,384]{1,0:T(1,128)}, f32[1,384]{1,0:T(1,128)S(1)}, u32[]{:S(2)}, u32[]{:S(2)}) collective-permute-start(f32[1,384]{1,0:T(1,128)} %get-tuple-element.8), channel_id=1, source_target_pairs={{0,1},{1,2},{2,3},{3,4},{4,5},{5,6},{6,7},{8,9},{9,10},{10,11},{11... | collective-permute-start | bytes 4616 | tf_op jit(solution)/shard_map/ppermute | solution.py:176
  9.7 1.2 %slice_bitcast_fusion.8 = (f32[3,96,128]{2,1,0:T(8,128)S(1)}, f32[3,96,128]{2,1,0:T(8,128)S(1)}, f32[3,96,128]{2,1,0:T(8,128)S(1)}, f32[3,96,128]{2,1,0:T(8,128)S(1)}) fusion(f32[4,3,96,128]{3,2,1,0:T(8,128)} %get-tuple-element.10), kind=kLoop, calls=%fused_computation.8 | loop fusion | bytes 1179648 | tf_op jit(solution)/shard_map/squeeze | solution.py:533
  10.9 0.3 collective-permute-start.4
  11.1 2.9 %collective-permute-start.3 = (f32[3,96,128]{2,1,0:T(8,128)S(1)}, f32[3,96,128]{2,1,0:T(8,128)S(1)}, u32[]{:S(2)}, u32[]{:S(2)}) collective-permute-start(f32[3,96,128]{2,1,0:T(8,128)S(1)} %get-tuple-element.21), channel_id=1, source_target_pairs={{0,16},{8,24},{16,0},{24,8},{1,17},{9,25},{17,1},{25,9},{2,18},{10... | collective-permute-start | bytes 442376 | tf_op jit(solution)/shard_map/ppermute | solution.py:533
  14.1 0.0 collective-permute-start.2
  14.1 0.0 collective-permute-done.refs_6_
  14.1 0.0 collective-permute-done.1.refs_7_
  14.1 0.0 copy-done
  14.1 0.0 copy-done.1
  14.1 0.0 copy-done.2
  14.1 0.0 copy-done.3
  14.1 0.0 copy-done.4
  14.1 1.3 %shard_map.150 = (f32[384,384]{1,0:T(8,128)}, f32[4,3,96,128]{3,2,1,0:T(8,128)S(1)}) custom-call(s32[1]{0:T(128)} %bitcast.refs_0_, f32[384,384]{1,0:T(8,128)S(1)} %copy-done.2, f32[384,384]{1,0:T(8,128)S(1)} %copy-done, f32[384,384]{1,0:T(8,128)S(1)} %copy-done.1, f32[384,384]{1,0:T(8,128)S(1)} %copy-done.3, s32[384,384]{1,0:T(8,128)S(1)} %copy-done.4, ...), custom_call_target="tpu_custom_call" | custom-call | tf_op jit(solution)/shard_map/pallas_call | solution.py:306
  15.4 0.2 collective-permute-start.7
  15.6 2.0 %collective-permute-start.6 = (f32[3,96,128]{2,1,0:T(8,128)S(1)}, f32[3,96,128]{2,1,0:T(8,128)S(1)}, u32[]{:S(2)}, u32[]{:S(2)}) collective-permute-start(f32[3,96,128]{2,1,0:T(8,128)S(1)} %get-tuple-element.17), channel_id=1, source_target_pairs={{0,16},{8,24},{16,0},{24,8},{1,17},{9,25},{17,1},{25,9},{2,18},{10... | collective-permute-start | bytes 442376 | tf_op jit(solution)/shard_map/ppermute | solution.py:533
  17.6 0.0 collective-permute-done.4.refs_4_
  17.6 1.2 %collective-permute-start.5 = (f32[3,96,128]{2,1,0:T(8,128)S(1)}, f32[3,96,128]{2,1,0:T(8,128)S(1)}, u32[]{:S(2)}, u32[]{:S(2)}) collective-permute-start(f32[3,96,128]{2,1,0:T(8,128)S(1)} %get-tuple-element.18), channel_id=1, source_target_pairs={{0,8},{8,0},{16,24},{24,16},{1,9},{9,1},{17,25},{25,17},{2,10},{10... | collective-permute-start | bytes 442376 | tf_op jit(solution)/shard_map/ppermute | solution.py:533
  18.9 3.0 %collective-permute-done.3.refs_3_ = f32[3,96,128]{2,1,0:T(8,128)S(1)} collective-permute-done((f32[3,96,128]{2,1,0:T(8,128)S(1)}, f32[3,96,128]{2,1,0:T(8,128)S(1)}, u32[]{:S(2)}, u32[]{:S(2)}) %collective-permute-start.3) | collective-permute-done | bytes 147488 | tf_op jit(solution)/shard_map/ppermute | solution.py:533
  21.9 0.0 collective-permute-done.2.refs_2_
  21.9 0.0 collective-permute-done.7.refs_8_
  21.9 4.6 %collective-permute-done.6.refs_7_ = f32[3,96,128]{2,1,0:T(8,128)S(1)} collective-permute-done((f32[3,96,128]{2,1,0:T(8,128)S(1)}, f32[3,96,128]{2,1,0:T(8,128)S(1)}, u32[]{:S(2)}, u32[]{:S(2)}) %collective-permute-start.6) | collective-permute-done | bytes 147488 | tf_op jit(solution)/shard_map/ppermute | solution.py:533
  26.6 0.0 collective-permute-done.5.refs_6_
  26.6 0.0 copy-done.5
  26.6 0.0 copy-done.12
  26.6 2.8 %shard_map.151 = f32[32,8,1152]{2,1,0:T(8,128)} custom-call(s32[1]{0:T(128)} %bitcast.refs_0_, f32[3,96,128]{2,1,0:T(8,128)S(1)} %get-tuple-element.23.refs_1_, f32[3,96,128]{2,1,0:T(8,128)S(1)} %collective-permute-done.2.refs_2_, f32[3,96,128]{2,1,0:T(8,128)S(1)} %collective-permute-done.3.refs_3_, f32[3,96,128]{2,1,0:T(8,128)S(1)} %collective-permute-done.4.refs_4_, ...), custom_call_target="tpu_custom_call" | custom-call | tf_op jit(solution)/shard_map/pallas_call | solution.py:306
  29.4 0.0 copy-start.11
  29.4 4.0 %all-to-all-start = ((f32[32,8,1152]{2,1,0:T(8,128)}), f32[32,8,1152]{2,1,0:T(8,128)S(1)}, u32[]{:S(2)}, u32[]{:S(2)}) async-start(f32[32,8,1152]{2,1,0:T(8,128)} %shard_map.151), calls=%async_computation | async-start | bytes 2359296 | tf_op jit(solution)/shard_map/all_to_all | solution.py:170
  33.4 29.0 %all-to-all-done.refs_1_ = f32[32,8,1152]{2,1,0:T(8,128)S(1)} async-done(((f32[32,8,1152]{2,1,0:T(8,128)}), f32[32,8,1152]{2,1,0:T(8,128)S(1)}, u32[]{:S(2)}, u32[]{:S(2)}) %all-to-all-start) | async-done | bytes 1179680 | tf_op jit(solution)/shard_map/all_to_all | solution.py:170
  62.4 0.0 copy-done.7
  62.4 0.0 copy-done.8
  62.4 2.6 %shard_map.152 = f32[32,8,576]{2,1,0:T(8,128)S(1)} custom-call(s32[1]{0:T(128)} %bitcast.1.refs_0_, f32[32,8,1152]{2,1,0:T(8,128)S(1)} %all-to-all-done.refs_1_, bf16[2,256,256]{2,1,0:T(8,128)(2,1)S(1)} %copy-done.8, bf16[2,192,192]{2,1,0:T(8,128)(2,1)S(1)} %copy-done.10, bf16[2,192,192]{2,1,0:T(8,128)(2,1)S(1)} %copy-done.9, ...), custom_call_target="tpu_custom_call" | custom-call | tf_op jit(solution)/shard_map/pallas_call | solution.py:306
  65.1 0.0 copy-start.6
  65.1 21.4 %all_to_all.10.refs_1_ = f32[32,8,576]{2,1,0:T(8,128)S(1)} all-to-all(f32[32,8,576]{2,1,0:T(8,128)S(1)} %shard_map.152), channel_id=1, replica_groups=mesh['gx'=4,'gy'=8] {'gy','gx'}, dimensions={0} | all-to-all | bytes 1179648 | tf_op jit(solution)/shard_map/all_to_all | solution.py:170
  86.5 0.8 shard_map.153
  87.3 1.2 %collective-permute-start.10 = (f32[3,96,128]{2,1,0:T(8,128)S(1)}, f32[3,96,128]{2,1,0:T(8,128)S(1)}, u32[]{:S(2)}, u32[]{:S(2)}) collective-permute-start(f32[3,96,128]{2,1,0:T(8,128)S(1)} %get-tuple-element.12), channel_id=1, source_target_pairs={{0,24},{8,16},{16,8},{24,0},{1,25},{9,17},{17,9},{25,1},{2,26},{10... | collective-permute-start | bytes 442376 | tf_op jit(solution)/shard_map/ppermute | solution.py:533
  88.6 0.5 collective-permute-start.9
  89.1 0.2 collective-permute-start.8
  89.2 4.0 %collective-permute-done.10.refs_4_ = f32[3,96,128]{2,1,0:T(8,128)S(1)} collective-permute-done((f32[3,96,128]{2,1,0:T(8,128)S(1)}, f32[3,96,128]{2,1,0:T(8,128)S(1)}, u32[]{:S(2)}, u32[]{:S(2)}) %collective-permute-start.10) | collective-permute-done | bytes 147488 | tf_op jit(solution)/shard_map/ppermute | solution.py:533
  93.3 3.4 %collective-permute-done.9.refs_3_ = f32[3,96,128]{2,1,0:T(8,128)S(1)} collective-permute-done((f32[3,96,128]{2,1,0:T(8,128)S(1)}, f32[3,96,128]{2,1,0:T(8,128)S(1)}, u32[]{:S(2)}, u32[]{:S(2)}) %collective-permute-start.9) | collective-permute-done | bytes 147488 | tf_op jit(solution)/shard_map/ppermute | solution.py:533
  96.7 0.0 collective-permute-done.8.refs_2_
  96.7 1.1 %shard_map.154 = f32[384,384]{1,0:T(8,128)} custom-call(s32[1]{0:T(128)} %bitcast.refs_0_, f32[3,96,128]{2,1,0:T(8,128)S(1)} %get-tuple-element.15.refs_1_, f32[3,96,128]{2,1,0:T(8,128)S(1)} %collective-permute-done.8.refs_2_, f32[3,96,128]{2,1,0:T(8,128)S(1)} %collective-permute-done.9.refs_3_, f32[3,96,128]{2,1,0:T(8,128)S(1)} %collective-permute-done.10.refs_4_), custom_call_target="tpu_custom_call" | custom-call | tf_op jit(solution)/shard_map/pallas_call | solution.py:306
  (12 shorter events, 0.1 us)
Async XLA Ops:
  0.6 13.4 %copy-start = (f32[384,384]{1,0:T(8,128)S(1)}, f32[384,384]{1,0:T(8,128)}, u32[]{:S(2)}) copy-start(f32[384,384]{1,0:T(8,128)} %refs_2_.5) | copy-start | bytes 1769476
  0.6 13.4 %copy-start.1 = (f32[384,384]{1,0:T(8,128)S(1)}, f32[384,384]{1,0:T(8,128)}, u32[]{:S(2)}) copy-start(f32[384,384]{1,0:T(8,128)} %refs_3_.5) | copy-start | bytes 1769476
  0.7 13.4 %copy-start.2 = (f32[384,384]{1,0:T(8,128)S(1)}, f32[384,384]{1,0:T(8,128)}, u32[]{:S(2)}) copy-start(f32[384,384]{1,0:T(8,128)} %refs_1_.3) | copy-start | bytes 1769476
  0.7 13.4 %copy-start.3 = (f32[384,384]{1,0:T(8,128)S(1)}, f32[384,384]{1,0:T(8,128)}, u32[]{:S(2)}) copy-start(f32[384,384]{1,0:T(8,128)} %refs_4_.2) | copy-start | bytes 1769476
  0.7 13.4 %copy-start.4 = (s32[384,384]{1,0:T(8,128)S(1)}, s32[384,384]{1,0:T(8,128)}, u32[]{:S(2)}) copy-start(s32[384,384]{1,0:T(8,128)} %refs_5_.2) | copy-start | bytes 1769476
  3.0 11.0 %collective-permute-start = (f32[1,384]{1,0:T(1,128)}, f32[1,384]{1,0:T(1,128)S(1)}, u32[]{:S(2)}, u32[]{:S(2)}) collective-permute-start(f32[1,384]{1,0:T(1,128)} %get-tuple-element.7), channel_id=1, source_target_pairs={{0,8},{8,16},{16,24},{1,9},{9,17},{17,25},{2,10},{10,18},{18,26},{... | collective-permute-start | bytes 4616 | tf_op jit(solution)/shard_map/ppermute | solution.py:176
  5.4 8.6 %collective-permute-start.1 = (f32[1,384]{1,0:T(1,128)}, f32[1,384]{1,0:T(1,128)S(1)}, u32[]{:S(2)}, u32[]{:S(2)}) collective-permute-start(f32[1,384]{1,0:T(1,128)} %get-tuple-element.8), channel_id=1, source_target_pairs={{0,1},{1,2},{2,3},{3,4},{4,5},{5,6},{6,7},{8,9},{9,10},{10,11},{11... | collective-permute-start | bytes 4616 | tf_op jit(solution)/shard_map/ppermute | solution.py:176
  10.9 6.8 %collective-permute-start.4 = (f32[3,96,128]{2,1,0:T(8,128)S(1)}, f32[3,96,128]{2,1,0:T(8,128)S(1)}, u32[]{:S(2)}, u32[]{:S(2)}) collective-permute-start(f32[3,96,128]{2,1,0:T(8,128)S(1)} %get-tuple-element.20), channel_id=1, source_target_pairs={{0,24},{8,16},{16,8},{24,0},{1,25},{9,17},{17,9},{25,1},{2,26},{10... | collective-permute-start | bytes 442376 | tf_op jit(solution)/shard_map/ppermute | solution.py:533
  11.1 10.8 %collective-permute-start.3 = (f32[3,96,128]{2,1,0:T(8,128)S(1)}, f32[3,96,128]{2,1,0:T(8,128)S(1)}, u32[]{:S(2)}, u32[]{:S(2)}) collective-permute-start(f32[3,96,128]{2,1,0:T(8,128)S(1)} %get-tuple-element.21), channel_id=1, source_target_pairs={{0,16},{8,24},{16,0},{24,8},{1,17},{9,25},{17,1},{25,9},{2,18},{10... | collective-permute-start | bytes 442376 | tf_op jit(solution)/shard_map/ppermute | solution.py:533
  14.1 7.9 %collective-permute-start.2 = (f32[3,96,128]{2,1,0:T(8,128)S(1)}, f32[3,96,128]{2,1,0:T(8,128)S(1)}, u32[]{:S(2)}, u32[]{:S(2)}) collective-permute-start(f32[3,96,128]{2,1,0:T(8,128)S(1)} %get-tuple-element.22), channel_id=1, source_target_pairs={{0,8},{8,0},{16,24},{24,16},{1,9},{9,1},{17,25},{25,17},{2,10},{10... | collective-permute-start | bytes 442376 | tf_op jit(solution)/shard_map/ppermute | solution.py:533
  15.4 11.2 %copy-start.5 = (bf16[2,2,256,256]{3,2,1,0:T(8,128)(2,1)S(1)}, bf16[2,2,256,256]{3,2,1,0:T(8,128)(2,1)}, u32[]{:S(2)}) copy-start(bf16[2,2,256,256]{3,2,1,0:T(8,128)(2,1)} %constant.27.clone.refs_10_) | copy-start | bytes 1572868
  15.4 11.2 %copy-start.12 = (f32[2,6,128]{2,1,0:T(8,128)S(1)}, f32[2,6,128]{2,1,0:T(8,128)}, u32[]{:S(2)}) copy-start(f32[2,6,128]{2,1,0:T(8,128)} %constant.26.clone.refs_9_.refs_2_) | copy-start | bytes 18436
  15.4 6.5 %collective-permute-start.7 = (f32[3,96,128]{2,1,0:T(8,128)S(1)}, f32[3,96,128]{2,1,0:T(8,128)S(1)}, u32[]{:S(2)}, u32[]{:S(2)}) collective-permute-start(f32[3,96,128]{2,1,0:T(8,128)S(1)} %get-tuple-element.16), channel_id=1, source_target_pairs={{0,24},{8,16},{16,8},{24,0},{1,25},{9,17},{17,9},{25,1},{2,26},{10... | collective-permute-start | bytes 442376 | tf_op jit(solution)/shard_map/ppermute | solution.py:533
  15.6 10.9 %collective-permute-start.6 = (f32[3,96,128]{2,1,0:T(8,128)S(1)}, f32[3,96,128]{2,1,0:T(8,128)S(1)}, u32[]{:S(2)}, u32[]{:S(2)}) collective-permute-start(f32[3,96,128]{2,1,0:T(8,128)S(1)} %get-tuple-element.17), channel_id=1, source_target_pairs={{0,16},{8,24},{16,0},{24,8},{1,17},{9,25},{17,1},{25,9},{2,18},{10... | collective-permute-start | bytes 442376 | tf_op jit(solution)/shard_map/ppermute | solution.py:533
  17.6 8.9 %collective-permute-start.5 = (f32[3,96,128]{2,1,0:T(8,128)S(1)}, f32[3,96,128]{2,1,0:T(8,128)S(1)}, u32[]{:S(2)}, u32[]{:S(2)}) collective-permute-start(f32[3,96,128]{2,1,0:T(8,128)S(1)} %get-tuple-element.18), channel_id=1, source_target_pairs={{0,8},{8,0},{16,24},{24,16},{1,9},{9,1},{17,25},{25,17},{2,10},{10... | collective-permute-start | bytes 442376 | tf_op jit(solution)/shard_map/ppermute | solution.py:533
  29.4 33.0 %copy-start.7 = (bf16[2,256,256]{2,1,0:T(8,128)(2,1)S(1)}, bf16[2,256,256]{2,1,0:T(8,128)(2,1)}, u32[]{:S(2)}) copy-start(bf16[2,256,256]{2,1,0:T(8,128)(2,1)} %constant.31.clone.refs_5_) | copy-start | bytes 786436
  29.4 33.0 %copy-start.8 = (bf16[2,256,256]{2,1,0:T(8,128)(2,1)S(1)}, bf16[2,256,256]{2,1,0:T(8,128)(2,1)}, u32[]{:S(2)}) copy-start(bf16[2,256,256]{2,1,0:T(8,128)(2,1)} %constant.28.clone.refs_2_) | copy-start | bytes 786436
  29.4 33.0 %copy-start.9 = (bf16[2,192,192]{2,1,0:T(8,128)(2,1)S(1)}, bf16[2,192,192]{2,1,0:T(8,128)(2,1)}, u32[]{:S(2)}) copy-start(bf16[2,192,192]{2,1,0:T(8,128)(2,1)} %constant.30.clone.refs_4_) | copy-start | bytes 442372
  29.4 33.0 %copy-start.10 = (bf16[2,192,192]{2,1,0:T(8,128)(2,1)S(1)}, bf16[2,192,192]{2,1,0:T(8,128)(2,1)}, u32[]{:S(2)}) copy-start(bf16[2,192,192]{2,1,0:T(8,128)(2,1)} %constant.29.clone.refs_3_) | copy-start | bytes 442372
  29.4 33.0 %copy-start.11 = (f32[2,96,128]{2,1,0:T(8,128)S(1)}, f32[2,96,128]{2,1,0:T(8,128)}, u32[]{:S(2)}) copy-start(f32[2,96,128]{2,1,0:T(8,128)} %constant.32.clone.refs_6_) | copy-start | bytes 294916
  29.4 33.0 %all-to-all-start = ((f32[32,8,1152]{2,1,0:T(8,128)}), f32[32,8,1152]{2,1,0:T(8,128)S(1)}, u32[]{:S(2)}, u32[]{:S(2)}) async-start(f32[32,8,1152]{2,1,0:T(8,128)} %shard_map.151), calls=%async_computation | async-start | bytes 2359296 | tf_op jit(solution)/shard_map/all_to_all | solution.py:170
  65.1 21.4 %copy-start.6 = (bf16[2,2,256,256]{3,2,1,0:T(8,128)(2,1)S(1)}, bf16[2,2,256,256]{3,2,1,0:T(8,128)(2,1)}, u32[]{:S(2)}) copy-start(bf16[2,2,256,256]{3,2,1,0:T(8,128)(2,1)} %constant.33.clone.refs_3_) | copy-start | bytes 1572868
  87.3 6.0 %collective-permute-start.10 = (f32[3,96,128]{2,1,0:T(8,128)S(1)}, f32[3,96,128]{2,1,0:T(8,128)S(1)}, u32[]{:S(2)}, u32[]{:S(2)}) collective-permute-start(f32[3,96,128]{2,1,0:T(8,128)S(1)} %get-tuple-element.12), channel_id=1, source_target_pairs={{0,24},{8,16},{16,8},{24,0},{1,25},{9,17},{17,9},{25,1},{2,26},{10... | collective-permute-start | bytes 442376 | tf_op jit(solution)/shard_map/ppermute | solution.py:533
  88.6 8.1 %collective-permute-start.9 = (f32[3,96,128]{2,1,0:T(8,128)S(1)}, f32[3,96,128]{2,1,0:T(8,128)S(1)}, u32[]{:S(2)}, u32[]{:S(2)}) collective-permute-start(f32[3,96,128]{2,1,0:T(8,128)S(1)} %get-tuple-element.13), channel_id=1, source_target_pairs={{0,16},{8,24},{16,0},{24,8},{1,17},{9,25},{17,1},{25,9},{2,18},{10... | collective-permute-start | bytes 442376 | tf_op jit(solution)/shard_map/ppermute | solution.py:533
  89.1 7.6 %collective-permute-start.8 = (f32[3,96,128]{2,1,0:T(8,128)S(1)}, f32[3,96,128]{2,1,0:T(8,128)S(1)}, u32[]{:S(2)}, u32[]{:S(2)}) collective-permute-start(f32[3,96,128]{2,1,0:T(8,128)S(1)} %get-tuple-element.14), channel_id=1, source_target_pairs={{0,8},{8,0},{16,24},{24,16},{1,9},{9,1},{17,25},{25,17},{2,10},{10... | collective-permute-start | bytes 442376 | tf_op jit(solution)/shard_map/ppermute | solution.py:533

commit v2 on v1

--- a/solution.py
+++ b/solution.py
@@ -30,6 +30,8 @@
         self.deep = lanes // self.m_parts
         self.own_groups = self.groups // self.g_parts
         self.rows = 2 * self.deep
+        self.tail = -(-(2 + 2 * self.here) // 8) * 8
+        self.piece_rows = self.here * self.cols + self.tail
 
     def slot_matrix(self):
         n2 = np.arange(lanes)[None, :]
@@ -294,125 +296,306 @@
 def call(body, outs, scratch, scalars, *operands):
     scalar = pl.BlockSpec(memory_space=pltpu.SMEM)
     whole = pl.BlockSpec(memory_space=pltpu.VMEM)
-    shapes = [jax.ShapeDtypeStruct(shape, jnp.float32) for shape in outs]
     run = pl.pallas_call(
         body,
-        out_shape=shapes,
+        out_shape=outs,
         in_specs=[scalar] * len(scalars) + [whole] * len(operands),
         out_specs=[whole] * len(outs),
         scratch_shapes=scratch,
-        compiler_params=pltpu.CompilerParams(vmem_limit_bytes=48 << 20),
+        compiler_params=pltpu.CompilerParams(vmem_limit_bytes=16 << 20),
     )
     return run(*scalars, *operands)
 
 
-def lines_out(plan, own, block, here, out_ref):
-    turned = block.T
-    for part in range(plan.gx):
-        out_ref[own ^ part, here] = turned[part * plan.cols : (part + 1) * plan.cols]
-
-
-def uplift_kernel(plan, own_ref, uplift_ref, flux_x_ref, flux_y_ref, out_ref, face_x_ref, face_y_ref):
+def real_array(*shape):
+    return jax.ShapeDtypeStruct(shape, jnp.float32)
+
+
+def lines_out(plan, own, block, here, turned_ref, out_refs):
+    turned_ref[here] = block.T
+    for step in range(plan.gx):
+        start = pl.multiple_of((own ^ step) * plan.cols, 8)
+        out_refs[step][here * plan.cols : (here + 1) * plan.cols, :] = turned_ref[here, pl.ds(start, plan.cols), :]
+
+
+def own_part(plan, part, row):
+    wide = jnp.concatenate([row, row[:, :lanes]], 1)
+    wide = jnp.broadcast_to(wide, (8, wide.shape[1]))
+    out = wide[:, :lanes]
+    for k in range(1, plan.gx):
+        start = k * plan.cols
+        low = start // lanes * lanes
+        block = wide[:, low : low + 2 * lanes]
+        if start % lanes:
+            block = pltpu.roll(block, 2 * lanes - start % lanes, 1)
+        out = jnp.where(part == k, block[:, :lanes], out)
+    return out[:1]
+
+
+def kernel_call(body, outs, scratch, scalars, inputs, faces=()):
+    whole = pl.BlockSpec(memory_space=pltpu.VMEM)
+    run = pl.pallas_call(
+        body,
+        out_shape=outs,
+        in_specs=[pl.BlockSpec(memory_space=pltpu.SMEM)] * len(scalars) + [pl.BlockSpec(memory_space=pl.ANY)] * len(inputs) + [whole] * len(faces),
+        out_specs=[whole] * len(outs),
+        scratch_shapes=scratch,
+    )
+    return run(*scalars, *inputs, *faces)
+
+
+def uplift_kernel(plan, own_ref, uplift_hbm, flux_x_hbm, flux_y_hbm, *refs):
     own = own_ref[0]
-    size = flux_x_ref.shape[0]
-    face_x_ref[...] = flux_x_ref[7:8, :]
-    face_y_ref[...] = flux_y_ref[...].T[lanes - 1 : lanes, :]
+    out_refs = refs[: plan.gx]
+    field_ref, turned_ref, last_x_ref, last_y_ref, sems = refs[plan.gx :]
+    rows, cols = uplift_hbm.shape
+    copies = [
+        pltpu.make_async_copy(flux_x_hbm.at[pl.ds(rows - 8, 8), :], last_x_ref, sems.at[0]),
+        pltpu.make_async_copy(flux_y_hbm.at[:, pl.ds(cols - lanes, lanes)], last_y_ref, sems.at[1]),
+    ]
     for here in range(plan.here):
-        lines_out(plan, own, uplift_ref[here * lanes : (here + 1) * lanes, :], here, out_ref)
+        source = uplift_hbm.at[pl.ds(here * lanes, lanes), :]
+        copies.append(pltpu.make_async_copy(source, field_ref.at[here], sems.at[2 + here]))
+    for copy in copies:
+        copy.start()
+    for here in range(plan.here):
+        copies[2 + here].wait()
+        lines_out(plan, own, field_ref[here], here, turned_ref, out_refs)
+    copies[0].wait()
+    last_x = last_x_ref[7:8, :]
+    copies[1].wait()
+    last_y = last_y_ref[...].T[lanes - 1 : lanes, :]
+    tail = plan.here * plan.cols
+    parts = [last[:, a * lanes : (a + 1) * lanes] for last in (last_x, last_y) for a in range(plan.here)]
+    parts.append(jnp.zeros((plan.tail - 2 * plan.here, lanes), jnp.float32))
+    parts = jnp.concatenate(parts, 0)
+    for step in range(plan.gx):
+        out_refs[step][tail : tail + plan.tail, :] = parts
 
 
 def send_uplift(plan, own, bed_uplift, flux_x, flux_y):
     rows, cols = bed_uplift.shape
-    run = pl.pallas_call(
+    return kernel_call(
         lambda *refs: uplift_kernel(plan, *refs),
-        grid=(1,),
-        out_shape=[
-            jax.ShapeDtypeStruct((plan.gx, plan.here, plan.cols, lanes), jnp.float32),
-            jax.ShapeDtypeStruct((1, cols), jnp.float32),
-            jax.ShapeDtypeStruct((1, rows), jnp.float32),
+        [real_array(plan.piece_rows, lanes)] * plan.gx,
+        [
+            pltpu.VMEM((plan.here, lanes, cols), jnp.float32),
+            pltpu.VMEM((plan.here, cols, lanes), jnp.float32),
+            pltpu.VMEM((8, cols), jnp.float32),
+            pltpu.VMEM((rows, lanes), jnp.float32),
+            pltpu.SemaphoreType.DMA((2 + plan.here,)),
         ],
-        in_specs=[
-            pl.BlockSpec(memory_space=pltpu.SMEM),
-            pl.BlockSpec((rows, cols), lambda i: (0, 0)),
-            pl.BlockSpec((8, cols), lambda i: (rows // 8 - 1, 0)),
-            pl.BlockSpec((rows, lanes), lambda i: (0, cols // lanes - 1)),
-        ],
+        [own],
+        (bed_uplift, flux_x, flux_y),
     )
-    return run(own, bed_uplift, flux_x, flux_y)
-
-
-def load_kernel(plan, own_ref, thick_ref, fx_ref, fy_ref, mb_ref, mask_ref, face_x_ref, face_y_ref, out_ref, line_ref):
+
+
+def fetch_fields(plan, sources, mask_ref, floats_ref, sems):
+    targets = [floats_ref.at[k] for k in range(4)] + [mask_ref]
+    copies = []
+    for here in range(plan.here):
+        rows = pl.ds(here * lanes, lanes)
+        group = [
+            pltpu.make_async_copy(source.at[rows, :], target.at[rows, :], sems.at[here, k])
+            for k, (source, target) in enumerate(zip(sources, targets))
+        ]
+        for copy in group:
+            copy.start()
+        copies.append(group)
+    return copies
+
+
+def trial_block(floats_ref, here, above, left_edge):
+    rows = slice(here * lanes, (here + 1) * lanes)
+    fx, fy = floats_ref[1, rows, :], floats_ref[2, rows, :]
+    row = lax.broadcasted_iota(jnp.int32, fx.shape, 0)
+    col = lax.broadcasted_iota(jnp.int32, fx.shape, 1)
+    if here:
+        above = floats_ref[1, here * lanes - 1 : here * lanes, :]
+    below = jnp.where(row == 0, jnp.broadcast_to(above, fx.shape) if here or above.ndim else above, pltpu.roll(fx, 1, 0))
+    left = jnp.where(col == 0, left_edge, pltpu.roll(fy, 1, 1))
+    divergence = fx - below + fy - left
+    return floats_ref[0, rows, :] + time_step * (floats_ref[3, rows, :] - divergence)
+
+
+hidden = np.float32(-1e30)
+
+
+def load_kernel(plan, own_ref, *refs):
     own = own_ref[0]
+    sources, refs = refs[:5], refs[5:]
+    line_refs, (mask_ref, floats_ref, turned_ref, sems) = refs[: plan.gx], refs[plan.gx :]
+    copies = fetch_fields(plan, sources, mask_ref, floats_ref, sems)
+    columns_trial, columns_thick = [], []
     for here in range(plan.here):
+        for copy in copies[here]:
+            copy.wait()
         rows = slice(here * lanes, (here + 1) * lanes)
-        fx, fy = fx_ref[rows, :], fy_ref[rows, :]
-        row = lax.broadcasted_iota(jnp.int32, fx.shape, 0)
-        col = lax.broadcasted_iota(jnp.int32, fx.shape, 1)
-        above = face_x_ref[...] if here == 0 else fx_ref[here * lanes - 1 : here * lanes, :]
-        below = jnp.where(row == 0, jnp.broadcast_to(above, fx.shape), pltpu.roll(fx, 1, 0))
-        side = jnp.broadcast_to(face_y_ref[:, rows], (lanes, lanes)).T
-        left = jnp.where(col == 0, jnp.concatenate([side] * (fx.shape[1] // lanes), 1), pltpu.roll(fy, 1, 1))
-        divergence = fx - below + fy - left
-        thick, mask = thick_ref[rows, :], mask_ref[rows, :]
-        trial = thick + time_step * (mb_ref[rows, :] - divergence)
-        new = jnp.where(mask == 2, 0.0, jnp.maximum(trial, 0.0))
-        out_ref[rows, :] = new
-        lines_out(plan, own, jnp.where(mask == 0, new - thick, 0.0), here, line_ref)
-
-
-def forward_kernel(plan, own_ref, *refs):
-    pieces, (twiddle_ref, table_ref, out_ref, line_ref, high_ref, low_ref) = refs[:-6], refs[-6:]
+        trial = trial_block(floats_ref, here, jnp.float32(0.0), 0.0)
+        free = mask_ref[rows, :] == 0
+        thick = jnp.where(free, floats_ref[0, rows, :], 0.0)
+        trial = jnp.where(free, trial, hidden)
+        lines_out(plan, own, jnp.maximum(trial, 0.0) - thick, here, turned_ref, line_refs)
+        lane = lax.broadcasted_iota(jnp.int32, (lanes, lanes), 1)
+        packed = jnp.where(lane == 0, trial[:, :lanes], pltpu.roll(thick[:, :lanes], 1, 1)).T
+        columns_trial.append(packed[0:1])
+        columns_thick.append(packed[1:2])
+        if here == 0:
+            row_trial, row_thick = trial[0:1], thick[0:1]
+    tail = plan.here * plan.cols
+    rest = plan.tail - 2 - 2 * plan.here
+    for step in range(plan.gx):
+        parts = [own_part(plan, own ^ step, row_trial), own_part(plan, own ^ step, row_thick)] + columns_trial + columns_thick
+        if rest:
+            parts.append(jnp.zeros((rest, lanes), jnp.float32))
+        line_refs[step][tail : tail + plan.tail, :] = jnp.concatenate(parts, 0)
+
+
+def field_scratch(shape):
+    return [
+        pltpu.VMEM(shape, jnp.int32),
+        pltpu.VMEM((4,) + shape, jnp.float32),
+    ]
+
+
+def make_load(plan, own, fields):
+    shape = fields[0].shape
+    scratch = field_scratch(shape) + [
+        pltpu.VMEM((plan.here, shape[1], lanes), jnp.float32),
+        pltpu.SemaphoreType.DMA((plan.here, 5)),
+    ]
+    outs = [real_array(plan.piece_rows, lanes)] * plan.gx
+    return kernel_call(lambda *refs: load_kernel(plan, *refs), outs, scratch, [own], fields)
+
+
+def row_above(plan, own, block, tails):
+    above = [jnp.zeros((1, lanes), jnp.float32)] * plan.here
+    for step in range(plan.gx):
+        match = (own ^ step) + 1 == block
+        above = [jnp.where(match, tails[step][a : a + 1, :], above[a]) for a in range(plan.here)]
+    return jnp.concatenate(above, 1)
+
+
+def thickness_kernel(plan, own_ref, *refs):
     own = own_ref[0]
+    sources, (tails_ref, side_ref, out_ref, mask_ref, floats_ref, sems) = refs[:5], refs[5:]
+    copies = fetch_fields(plan, sources, mask_ref, floats_ref, sems)
+    above = row_above(plan, own, own, [tails_ref[step] for step in range(plan.gx)])
+    for here in range(plan.here):
+        for copy in copies[here]:
+            copy.wait()
+        rows = slice(here * lanes, (here + 1) * lanes)
+        side = jnp.broadcast_to(side_ref[own * plan.here + here], (lanes, lanes)).T
+        side = jnp.concatenate([side] * (out_ref.shape[1] // lanes), 1)
+        trial = trial_block(floats_ref, here, above, side)
+        out_ref[rows, :] = jnp.where(mask_ref[rows, :] == 2, 0.0, jnp.maximum(trial, 0.0))
+
+
+def make_thickness(plan, own, fields, faces):
+    shape = fields[0].shape
+    scratch = field_scratch(shape) + [pltpu.SemaphoreType.DMA((plan.here, 5))]
+    return kernel_call(lambda *refs: thickness_kernel(plan, *refs), [real_array(*shape)], scratch, [own], fields, faces)[0]
+
+
+def finish_load(plan, own, line_ref, uplift_tails, load_tails, side_ref):
+    cols, here = plan.cols, plan.here
+    row = lax.broadcasted_iota(jnp.int32, (8, lanes), 0)
+    lane = lax.broadcasted_iota(jnp.int32, (8, lanes), 1)
+    wide_lane = lax.broadcasted_iota(jnp.int32, (cols, lanes), 1)
+    for step in range(plan.gx):
+        block = own ^ step
+        above = own_part(plan, own, row_above(plan, own, block, uplift_tails))
+        tail = load_tails[step]
+        new = jnp.maximum(tail[0:1, :] + time_step * above, 0.0) - tail[1:2, :]
+        turned = jnp.broadcast_to(new, (lanes, lanes)).T[:cols]
+        line_ref[block * here] = jnp.where(wide_lane == 0, turned, line_ref[block * here])
+
+        @pl.when(own == 0)
+        def _(block=block, tail=tail, above=above):
+            for a in range(here):
+                corner = jnp.where(lane[:1] == 0, jnp.broadcast_to(above[:, :1], (1, lanes)), 0.0) if a == 0 else 0.0
+                trial = tail[2 + a : 3 + a, :] + time_step * (side_ref[block * here + a] + corner)
+                line_ref[block * here + a, 0:1, :] = jnp.maximum(trial, 0.0) - tail[2 + here + a : 3 + here + a, :]
+
+
+def forward_kernel(plan, lead, own_ref, *refs):
+    pieces, refs = refs[: plan.gx], refs[plan.gx :]
     cols, radix, groups, here = plan.cols, plan.radix, plan.groups, plan.here
+    own = own_ref[0]
+    tail = slice(here * cols, here * cols + plan.tail)
+    if lead:
+        uplift_tails, side_ref, other_ref, *refs = refs
+        twiddle_ref, table_ref, out_ref, line_ref, high_ref, low_ref = refs
+    else:
+        twiddle_ref, table_ref, out_ref, tails_ref, edge_ref, line_ref, high_ref, low_ref = refs
+        for step in range(plan.gx):
+            tails_ref[step] = pieces[step][tail, :]
+            for a in range(here):
+                edge_ref[(own ^ step) * here + a] = pieces[step][here * (cols + 1) + a : here * (cols + 1) + a + 1, :]
     step_rows = 16
-    for field in range(2):
-        for step in range(plan.gx):
-            piece = pieces[field * plan.gx + step]
-            for a in range(here):
-                line_ref[(own ^ step) * here + a] = piece[a]
-
-        def chunk(index, carry, field=field):
-            row = pl.multiple_of(index * step_rows, step_rows)
-            real, imag = radix_forward([line_ref[n, pl.ds(row, step_rows), :] for n in range(radix)])
-            for g in range(groups):
-                if g == 0:
-                    first, second = real[0], real[groups]
-                else:
-                    cos, sin = twiddle_ref[0, g : g + 1, :], twiddle_ref[1, g : g + 1, :]
-                    first = real[g] * cos + imag[g - 1] * sin
-                    second = imag[g - 1] * cos - real[g] * sin
-                high, low = halves(jnp.concatenate([first, second], 1))
-                place = pl.ds((2 * g + field) * cols + row, step_rows)
-                high_ref[place, :] = high
-                low_ref[place, :] = low
-            return carry
-
-        lax.fori_loop(0, cols // step_rows, chunk, 0)
-
+    total = groups * cols
+    for step in range(plan.gx):
+        for a in range(here):
+            line_ref[(own ^ step) * here + a] = pieces[step][a * cols : (a + 1) * cols, :]
+    if lead:
+        finish_load(plan, own, line_ref, [uplift_tails[k] for k in range(plan.gx)], [piece[tail, :] for piece in pieces], side_ref)
+    skip = lead % lanes
+
+    def chunk(index, carry):
+        row = pl.multiple_of(index * step_rows, step_rows)
+        real, imag = radix_forward([line_ref[n, pl.ds(row, step_rows), :] for n in range(radix)])
+        for g in range(groups):
+            if g == 0:
+                first, second = real[0], real[groups]
+            else:
+                cos, sin = twiddle_ref[0, g : g + 1, :], twiddle_ref[1, g : g + 1, :]
+                first = real[g] * cos + imag[g - 1] * sin
+                second = imag[g - 1] * cos - real[g] * sin
+            high, low = halves(jnp.concatenate([first, second], 1))
+            place = pl.ds(skip + g * cols + row, step_rows)
+            high_ref[place, :] = high
+            low_ref[place, :] = low
+        return carry
+
+    lax.fori_loop(0, cols // step_rows, chunk, 0)
+    for edge in ((0, skip), (skip + total, high_ref.shape[0])):
+        if edge[0] < edge[1]:
+            high_ref[edge[0] : edge[1], :] = jnp.zeros((edge[1] - edge[0], 2 * lanes), jnp.bfloat16)
+            low_ref[edge[0] : edge[1], :] = jnp.zeros((edge[1] - edge[0], 2 * lanes), jnp.bfloat16)
     general = (table_ref[0, 0], table_ref[0, 1])
     special = (table_ref[1, 0], table_ref[1, 1])
-    edge = 2 * cols
-    starts = []
-    for start in range(0, 2 * groups * cols, lanes):
+    before = lead - skip
+    for start in range(0, before, lanes):
+        out_ref[:, :, start : start + lanes] = other_ref[:, :, start : start + lanes]
+    for start in range(0, high_ref.shape[0], lanes):
         rows = slice(start, start + lanes)
         data = (high_ref[rows, :], low_ref[rows, :])
-        if start + lanes <= edge:
+        end = skip + cols
+        lane = lax.broadcasted_iota(jnp.int32, (2 * lanes, lanes), 1)
+        if start + lanes <= end:
             out = product(special, data, True)
         else:
             out = product(general, data, True)
-            if start < edge:
-                lane = lax.broadcasted_iota(jnp.int32, out.shape, 1)
-                out = jnp.where(lane < edge - start, product(special, data, True), out)
-        out_ref[:, :, start : start + lanes] = out.reshape(plan.devices, plan.rows, lanes)
-    size = 2 * lanes
-    block = out_ref[0, :, :size]
-    row = lax.broadcasted_iota(jnp.int32, block.shape, 0)
-    lane = lax.broadcasted_iota(jnp.int32, block.shape, 1)
-    swapped = pltpu.roll(block, plan.deep, 0)
-    to_left, to_right = pltpu.roll(swapped, size - cols, 1), pltpu.roll(swapped, cols, 1)
-    block = jnp.where((row == plan.deep) & (lane < cols), to_left, block)
-    block = jnp.where((row == 0) & (lane >= cols) & (lane < 2 * cols), to_right, block)
-    out_ref[0, :, :size] = block
+            if start < end:
+                out = jnp.where(lane < end - start, product(special, data, True), out)
+        out = out.reshape(plan.devices, plan.rows, lanes)
+        at = before + start
+        if start < skip:
+            lane = lax.broadcasted_iota(jnp.int32, out.shape, 2)
+            out = jnp.where(lane < skip - start, other_ref[:, :, at : at + lanes], out)
+        out_ref[:, :, at : at + lanes] = out
+    if lead:
+        one, two = out_ref[0, :, :lanes], out_ref[0, :, before : before + 2 * lanes]
+        row = lax.broadcasted_iota(jnp.int32, two.shape, 0)
+        lane = lax.broadcasted_iota(jnp.int32, two.shape, 1)
+        wide = pltpu.roll(jnp.concatenate([one, one], 1), plan.deep, 0)
+        to_right = pltpu.roll(wide, skip, 1) if skip else wide
+        swapped = pltpu.roll(two, plan.deep, 0)
+        to_left = pltpu.roll(swapped, 2 * lanes - skip, 1) if skip else swapped
+        take = (row == plan.deep) & (lane < cols)
+        out_ref[0, :, :lanes] = jnp.where(take, to_left, jnp.concatenate([one, one], 1))[:, :lanes]
+        take = (row == 0) & (lane >= skip) & (lane < skip + cols)
+        out_ref[0, :, before : before + 2 * lanes] = jnp.where(take, to_right, two)
 
 
 def middle_kernel(plan, position_ref, in_ref, t1_ref, t2_ref, t2i_ref, t1i_ref, twiddle_ref, out_ref, high_ref, low_ref, back_high, back_low, turn_ref):
@@ -434,12 +617,16 @@
     m = position * deep + q
     special = jnp.broadcast_to((position == 0) & (q == 0), (cols, width))
     results = []
+    mixed = []
     for g in range(groups):
-        rows = slice(2 * g * cols, 2 * (g + 1) * cols)
-        mixed = product((high_ref[rows, :], low_ref[rows, :]), t1)
+        if g % 2 == 0:
+            mixed = []
+            for field in range(2):
+                rows = slice((field * groups + g) * cols, (field * groups + min(g + 2, groups)) * cols)
+                mixed.append(product((high_ref[rows, :], low_ref[rows, :]), t1))
         sides = []
         for field in range(2):
-            part = mixed[field * cols : (field + 1) * cols]
+            part = mixed[field][(g % 2) * cols : (g % 2 + 1) * cols]
             re, im = part[:, :width], part[:, width:]
             sides.append(jnp.concatenate([re * cos + im * sin, im * cos - re * sin], 0))
         spectra = product(t2, halves(jnp.concatenate(sides, 1)))
@@ -483,7 +670,8 @@
         out_ref[:, :, start : start + keep] = block.reshape(count, plan.rows, lanes)[:, :, :keep]
 
 
-def inverse_kernel(plan, own_ref, in_ref, twiddle_ref, table_ref, out_ref, turn_ref, mid_ref):
+def inverse_kernel(plan, own_ref, in_ref, twiddle_ref, table_ref, *refs):
+    out_refs, (line_ref, turn_ref, mid_ref) = refs[: plan.gx], refs[plan.gx :]
     own = own_ref[0]
     cols, groups, here = plan.cols, plan.groups, plan.here
     size = 2 * lanes
@@ -510,10 +698,13 @@
         place = pl.ds(row, step_rows)
         values = radix_inverse(mid_ref[place, :lanes], mid_ref[place, lanes:], real, imag)
         for n, value in enumerate(values):
-            out_ref[own ^ (n // here), n % here, place, :] = value
+            line_ref[n, place, :] = value
         return carry
 
     lax.fori_loop(0, cols // step_rows, chunk, 0)
+    for step in range(plan.gx):
+        for a in range(here):
+            out_refs[step][a] = line_ref[(own ^ step) * here + a]
 
 
 def final_kernel(plan, own_ref, *refs):
@@ -537,58 +728,65 @@
 def build_kernels(plan):
     vmem, f32, bf16 = pltpu.VMEM, jnp.float32, jnp.bfloat16
     size, cols, groups = 2 * lanes, plan.cols, plan.groups
-    piece_shape = (plan.gx, plan.here, cols, lanes)
+    half = groups * cols
+    pieces = [real_array(plan.here, cols, lanes)] * plan.gx
+    line = vmem((plan.radix, cols, lanes), f32)
+
+    def forward(lead, own, *operands):
+        skip = lead % lanes
+        rounded = -(-(skip + half) // lanes) * lanes
+        outs = [real_array(plan.devices, plan.rows, lead - skip + rounded)]
+        if not lead:
+            outs += [real_array(plan.gx, plan.tail, lanes), real_array(plan.radix, 1, lanes)]
+        return call(
+            lambda *refs: forward_kernel(plan, lead, *refs),
+            outs,
+            [line] + [vmem((rounded, size), bf16)] * 2,
+            [own],
+            *operands,
+        )
 
     def local(thickness, bed_uplift, flux_x, flux_y, mass_balance, ice_mask):
         own = lax.axis_index("gx").reshape(1)
         position = (lax.axis_index("gy") * plan.gx + lax.axis_index("gx")).reshape(1)
-        uplift, face_x, face_y = send_uplift(plan, own, bed_uplift, flux_x, flux_y)
-        lower_face = passed_along(face_x, "gx", 1)
-        left_face = passed_along(face_y, "gy", 1)
+        fields = (thickness, flux_x, flux_y, mass_balance, ice_mask)
+        uplift = send_uplift(plan, own, bed_uplift, flux_x, flux_y)
         lines_u = swap_gx(plan, uplift)
-        thickness_new, load = call(
-            lambda *refs: load_kernel(plan, *refs),
-            [thickness.shape, piece_shape],
-            [],
-            [own],
-            *(thickness, flux_x, flux_y, mass_balance, ice_mask, lower_face, left_face),
-        )
+        load = make_load(plan, own, fields)
         lines_v = swap_gx(plan, load)
         twiddle = plan.slot_twiddle()
-        forward = np.stack([table_halves(table) for table in plan.slot_matrix()])
-        (spectrum,) = call(
-            lambda *refs: forward_kernel(plan, *refs),
-            [(plan.devices, plan.rows, 2 * groups * cols)],
-            [vmem((plan.radix, cols, lanes), f32)] + [vmem((2 * groups * cols, size), bf16)] * 2,
-            [own],
-            *(lines_u + lines_v + [twiddle, forward]),
-        )
+        tables = np.stack([table_halves(table) for table in plan.slot_matrix()])
+        spectrum_u, tails_u, edge = forward(0, own, *(lines_u + [twiddle, tables]))
+        side = passed_along(edge, "gy", 1)
+        (spectrum,) = forward(half, own, *(lines_v + [tails_u, side, spectrum_u, twiddle, tables]))
+        thickness_new = make_thickness(plan, own, fields, (tails_u, side))
         received = exchange_all(spectrum)
-        source, line = plan.source_matrix(), plan.line_matrix()
+        source, across = plan.source_matrix(), plan.line_matrix()
         scale = np.float32(1.0 / plan.length_y)
-        tables = [table_halves(table) for table in (source, line, line.T * scale, source.T)]
+        tables = [table_halves(table) for table in (source, across, across.T * scale, source.T)]
         (middle,) = call(
             lambda *refs: middle_kernel(plan, *refs),
-            [(plan.devices, plan.rows, groups * cols)],
-            [vmem((2 * groups * cols, size), bf16)] * 2 + [vmem(((groups + 1) * cols, size), bf16)] * 2 + [vmem(((groups + 1) * cols, size), f32)],
+            [real_array(plan.devices, plan.rows, half)],
+            [vmem((2 * half, size), bf16)] * 2 + [vmem((half + cols, size), bf16)] * 2 + [vmem((half + cols, size), f32)],
             [position],
             *([received] + tables + [plan.line_twiddle()]),
         )
         back = exchange_all(middle)
         inverse = np.stack([table_halves(table) for table in plan.slot_inverse()])
-        (bed,) = call(
+        bed = call(
             lambda *refs: inverse_kernel(plan, *refs),
-            [piece_shape],
-            [vmem((groups * cols, size), f32)] * 2,
+            pieces,
+            [line] + [vmem((half, size), f32)] * 2,
             [own],
             *(back, twiddle, inverse),
         )
+        lines_b = swap_gx(plan, bed)
         (bed_new,) = call(
             lambda *refs: final_kernel(plan, *refs),
-            [thickness.shape],
+            [real_array(*thickness.shape)],
             [vmem((plan.here, plan.gx * cols, lanes), f32)],
             [own],
-            *swap_gx(plan, bed),
+            *lines_b,
         )
         return thickness_new, bed_new
 

time: 98 us -> 93.6 us (0.955)
  waiting for transfers between devices: 44.2 us -> 36.6 us
  Pallas kernels: 10.9 us -> 18 us
  starting transfers between devices: 19.1 us -> 16.4 us
  local copies, waits for them, and re-layouts: 1.3 us -> 0.06 us
    ppermute x9, waiting for transfers between devices: 15.1 us -> 7.57 us  [swap_gx(): lax.ppermute(pieces[step], 'gx', [(k, k ^ step) for k in range(plan.gx)])]
    pallas_call x1 -> x3, Pallas kernels: 2.36 us -> 9.41 us  [kernel_call(): return run(*scalars, *inputs, *faces)]
    ppermute x2 -> x1, starting transfers between devices: 6.63 us -> 3.42 us  [passed_along(): lax.ppermute(value, axis, [(source, source + steps) for source in range(l...]
    all_to_all x1, starting transfers between devices: 3.98 us -> 5.81 us  [exchange_all(): lax.all_to_all(value, ('gy', 'gx'), split_axis=0, concat_axis=0, tiled=True)]
    ppermute x9, starting transfers between devices: 8.55 us -> 7.2 us  [swap_gx(): lax.ppermute(pieces[step], 'gx', [(k, k ^ step) for k in range(plan.gx)])]
    squeeze x3 -> x0, local copies, waits for them, and re-layouts: 1.25 us -> none  [swap_gx(): pieces[step]]
  transfers between devices with their start and end apart: 12 -> 11, of which waited for: 5 -> 5; matrix products, arithmetic and copies ran while one was open for 1% -> 0% of each run, Pallas kernels for 1% -> 9%
where the time goes in v2:
time: 93.6 us; the launch traced here: 93.2 us
  waiting for transfers between devices  36.6 us (39%)
  blocking collectives  21.4 us (23%)
  Pallas kernels  18 us (19%)
  starting transfers between devices  16.4 us (18%)
    all_to_all x1, waiting for transfers between devices, exchange_all(): lax.all_to_all(value, ('gy', 'gx'), split_axis=0, concat_axis=0, tiled=True)  29 us
    all_to_all x1, blocking collectives, exchange_all(): lax.all_to_all(value, ('gy', 'gx'), split_axis=0, concat_axis=0, tiled=True)  21.4 us
    pallas_call x3, Pallas kernels, kernel_call(): return run(*scalars, *inputs, *faces)  9.41 us
    pallas_call x5, Pallas kernels, call(): return run(*scalars, *operands)  8.54 us
    ppermute x9, waiting for transfers between devices, swap_gx(): lax.ppermute(pieces[step], 'gx', [(k, k ^ step) for k in range(plan.gx)])  7.57 us
    ppermute x9, starting transfers between devices, swap_gx(): lax.ppermute(pieces[step], 'gx', [(k, k ^ step) for k in range(plan.gx)])  7.2 us
    all_to_all x1, starting transfers between devices, exchange_all(): lax.all_to_all(value, ('gy', 'gx'), split_axis=0, concat_axis=0, tiled=True)  5.81 us
    ppermute x1, starting transfers between devices, passed_along(): lax.ppermute(value, axis, [(source, source + steps) for source in range(l...  3.42 us
  transfers between devices with their start and end apart: 11, of which 5 were waited for; matrix products, arithmetic and copies ran while one was open for 0% of the time, Pallas kernels for 9%

profile of v2, /device:TPU:0, one launch (start us, length us, event | category | flops | bytes accessed | tf_op | source)
XLA Modules:
  0.0 93.2 jit_solution(3758265630867461698)
XLA Ops:
  0.6 2.5 %shard_map.149 = (f32[296,128]{1,0:T(8,128)}, f32[296,128]{1,0:T(8,128)}, f32[296,128]{1,0:T(8,128)}, f32[296,128]{1,0:T(8,128)}) custom-call(s32[1]{0:T(128)} %bitcast.refs_0_, f32[384,384]{1,0:T(8,128)} %refs_1_.3, f32[384,384]{1,0:T(8,128)} %refs_2_.7, f32[384,384]{1,0:T(8,128)} %refs_3_.7), custom_call_target="tpu_custom_call" | custom-call | tf_op jit(solution)/shard_map/pallas_call | solution.py:344
  3.1 0.6 collective-permute-start
  3.7 2.6 %collective-permute-start.1 = (f32[296,128]{1,0:T(8,128)}, f32[296,128]{1,0:T(8,128)S(1)}, u32[]{:S(2)}, u32[]{:S(2)}) collective-permute-start(f32[296,128]{1,0:T(8,128)} %get-tuple-element.19), channel_id=1, source_target_pairs={{0,16},{8,24},{16,0},{24,8},{1,17},{9,25},{17,1},{25,9},{2,18},{10... | collective-permute-start | bytes 454664 | tf_op jit(solution)/shard_map/ppermute | solution.py:724
  6.2 0.1 collective-permute-start.2
  6.4 3.2 %shard_map.152 = (f32[296,128]{1,0:T(8,128)}, f32[296,128]{1,0:T(8,128)}, f32[296,128]{1,0:T(8,128)}, f32[296,128]{1,0:T(8,128)}) custom-call(s32[1]{0:T(128)} %bitcast.refs_0_, f32[384,384]{1,0:T(8,128)} %refs_1_.5, f32[384,384]{1,0:T(8,128)} %refs_2_.7, f32[384,384]{1,0:T(8,128)} %refs_3_.7, f32[384,384]{1,0:T(8,128)} %refs_4_.4, s32[384,384]{1,0:T(8,128)} %refs_5_.5), custom_call_target="tpu_custom_call" | custom-call | tf_op jit(solution)/shard_map/pallas_call | solution.py:344
  9.6 0.0 copy-start.6
  9.6 0.2 collective-permute-start.4
  9.8 1.9 %collective-permute-start.5 = (f32[296,128]{1,0:T(8,128)}, f32[296,128]{1,0:T(8,128)S(1)}, u32[]{:S(2)}, u32[]{:S(2)}) collective-permute-start(f32[296,128]{1,0:T(8,128)} %get-tuple-element.25), channel_id=1, source_target_pairs={{0,16},{8,24},{16,0},{24,8},{1,17},{9,25},{17,1},{25,9},{2,18},{10... | collective-permute-start | bytes 454664 | tf_op jit(solution)/shard_map/ppermute | solution.py:724
  11.6 0.0 collective-permute-done.refs_2_
  11.6 0.0 collective-permute-start.6
  11.7 0.0 collective-permute-done.1.refs_3_
  11.7 2.5 %collective-permute-done.2.refs_4_ = f32[296,128]{1,0:T(8,128)S(1)} collective-permute-done((f32[296,128]{1,0:T(8,128)}, f32[296,128]{1,0:T(8,128)S(1)}, u32[]{:S(2)}, u32[]{:S(2)}) %collective-permute-start.2) | collective-permute-done | bytes 151584 | tf_op jit(solution)/shard_map/ppermute | solution.py:724
  14.1 0.0 copy-done
  14.1 0.0 copy-done.7
  14.1 0.0 copy-done.9
  14.1 1.1 %shard_map.150 = (f32[32,8,640]{2,1,0:T(8,128)S(1)}, f32[4,8,128]{2,1,0:T(8,128)S(1)}, f32[12,1,128]{2,1,0:T(1,128)S(1)}) custom-call(s32[1]{0:T(128)} %bitcast.refs_0_, f32[296,128]{1,0:T(8,128)S(1)} %copy-done.7, f32[296,128]{1,0:T(8,128)S(1)} %collective-permute-done.refs_2_, f32[296,128]{1,0:T(8,128)S(1)} %collective-permute-done.1.refs_3_, ...), custom_call_target="tpu_custom_call" | custom-call | tf_op jit(solution)/shard_map/pallas_call | solution.py:307
  15.2 0.0 copy-start.10
  15.2 3.4 %collective-permute-start.3 = (f32[12,1,128]{2,1,0:T(1,128)S(1)}, f32[12,1,128]{2,1,0:T(1,128)S(1)}, u32[]{:S(2)}, u32[]{:S(2)}) collective-permute-start(f32[12,1,128]{2,1,0:T(1,128)S(1)} %get-tuple-element.22), channel_id=1, source_target_pairs={{0,1},{1,2},{2,3},{3,4},{4,5},{5,6},{6,7},{8,9},{9,10},{10,11},{11... | collective-permute-start | bytes 18440 | tf_op jit(solution)/shard_map/ppermute | solution.py:178
  18.7 0.0 collective-permute-done.4.refs_2_
  18.7 0.0 collective-permute-done.5.refs_3_
  18.7 1.8 %collective-permute-done.6.refs_4_ = f32[296,128]{1,0:T(8,128)S(1)} collective-permute-done((f32[296,128]{1,0:T(8,128)}, f32[296,128]{1,0:T(8,128)S(1)}, u32[]{:S(2)}, u32[]{:S(2)}) %collective-permute-start.6) | collective-permute-done | bytes 151584 | tf_op jit(solution)/shard_map/ppermute | solution.py:724
  20.5 0.0 collective-permute-done.3.refs_7_.refs_6_
  20.5 0.0 copy-done.6
  20.5 3.0 %shard_map.153 = f32[32,8,1152]{2,1,0:T(8,128)} custom-call(s32[1]{0:T(128)} %bitcast.refs_0_, f32[296,128]{1,0:T(8,128)S(1)} %copy-done.6, f32[296,128]{1,0:T(8,128)S(1)} %collective-permute-done.4.refs_2_, f32[296,128]{1,0:T(8,128)S(1)} %collective-permute-done.5.refs_3_, f32[296,128]{1,0:T(8,128)S(1)} %collective-permute-done.6.refs_4_, ...), custom_call_target="tpu_custom_call" | custom-call | tf_op jit(solution)/shard_map/pallas_call | solution.py:307
  23.4 0.0 copy-done.10
  23.4 0.0 copy-done.11
  23.4 0.0 copy-start.4
  23.5 0.0 copy-start.5
  23.5 0.0 copy-start.8
  23.5 5.8 %all-to-all-start = ((f32[32,8,1152]{2,1,0:T(8,128)}), f32[32,8,1152]{2,1,0:T(8,128)S(1)}, u32[]{:S(2)}, u32[]{:S(2)}) async-start(f32[32,8,1152]{2,1,0:T(8,128)} %shard_map.153), calls=%async_computation | async-start | bytes 2359296 | tf_op jit(solution)/shard_map/all_to_all | solution.py:172
  29.3 29.0 %all-to-all-done.refs_1_ = f32[32,8,1152]{2,1,0:T(8,128)S(1)} async-done(((f32[32,8,1152]{2,1,0:T(8,128)}), f32[32,8,1152]{2,1,0:T(8,128)S(1)}, u32[]{:S(2)}, u32[]{:S(2)}) %all-to-all-start) | async-done | bytes 1179680 | tf_op jit(solution)/shard_map/all_to_all | solution.py:172
  58.3 0.0 copy-done.2
  58.3 0.0 copy-done.3
  58.3 0.0 copy-done.4
  58.3 0.0 copy-done.5
  58.3 0.0 copy-done.8
  58.3 2.6 %shard_map.154 = f32[32,8,576]{2,1,0:T(8,128)S(1)} custom-call(s32[1]{0:T(128)} %bitcast.1.refs_0_, f32[32,8,1152]{2,1,0:T(8,128)S(1)} %all-to-all-done.refs_1_, bf16[2,256,256]{2,1,0:T(8,128)(2,1)S(1)} %copy-done.2, bf16[2,192,192]{2,1,0:T(8,128)(2,1)S(1)} %copy-done.4, bf16[2,192,192]{2,1,0:T(8,128)(2,1)S(1)} %copy-done.5, ...), custom_call_target="tpu_custom_call" | custom-call | tf_op jit(solution)/shard_map/pallas_call | solution.py:307
  61.0 0.0 copy-start.1
  61.0 21.4 %all_to_all.10.refs_1_ = f32[32,8,576]{2,1,0:T(8,128)S(1)} all-to-all(f32[32,8,576]{2,1,0:T(8,128)S(1)} %shard_map.154), channel_id=1, replica_groups=mesh['gx'=4,'gy'=8] {'gy','gx'}, dimensions={0} | all-to-all | bytes 1179648 | tf_op jit(solution)/shard_map/all_to_all | solution.py:172
  82.4 0.8 shard_map.155
  83.2 0.1 collective-permute-start.7
  83.4 1.5 %collective-permute-start.8 = (f32[3,96,128]{2,1,0:T(8,128)S(1)}, f32[3,96,128]{2,1,0:T(8,128)S(1)}, u32[]{:S(2)}, u32[]{:S(2)}) collective-permute-start(f32[3,96,128]{2,1,0:T(8,128)S(1)} %get-tuple-element.30), channel_id=1, source_target_pairs={{0,16},{8,24},{16,0},{24,8},{1,17},{9,25},{17,1},{25,9},{2,18},{10... | collective-permute-start | bytes 442376 | tf_op jit(solution)/shard_map/ppermute | solution.py:724
  84.9 0.3 collective-permute-start.9
  85.1 3.7 %shard_map.151 = f32[384,384]{1,0:T(8,128)} custom-call(s32[1]{0:T(128)} %bitcast.refs_0_, f32[384,384]{1,0:T(8,128)} %refs_1_.5, f32[384,384]{1,0:T(8,128)} %refs_2_.7, f32[384,384]{1,0:T(8,128)} %refs_3_.7, f32[384,384]{1,0:T(8,128)} %refs_4_.4, s32[384,384]{1,0:T(8,128)} %refs_5_.5, f32[4,8,128]{2,1,0:T(8,128)} %copy-done.10, f32[12,1,128]{2,1,0:T(1,128)} %copy-done.11), custom_call_target="tpu_custom_call" | custom-call | tf_op jit(solution)/shard_map/pallas_call | solution.py:344
  88.8 0.0 collective-permute-done.7.refs_2_
  88.9 1.2 %collective-permute-done.8.refs_3_ = f32[3,96,128]{2,1,0:T(8,128)S(1)} collective-permute-done((f32[3,96,128]{2,1,0:T(8,128)S(1)}, f32[3,96,128]{2,1,0:T(8,128)S(1)}, u32[]{:S(2)}, u32[]{:S(2)}) %collective-permute-start.8) | collective-permute-done | bytes 147488 | tf_op jit(solution)/shard_map/ppermute | solution.py:724
  90.1 2.1 %collective-permute-done.9.refs_4_ = f32[3,96,128]{2,1,0:T(8,128)S(1)} collective-permute-done((f32[3,96,128]{2,1,0:T(8,128)S(1)}, f32[3,96,128]{2,1,0:T(8,128)S(1)}, u32[]{:S(2)}, u32[]{:S(2)}) %collective-permute-start.9) | collective-permute-done | bytes 147488 | tf_op jit(solution)/shard_map/ppermute | solution.py:724
  92.2 1.1 %shard_map.156 = f32[384,384]{1,0:T(8,128)} custom-call(s32[1]{0:T(128)} %bitcast.refs_0_, f32[3,96,128]{2,1,0:T(8,128)S(1)} %get-tuple-element.28.refs_1_, f32[3,96,128]{2,1,0:T(8,128)S(1)} %collective-permute-done.7.refs_2_, f32[3,96,128]{2,1,0:T(8,128)S(1)} %collective-permute-done.8.refs_3_, f32[3,96,128]{2,1,0:T(8,128)S(1)} %collective-permute-done.9.refs_4_), custom_call_target="tpu_custom_call" | custom-call | tf_op jit(solution)/shard_map/pallas_call | solution.py:307
  (7 shorter events, 0.0 us)
Async XLA Ops:
  3.1 8.5 %collective-permute-start = (f32[296,128]{1,0:T(8,128)}, f32[296,128]{1,0:T(8,128)S(1)}, u32[]{:S(2)}, u32[]{:S(2)}) collective-permute-start(f32[296,128]{1,0:T(8,128)} %get-tuple-element.18), channel_id=1, source_target_pairs={{0,8},{8,0},{16,24},{24,16},{1,9},{9,1},{17,25},{25,17},{2,10},{10... | collective-permute-start | bytes 454664 | tf_op jit(solution)/shard_map/ppermute | solution.py:724
  3.7 8.0 %collective-permute-start.1 = (f32[296,128]{1,0:T(8,128)}, f32[296,128]{1,0:T(8,128)S(1)}, u32[]{:S(2)}, u32[]{:S(2)}) collective-permute-start(f32[296,128]{1,0:T(8,128)} %get-tuple-element.19), channel_id=1, source_target_pairs={{0,16},{8,24},{16,0},{24,8},{1,17},{9,25},{17,1},{25,9},{2,18},{10... | collective-permute-start | bytes 454664 | tf_op jit(solution)/shard_map/ppermute | solution.py:724
  6.2 7.9 %copy-start = (bf16[2,2,256,256]{3,2,1,0:T(8,128)(2,1)S(1)}, bf16[2,2,256,256]{3,2,1,0:T(8,128)(2,1)}, u32[]{:S(2)}) copy-start(bf16[2,2,256,256]{3,2,1,0:T(8,128)(2,1)} %constant.27.clone.refs_6_.refs_9_) | copy-start | bytes 1572868
  6.2 7.9 %copy-start.7 = (f32[296,128]{1,0:T(8,128)S(1)}, f32[296,128]{1,0:T(8,128)}, u32[]{:S(2)}) copy-start(f32[296,128]{1,0:T(8,128)} %get-tuple-element.17.refs_1_) | copy-start | bytes 454660
  6.2 7.9 %copy-start.9 = (f32[2,6,128]{2,1,0:T(8,128)S(1)}, f32[2,6,128]{2,1,0:T(8,128)}, u32[]{:S(2)}) copy-start(f32[2,6,128]{2,1,0:T(8,128)} %constant.26.clone.refs_5_.refs_8_.refs_2_) | copy-start | bytes 18436
  6.2 7.9 %collective-permute-start.2 = (f32[296,128]{1,0:T(8,128)}, f32[296,128]{1,0:T(8,128)S(1)}, u32[]{:S(2)}, u32[]{:S(2)}) collective-permute-start(f32[296,128]{1,0:T(8,128)} %get-tuple-element.20), channel_id=1, source_target_pairs={{0,24},{8,16},{16,8},{24,0},{1,25},{9,17},{17,9},{25,1},{2,26},{10... | collective-permute-start | bytes 454664 | tf_op jit(solution)/shard_map/ppermute | solution.py:724
  9.6 10.9 %copy-start.6 = (f32[296,128]{1,0:T(8,128)S(1)}, f32[296,128]{1,0:T(8,128)}, u32[]{:S(2)}) copy-start(f32[296,128]{1,0:T(8,128)} %get-tuple-element.23.refs_1_) | copy-start | bytes 454660
  9.6 9.1 %collective-permute-start.4 = (f32[296,128]{1,0:T(8,128)}, f32[296,128]{1,0:T(8,128)S(1)}, u32[]{:S(2)}, u32[]{:S(2)}) collective-permute-start(f32[296,128]{1,0:T(8,128)} %get-tuple-element.24), channel_id=1, source_target_pairs={{0,8},{8,0},{16,24},{24,16},{1,9},{9,1},{17,25},{25,17},{2,10},{10... | collective-permute-start | bytes 454664 | tf_op jit(solution)/shard_map/ppermute | solution.py:724
  9.8 8.9 %collective-permute-start.5 = (f32[296,128]{1,0:T(8,128)}, f32[296,128]{1,0:T(8,128)S(1)}, u32[]{:S(2)}, u32[]{:S(2)}) collective-permute-start(f32[296,128]{1,0:T(8,128)} %get-tuple-element.25), channel_id=1, source_target_pairs={{0,16},{8,24},{16,0},{24,8},{1,17},{9,25},{17,1},{25,9},{2,18},{10... | collective-permute-start | bytes 454664 | tf_op jit(solution)/shard_map/ppermute | solution.py:724
  11.6 8.8 %collective-permute-start.6 = (f32[296,128]{1,0:T(8,128)}, f32[296,128]{1,0:T(8,128)S(1)}, u32[]{:S(2)}, u32[]{:S(2)}) collective-permute-start(f32[296,128]{1,0:T(8,128)} %get-tuple-element.26), channel_id=1, source_target_pairs={{0,24},{8,16},{16,8},{24,0},{1,25},{9,17},{17,9},{25,1},{2,26},{10... | collective-permute-start | bytes 454664 | tf_op jit(solution)/shard_map/ppermute | solution.py:724
  15.2 8.2 %copy-start.10 = (f32[4,8,128]{2,1,0:T(8,128)}, f32[4,8,128]{2,1,0:T(8,128)S(1)}, u32[]{:S(2)}) copy-start(f32[4,8,128]{2,1,0:T(8,128)S(1)} %get-tuple-element.21.refs_6_.refs_5_) | copy-start | bytes 49156
  15.2 5.2 %collective-permute-start.3 = (f32[12,1,128]{2,1,0:T(1,128)S(1)}, f32[12,1,128]{2,1,0:T(1,128)S(1)}, u32[]{:S(2)}, u32[]{:S(2)}) collective-permute-start(f32[12,1,128]{2,1,0:T(1,128)S(1)} %get-tuple-element.22), channel_id=1, source_target_pairs={{0,1},{1,2},{2,3},{3,4},{4,5},{5,6},{6,7},{8,9},{9,10},{10,11},{11... | collective-permute-start | bytes 18440 | tf_op jit(solution)/shard_map/ppermute | solution.py:178
  20.5 3.0 %copy-start.11 = (f32[12,1,128]{2,1,0:T(1,128)}, f32[12,1,128]{2,1,0:T(1,128)S(1)}, u32[]{:S(2)}) copy-start(f32[12,1,128]{2,1,0:T(1,128)S(1)} %collective-permute-done.3.refs_7_.refs_6_) | copy-start | bytes 18436
  23.4 34.9 %copy-start.2 = (bf16[2,256,256]{2,1,0:T(8,128)(2,1)S(1)}, bf16[2,256,256]{2,1,0:T(8,128)(2,1)}, u32[]{:S(2)}) copy-start(bf16[2,256,256]{2,1,0:T(8,128)(2,1)} %constant.28.clone.refs_2_) | copy-start | bytes 786436
  23.4 34.9 %copy-start.3 = (bf16[2,256,256]{2,1,0:T(8,128)(2,1)S(1)}, bf16[2,256,256]{2,1,0:T(8,128)(2,1)}, u32[]{:S(2)}) copy-start(bf16[2,256,256]{2,1,0:T(8,128)(2,1)} %constant.31.clone.refs_5_) | copy-start | bytes 786436
  23.4 34.9 %copy-start.4 = (bf16[2,192,192]{2,1,0:T(8,128)(2,1)S(1)}, bf16[2,192,192]{2,1,0:T(8,128)(2,1)}, u32[]{:S(2)}) copy-start(bf16[2,192,192]{2,1,0:T(8,128)(2,1)} %constant.29.clone.refs_3_) | copy-start | bytes 442372
  23.5 34.9 %copy-start.5 = (bf16[2,192,192]{2,1,0:T(8,128)(2,1)S(1)}, bf16[2,192,192]{2,1,0:T(8,128)(2,1)}, u32[]{:S(2)}) copy-start(bf16[2,192,192]{2,1,0:T(8,128)(2,1)} %constant.30.clone.refs_4_) | copy-start | bytes 442372
  23.5 34.9 %copy-start.8 = (f32[2,96,128]{2,1,0:T(8,128)S(1)}, f32[2,96,128]{2,1,0:T(8,128)}, u32[]{:S(2)}) copy-start(f32[2,96,128]{2,1,0:T(8,128)} %constant.32.clone.refs_6_) | copy-start | bytes 294916
  23.5 34.8 %all-to-all-start = ((f32[32,8,1152]{2,1,0:T(8,128)}), f32[32,8,1152]{2,1,0:T(8,128)S(1)}, u32[]{:S(2)}, u32[]{:S(2)}) async-start(f32[32,8,1152]{2,1,0:T(8,128)} %shard_map.153), calls=%async_computation | async-start | bytes 2359296 | tf_op jit(solution)/shard_map/all_to_all | solution.py:172
  61.0 21.4 %copy-start.1 = (bf16[2,2,256,256]{3,2,1,0:T(8,128)(2,1)S(1)}, bf16[2,2,256,256]{3,2,1,0:T(8,128)(2,1)}, u32[]{:S(2)}) copy-start(bf16[2,2,256,256]{3,2,1,0:T(8,128)(2,1)} %constant.33.clone.refs_3_) | copy-start | bytes 1572868
  83.2 5.6 %collective-permute-start.7 = (f32[3,96,128]{2,1,0:T(8,128)S(1)}, f32[3,96,128]{2,1,0:T(8,128)S(1)}, u32[]{:S(2)}, u32[]{:S(2)}) collective-permute-start(f32[3,96,128]{2,1,0:T(8,128)S(1)} %get-tuple-element.29), channel_id=1, source_target_pairs={{0,8},{8,0},{16,24},{24,16},{1,9},{9,1},{17,25},{25,17},{2,10},{10... | collective-permute-start | bytes 442376 | tf_op jit(solution)/shard_map/ppermute | solution.py:724
  83.4 6.7 %collective-permute-start.8 = (f32[3,96,128]{2,1,0:T(8,128)S(1)}, f32[3,96,128]{2,1,0:T(8,128)S(1)}, u32[]{:S(2)}, u32[]{:S(2)}) collective-permute-start(f32[3,96,128]{2,1,0:T(8,128)S(1)} %get-tuple-element.30), channel_id=1, source_target_pairs={{0,16},{8,24},{16,0},{24,8},{1,17},{9,25},{17,1},{25,9},{2,18},{10... | collective-permute-start | bytes 442376 | tf_op jit(solution)/shard_map/ppermute | solution.py:724
  84.9 7.3 %collective-permute-start.9 = (f32[3,96,128]{2,1,0:T(8,128)S(1)}, f32[3,96,128]{2,1,0:T(8,128)S(1)}, u32[]{:S(2)}, u32[]{:S(2)}) collective-permute-start(f32[3,96,128]{2,1,0:T(8,128)S(1)} %get-tuple-element.31), channel_id=1, source_target_pairs={{0,24},{8,16},{16,8},{24,0},{1,25},{9,17},{17,9},{25,1},{2,26},{10... | collective-permute-start | bytes 442376 | tf_op jit(solution)/shard_map/ppermute | solution.py:724

commit v3 on v2

--- a/solution.py
+++ b/solution.py
@@ -347,47 +347,61 @@
 def uplift_kernel(plan, own_ref, uplift_hbm, flux_x_hbm, flux_y_hbm, *refs):
     own = own_ref[0]
     out_refs = refs[: plan.gx]
-    field_ref, turned_ref, last_x_ref, last_y_ref, sems = refs[plan.gx :]
+    field_ref, turned_ref, tail_ref, last_x_ref, last_y_ref, sems, out_sems = refs[plan.gx :]
     rows, cols = uplift_hbm.shape
     copies = [
         pltpu.make_async_copy(flux_x_hbm.at[pl.ds(rows - 8, 8), :], last_x_ref, sems.at[0]),
         pltpu.make_async_copy(flux_y_hbm.at[:, pl.ds(cols - lanes, lanes)], last_y_ref, sems.at[1]),
     ]
+    half = lanes // 2
+    for part in range(2 * plan.here):
+        source = uplift_hbm.at[pl.ds(part * half, half), :]
+        copies.append(pltpu.make_async_copy(source, field_ref.at[pl.ds(part * half, half), :], sems.at[2 + part]))
+    for copy in copies[2:] + copies[:2]:
+        copy.start()
+    sent = []
     for here in range(plan.here):
-        source = uplift_hbm.at[pl.ds(here * lanes, lanes), :]
-        copies.append(pltpu.make_async_copy(source, field_ref.at[here], sems.at[2 + here]))
-    for copy in copies:
-        copy.start()
-    for here in range(plan.here):
-        copies[2 + here].wait()
-        lines_out(plan, own, field_ref[here], here, turned_ref, out_refs)
+        copies[2 + 2 * here].wait()
+        copies[3 + 2 * here].wait()
+        turned_ref[here] = field_ref[here * lanes : (here + 1) * lanes, :].T
+        for step in range(plan.gx):
+            source = turned_ref.at[here, pl.ds(pl.multiple_of((own ^ step) * plan.cols, 8), plan.cols), :]
+            target = out_refs[step].at[pl.ds(here * plan.cols, plan.cols), :]
+            sent.append(pltpu.make_async_copy(source, target, out_sems.at[here, step]))
+            sent[-1].start()
     copies[0].wait()
+    copies[1].wait()
     last_x = last_x_ref[7:8, :]
-    copies[1].wait()
     last_y = last_y_ref[...].T[lanes - 1 : lanes, :]
-    tail = plan.here * plan.cols
     parts = [last[:, a * lanes : (a + 1) * lanes] for last in (last_x, last_y) for a in range(plan.here)]
     parts.append(jnp.zeros((plan.tail - 2 * plan.here, lanes), jnp.float32))
-    parts = jnp.concatenate(parts, 0)
+    tail_ref[...] = jnp.concatenate(parts, 0)
     for step in range(plan.gx):
-        out_refs[step][tail : tail + plan.tail, :] = parts
+        target = out_refs[step].at[pl.ds(plan.here * plan.cols, plan.tail), :]
+        sent.append(pltpu.make_async_copy(tail_ref, target, out_sems.at[plan.here, step]))
+        sent[-1].start()
+    for copy in sent:
+        copy.wait()
 
 
 def send_uplift(plan, own, bed_uplift, flux_x, flux_y):
     rows, cols = bed_uplift.shape
-    return kernel_call(
+    run = pl.pallas_call(
         lambda *refs: uplift_kernel(plan, *refs),
-        [real_array(plan.piece_rows, lanes)] * plan.gx,
-        [
-            pltpu.VMEM((plan.here, lanes, cols), jnp.float32),
+        out_shape=[real_array(plan.piece_rows, lanes)] * plan.gx,
+        in_specs=[pl.BlockSpec(memory_space=pltpu.SMEM)] + [pl.BlockSpec(memory_space=pl.ANY)] * 3,
+        out_specs=[pl.BlockSpec(memory_space=pl.ANY)] * plan.gx,
+        scratch_shapes=[
+            pltpu.VMEM((rows, cols), jnp.float32),
             pltpu.VMEM((plan.here, cols, lanes), jnp.float32),
+            pltpu.VMEM((plan.tail, lanes), jnp.float32),
             pltpu.VMEM((8, cols), jnp.float32),
             pltpu.VMEM((rows, lanes), jnp.float32),
-            pltpu.SemaphoreType.DMA((2 + plan.here,)),
+            pltpu.SemaphoreType.DMA((2 + 2 * plan.here,)),
+            pltpu.SemaphoreType.DMA((plan.here + 1, plan.gx)),
         ],
-        [own],
-        (bed_uplift, flux_x, flux_y),
     )
+    return run(own, bed_uplift, flux_x, flux_y)
 
 
 def fetch_fields(plan, sources, mask_ref, floats_ref, sems):
@@ -485,7 +499,7 @@
         for copy in copies[here]:
             copy.wait()
         rows = slice(here * lanes, (here + 1) * lanes)
-        side = jnp.broadcast_to(side_ref[own * plan.here + here], (lanes, lanes)).T
+        side = jnp.broadcast_to(side_ref[0, plan.here + here : plan.here + here + 1, :], (lanes, lanes)).T
         side = jnp.concatenate([side] * (out_ref.shape[1] // lanes), 1)
         trial = trial_block(floats_ref, here, above, side)
         out_ref[rows, :] = jnp.where(mask_ref[rows, :] == 2, 0.0, jnp.maximum(trial, 0.0))
@@ -499,23 +513,34 @@
 
 def finish_load(plan, own, line_ref, uplift_tails, load_tails, side_ref):
     cols, here = plan.cols, plan.here
-    row = lax.broadcasted_iota(jnp.int32, (8, lanes), 0)
-    lane = lax.broadcasted_iota(jnp.int32, (8, lanes), 1)
+    lane = lax.broadcasted_iota(jnp.int32, (1, lanes), 1)
     wide_lane = lax.broadcasted_iota(jnp.int32, (cols, lanes), 1)
+    above, new = [], []
     for step in range(plan.gx):
-        block = own ^ step
-        above = own_part(plan, own, row_above(plan, own, block, uplift_tails))
+        above.append(own_part(plan, own, row_above(plan, own, own ^ step, uplift_tails)))
         tail = load_tails[step]
-        new = jnp.maximum(tail[0:1, :] + time_step * above, 0.0) - tail[1:2, :]
-        turned = jnp.broadcast_to(new, (lanes, lanes)).T[:cols]
-        line_ref[block * here] = jnp.where(wide_lane == 0, turned, line_ref[block * here])
-
-        @pl.when(own == 0)
-        def _(block=block, tail=tail, above=above):
+        new.append(jnp.maximum(tail[0:1, :] + time_step * above[step], 0.0) - tail[1:2, :])
+    turned = jnp.concatenate(new + [jnp.zeros((lanes - plan.gx, lanes), jnp.float32)], 0).T[:cols]
+    for step in range(plan.gx):
+        place = (own ^ step) * here
+        first = pltpu.roll(turned, lanes - step, 1) if step else turned
+        line_ref[place] = jnp.where(wide_lane == 0, first, line_ref[place])
+
+    @pl.when(own == 0)
+    def _():
+        for step in range(plan.gx):
+            tail = load_tails[step]
             for a in range(here):
-                corner = jnp.where(lane[:1] == 0, jnp.broadcast_to(above[:, :1], (1, lanes)), 0.0) if a == 0 else 0.0
-                trial = tail[2 + a : 3 + a, :] + time_step * (side_ref[block * here + a] + corner)
-                line_ref[block * here + a, 0:1, :] = jnp.maximum(trial, 0.0) - tail[2 + here + a : 3 + here + a, :]
+                corner = jnp.where(lane == 0, jnp.broadcast_to(above[step][:, :1], (1, lanes)), 0.0) if a == 0 else 0.0
+                trial = tail[2 + a : 3 + a, :] + time_step * (side_ref[step, here + a : here + a + 1, :] + corner)
+                line_ref[step * here + a, 0:1, :] = jnp.maximum(trial, 0.0) - tail[2 + here + a : 3 + here + a, :]
+
+
+def tails_kernel(plan, *refs):
+    pieces, tails_ref = refs[: plan.gx], refs[plan.gx]
+    start = plan.here * plan.cols
+    for step in range(plan.gx):
+        tails_ref[step] = pieces[step][start : start + plan.tail, :]
 
 
 def forward_kernel(plan, lead, own_ref, *refs):
@@ -524,21 +549,18 @@
     own = own_ref[0]
     tail = slice(here * cols, here * cols + plan.tail)
     if lead:
-        uplift_tails, side_ref, other_ref, *refs = refs
-        twiddle_ref, table_ref, out_ref, line_ref, high_ref, low_ref = refs
+        uplift_tails, side_ref, edge_ref, head_ref, _, twiddle_ref, table_ref, *refs = refs
+        out_hbm, line_ref, high_ref, low_ref, block_ref, sems = refs
     else:
-        twiddle_ref, table_ref, out_ref, tails_ref, edge_ref, line_ref, high_ref, low_ref = refs
-        for step in range(plan.gx):
-            tails_ref[step] = pieces[step][tail, :]
-            for a in range(here):
-                edge_ref[(own ^ step) * here + a] = pieces[step][here * (cols + 1) + a : here * (cols + 1) + a + 1, :]
+        twiddle_ref, table_ref, out_hbm, edge_ref, head_ref, line_ref, high_ref, low_ref, block_ref, sems = refs
     step_rows = 16
     total = groups * cols
     for step in range(plan.gx):
         for a in range(here):
             line_ref[(own ^ step) * here + a] = pieces[step][a * cols : (a + 1) * cols, :]
     if lead:
-        finish_load(plan, own, line_ref, [uplift_tails[k] for k in range(plan.gx)], [piece[tail, :] for piece in pieces], side_ref)
+        tails = [uplift_tails[step] for step in range(plan.gx)]
+        finish_load(plan, own, line_ref, tails, [piece[tail, :] for piece in pieces], side_ref)
     skip = lead % lanes
 
     def chunk(index, carry):
@@ -564,10 +586,18 @@
             low_ref[edge[0] : edge[1], :] = jnp.zeros((edge[1] - edge[0], 2 * lanes), jnp.bfloat16)
     general = (table_ref[0, 0], table_ref[0, 1])
     special = (table_ref[1, 0], table_ref[1, 1])
-    before = lead - skip
-    for start in range(0, before, lanes):
-        out_ref[:, :, start : start + lanes] = other_ref[:, :, start : start + lanes]
-    for start in range(0, high_ref.shape[0], lanes):
+    before = (lead - skip) // lanes
+    blocks = high_ref.shape[0] // lanes
+    sent = []
+
+    def send(block):
+        lane = pl.ds((before + block) * lanes, lanes)
+        sent.append(pltpu.make_async_copy(block_ref.at[block], out_hbm.at[:, :, lane], sems.at[block]))
+        sent[-1].start()
+
+    held = -(-(skip + cols) // lanes) if lead else 0
+    for block in range(blocks):
+        start = block * lanes
         rows = slice(start, start + lanes)
         data = (high_ref[rows, :], low_ref[rows, :])
         end = skip + cols
@@ -579,23 +609,73 @@
             if start < end:
                 out = jnp.where(lane < end - start, product(special, data, True), out)
         out = out.reshape(plan.devices, plan.rows, lanes)
-        at = before + start
         if start < skip:
             lane = lax.broadcasted_iota(jnp.int32, out.shape, 2)
-            out = jnp.where(lane < skip - start, other_ref[:, :, at : at + lanes], out)
-        out_ref[:, :, at : at + lanes] = out
-    if lead:
-        one, two = out_ref[0, :, :lanes], out_ref[0, :, before : before + 2 * lanes]
-        row = lax.broadcasted_iota(jnp.int32, two.shape, 0)
-        lane = lax.broadcasted_iota(jnp.int32, two.shape, 1)
-        wide = pltpu.roll(jnp.concatenate([one, one], 1), plan.deep, 0)
-        to_right = pltpu.roll(wide, skip, 1) if skip else wide
-        swapped = pltpu.roll(two, plan.deep, 0)
-        to_left = pltpu.roll(swapped, 2 * lanes - skip, 1) if skip else swapped
-        take = (row == plan.deep) & (lane < cols)
-        out_ref[0, :, :lanes] = jnp.where(take, to_left, jnp.concatenate([one, one], 1))[:, :lanes]
-        take = (row == 0) & (lane >= skip) & (lane < skip + cols)
-        out_ref[0, :, before : before + 2 * lanes] = jnp.where(take, to_right, two)
+            out = jnp.where(lane < skip - start, edge_ref[...], out)
+        if not lead and (block + 1) * lanes > total:
+            edge_ref[...] = out
+            continue
+        block_ref[block] = out
+        if not lead and block == 0:
+            head_ref[...] = out[0]
+        if block + 1 == held:
+            two = jnp.concatenate([block_ref[k, 0] for k in range(held)], 1)
+            width = held * lanes
+            row = lax.broadcasted_iota(jnp.int32, two.shape, 0)
+            lane = lax.broadcasted_iota(jnp.int32, two.shape, 1)
+            head = head_ref[...]
+            wide = pltpu.roll(jnp.concatenate([head] * held, 1), plan.deep, 0)
+            to_right = pltpu.roll(wide, skip, 1) if skip else wide
+            swapped = pltpu.roll(two, plan.deep, 0)
+            to_left = pltpu.roll(swapped, width - skip, 1) if skip else swapped
+            take = (row[:, :lanes] == plan.deep) & (lane[:, :lanes] < cols)
+            head_out = block_ref.at[blocks, 0]
+            head_out[...] = jnp.where(take, to_left[:, :lanes], head)
+            take = (row == 0) & (lane >= skip) & (lane < skip + cols)
+            fixed = jnp.where(take, to_right, two)
+            for k in range(held):
+                block_ref[k, 0] = fixed[:, k * lanes : (k + 1) * lanes]
+                send(k)
+            sent.append(pltpu.make_async_copy(head_out, out_hbm.at[0, :, pl.ds(0, lanes)], sems.at[blocks]))
+            sent[-1].start()
+        elif block >= held:
+            send(block)
+    for copy in sent:
+        copy.wait()
+
+
+def make_forward(plan, own, pieces, tables, before=None):
+    half = plan.groups * plan.cols
+    lead = half if before else 0
+    skip = lead % lanes
+    blocks = -(-(skip + half) // lanes)
+    any_space, whole = pl.BlockSpec(memory_space=pl.ANY), pl.BlockSpec(memory_space=pltpu.VMEM)
+    outs, out_specs, operands, alias = [real_array(plan.devices, plan.rows, 2 * half)], [any_space], list(pieces), {}
+    in_specs = [pl.BlockSpec(memory_space=pltpu.SMEM)] + [whole] * len(pieces)
+    if before:
+        tails, side, spectrum, edge, head = before
+        operands += [tails, side, edge, head, spectrum]
+        in_specs += [whole] * 4 + [any_space]
+        alias = {len(operands): 0}
+    else:
+        outs += [real_array(plan.devices, plan.rows, lanes), real_array(plan.rows, lanes)]
+        out_specs += [whole] * 2
+    run = pl.pallas_call(
+        lambda *refs: forward_kernel(plan, lead, *refs),
+        out_shape=outs,
+        in_specs=in_specs + [whole] * 2,
+        out_specs=out_specs,
+        scratch_shapes=[
+            pltpu.VMEM((plan.radix, plan.cols, lanes), jnp.float32),
+            pltpu.VMEM((blocks * lanes, 2 * lanes), jnp.bfloat16),
+            pltpu.VMEM((blocks * lanes, 2 * lanes), jnp.bfloat16),
+            pltpu.VMEM((blocks + 1, plan.devices, plan.rows, lanes), jnp.float32),
+            pltpu.SemaphoreType.DMA((blocks + 1,)),
+        ],
+        input_output_aliases=alias,
+        compiler_params=pltpu.CompilerParams(vmem_limit_bytes=16 << 20),
+    )
+    return run(own, *operands, *tables)
 
 
 def middle_kernel(plan, position_ref, in_ref, t1_ref, t2_ref, t2i_ref, t1i_ref, twiddle_ref, out_ref, high_ref, low_ref, back_high, back_low, turn_ref):
@@ -665,9 +745,15 @@
             lines = jnp.where(moved, pltpu.roll(extra, deep, 1), lines)
         turn_ref[rows, :] = lines
     for start in range(0, groups * cols, lanes):
-        block = turn_ref[start : start + lanes, :].T
+        block = turn_ref[start : start + lanes, :].T.reshape(count, plan.rows, lanes)
         keep = min(lanes, groups * cols - start)
-        out_ref[:, :, start : start + keep] = block.reshape(count, plan.rows, lanes)[:, :, :keep]
+        real, imag = block[:, :deep], block[:, deep:]
+        if keep < lanes:
+            place = lax.broadcasted_iota(jnp.int32, real.shape, 2)
+            out_ref[:, :, 2 * start : 2 * start + 2 * keep] = jnp.where(place < keep, real, pltpu.roll(imag, keep, 2))[:, :, : 2 * keep]
+        else:
+            out_ref[:, :, 2 * start : 2 * start + lanes] = real
+            out_ref[:, :, 2 * start + lanes : 2 * start + 2 * lanes] = imag
 
 
 def inverse_kernel(plan, own_ref, in_ref, twiddle_ref, table_ref, *refs):
@@ -678,8 +764,10 @@
     total = groups * cols
     for start in range(0, total, lanes):
         keep = min(lanes, total - start)
-        block = in_ref[:, :, start : start + keep].reshape(size, keep)
-        turn_ref[start : start + keep, :] = block.T
+        real = in_ref[:, :, 2 * start : 2 * start + lanes]
+        imag = pltpu.roll(real, keep, 2) if keep < lanes else in_ref[:, :, 2 * start + lanes : 2 * start + 2 * lanes]
+        block = jnp.concatenate([real, imag], 1).reshape(size, lanes)
+        turn_ref[start : start + keep, :] = block.T[:keep]
     for g in range(groups):
         rows = slice(g * cols, (g + 1) * cols)
         kind = 1 if g == 0 else 0
@@ -708,14 +796,35 @@
 
 
 def final_kernel(plan, own_ref, *refs):
-    pieces, (out_ref, line_ref) = refs[:-2], refs[-2:]
+    pieces, (out_hbm, line_ref, block_ref, sems) = refs[: plan.gx], refs[plan.gx :]
     own = own_ref[0]
-    for step in range(plan.gx):
-        start = pl.multiple_of((own ^ step) * plan.cols, 8)
-        for a in range(plan.here):
+    sent = []
+    for a in range(plan.here):
+        for step in range(plan.gx):
+            start = pl.multiple_of((own ^ step) * plan.cols, 8)
             line_ref[a, pl.ds(start, plan.cols), :] = pieces[step][a]
-    for a in range(plan.here):
-        out_ref[a * lanes : (a + 1) * lanes, :] = line_ref[a].T
+        block_ref[a] = line_ref[a].T
+        sent.append(pltpu.make_async_copy(block_ref.at[a], out_hbm.at[pl.ds(a * lanes, lanes), :], sems.at[a]))
+        sent[-1].start()
+    for copy in sent:
+        copy.wait()
+
+
+def make_final(plan, own, pieces, shape):
+    whole = pl.BlockSpec(memory_space=pltpu.VMEM)
+    run = pl.pallas_call(
+        lambda *refs: final_kernel(plan, *refs),
+        out_shape=real_array(*shape),
+        in_specs=[pl.BlockSpec(memory_space=pltpu.SMEM)] + [whole] * plan.gx,
+        out_specs=pl.BlockSpec(memory_space=pl.ANY),
+        scratch_shapes=[
+            pltpu.VMEM((plan.here, shape[1], lanes), jnp.float32),
+            pltpu.VMEM((plan.here, lanes, shape[1]), jnp.float32),
+            pltpu.SemaphoreType.DMA((plan.here,)),
+        ],
+        compiler_params=pltpu.CompilerParams(vmem_limit_bytes=16 << 20),
+    )
+    return run(own, *pieces)
 
 
 def swap_gx(plan, pieces):
@@ -731,20 +840,6 @@
     half = groups * cols
     pieces = [real_array(plan.here, cols, lanes)] * plan.gx
     line = vmem((plan.radix, cols, lanes), f32)
-
-    def forward(lead, own, *operands):
-        skip = lead % lanes
-        rounded = -(-(skip + half) // lanes) * lanes
-        outs = [real_array(plan.devices, plan.rows, lead - skip + rounded)]
-        if not lead:
-            outs += [real_array(plan.gx, plan.tail, lanes), real_array(plan.radix, 1, lanes)]
-        return call(
-            lambda *refs: forward_kernel(plan, lead, *refs),
-            outs,
-            [line] + [vmem((rounded, size), bf16)] * 2,
-            [own],
-            *operands,
-        )
 
     def local(thickness, bed_uplift, flux_x, flux_y, mass_balance, ice_mask):
         own = lax.axis_index("gx").reshape(1)
@@ -756,9 +851,10 @@
         lines_v = swap_gx(plan, load)
         twiddle = plan.slot_twiddle()
         tables = np.stack([table_halves(table) for table in plan.slot_matrix()])
-        spectrum_u, tails_u, edge = forward(0, own, *(lines_u + [twiddle, tables]))
-        side = passed_along(edge, "gy", 1)
-        (spectrum,) = forward(half, own, *(lines_v + [tails_u, side, spectrum_u, twiddle, tables]))
+        (tails_u,) = call(lambda *refs: tails_kernel(plan, *refs), [real_array(plan.gx, plan.tail, lanes)], [], [], *lines_u)
+        side = passed_along(tails_u, "gy", 1)
+        partial = make_forward(plan, own, lines_u, (twiddle, tables))
+        (spectrum,) = make_forward(plan, own, lines_v, (twiddle, tables), (tails_u, side, *partial))
         thickness_new = make_thickness(plan, own, fields, (tails_u, side))
         received = exchange_all(spectrum)
         source, across = plan.source_matrix(), plan.line_matrix()
@@ -766,7 +862,7 @@
         tables = [table_halves(table) for table in (source, across, across.T * scale, source.T)]
         (middle,) = call(
             lambda *refs: middle_kernel(plan, *refs),
-            [real_array(plan.devices, plan.rows, half)],
+            [real_array(plan.devices, plan.deep, 2 * half)],
             [vmem((2 * half, size), bf16)] * 2 + [vmem((half + cols, size), bf16)] * 2 + [vmem((half + cols, size), f32)],
             [position],
             *([received] + tables + [plan.line_twiddle()]),
@@ -781,20 +877,14 @@
             *(back, twiddle, inverse),
         )
         lines_b = swap_gx(plan, bed)
-        (bed_new,) = call(
-            lambda *refs: final_kernel(plan, *refs),
-            [real_array(*thickness.shape)],
-            [vmem((plan.here, plan.gx * cols, lanes), f32)],
-            [own],
-            *lines_b,
-        )
+        bed_new = make_final(plan, own, lines_b, thickness.shape)
         return thickness_new, bed_new
 
     return local
 
 
 def build(plan):
-    if plan.devices * plan.rows == 2 * lanes and plan.cols % 16 == 0 and plan.radix <= 16 and plan.gx in (2, 4, 8):
+    if plan.devices * plan.rows == 2 * lanes and plan.cols % 16 == 0 and plan.radix <= 16 and plan.gx in (2, 4, 8) and plan.groups * plan.cols % lanes in (0, lanes // 2):
         return build_kernels(plan)
 
     def local(thickness, bed_uplift, flux_x, flux_y, mass_balance, ice_mask):

time: 93.6 us -> 91.5 us (0.978)
  blocking collectives: 21.4 us -> 20.2 us
    pallas_call x0 -> x4, Pallas kernels: none -> 7.35 us  [the longest x2 4.06 us: make_forward(): return run(own, *operands, *tables)]
    pallas_call x5 -> x3, Pallas kernels: 8.54 us -> 3.51 us  [call(): return run(*scalars, *operands)]
    pallas_call x3 -> x2, Pallas kernels: 9.41 us -> 6.96 us  [kernel_call(): return run(*scalars, *inputs, *faces)]
    all_to_all x1, blocking collectives: 21.4 us -> 20.2 us  [exchange_all(): lax.all_to_all(value, ('gy', 'gx'), split_axis=0, concat_axis=0, tiled=True)]
  transfers between devices with their start and end apart: 11 -> 11, of which waited for: 5 -> 5; matrix products, arithmetic and copies ran while one was open for 0% -> 0% of each run, Pallas kernels for 9% -> 10%
where the time goes in v3:
time: 91.5 us; the launch traced here: 91.1 us
  waiting for transfers between devices  35.8 us (39%)
  blocking collectives  20.2 us (22%)
  Pallas kernels  17.8 us (19%)
  starting transfers between devices  16.3 us (18%)
    all_to_all x1, waiting for transfers between devices, exchange_all(): lax.all_to_all(value, ('gy', 'gx'), split_axis=0, concat_axis=0, tiled=True)  29 us
    all_to_all x1, blocking collectives, exchange_all(): lax.all_to_all(value, ('gy', 'gx'), split_axis=0, concat_axis=0, tiled=True)  20.2 us
    ppermute x9, starting transfers between devices, swap_gx(): lax.ppermute(pieces[step], 'gx', [(k, k ^ step) for k in range(plan.gx)])  7.16 us
    pallas_call x2, Pallas kernels, kernel_call(): return run(*scalars, *inputs, *faces)  6.96 us
    ppermute x9, waiting for transfers between devices, swap_gx(): lax.ppermute(pieces[step], 'gx', [(k, k ^ step) for k in range(plan.gx)])  6.79 us
    all_to_all x1, starting transfers between devices, exchange_all(): lax.all_to_all(value, ('gy', 'gx'), split_axis=0, concat_axis=0, tiled=True)  5.76 us
    pallas_call x2, Pallas kernels, make_forward(): return run(own, *operands, *tables)  4.06 us
    pallas_call x3, Pallas kernels, call(): return run(*scalars, *operands)  3.51 us
  transfers between devices with their start and end apart: 11, of which 5 were waited for; matrix products, arithmetic and copies ran while one was open for 0% of the time, Pallas kernels for 10%

profile of v3, /device:TPU:0, one launch (start us, length us, event | category | flops | bytes accessed | tf_op | source)
XLA Modules:
  0.0 91.1 jit_solution(15729487287162037158)
XLA Ops:
  0.6 2.3 %shard_map.149 = (f32[296,128]{1,0:T(8,128)}, f32[296,128]{1,0:T(8,128)}, f32[296,128]{1,0:T(8,128)}, f32[296,128]{1,0:T(8,128)}) custom-call(s32[1]{0:T(128)} %bitcast.refs_0_, f32[384,384]{1,0:T(8,128)} %refs_1_.3, f32[384,384]{1,0:T(8,128)} %refs_2_.7, f32[384,384]{1,0:T(8,128)} %refs_3_.7), custom_call_target="tpu_custom_call" | custom-call | tf_op jit(solution)/shard_map/pallas_call | solution.py:404
  2.9 0.6 collective-permute-start
  3.5 2.6 %collective-permute-start.1 = (f32[296,128]{1,0:T(8,128)}, f32[296,128]{1,0:T(8,128)S(1)}, u32[]{:S(2)}, u32[]{:S(2)}) collective-permute-start(f32[296,128]{1,0:T(8,128)} %get-tuple-element.19), channel_id=1, source_target_pairs={{0,16},{8,24},{16,0},{24,8},{1,17},{9,25},{17,1},{25,9},{2,18},{10... | collective-permute-start | bytes 454664 | tf_op jit(solution)/shard_map/ppermute | solution.py:833
  6.1 0.1 collective-permute-start.2
  6.2 3.2 %shard_map.152 = (f32[296,128]{1,0:T(8,128)}, f32[296,128]{1,0:T(8,128)}, f32[296,128]{1,0:T(8,128)}, f32[296,128]{1,0:T(8,128)}) custom-call(s32[1]{0:T(128)} %bitcast.refs_0_, f32[384,384]{1,0:T(8,128)} %refs_1_.5, f32[384,384]{1,0:T(8,128)} %refs_2_.7, f32[384,384]{1,0:T(8,128)} %refs_3_.7, f32[384,384]{1,0:T(8,128)} %refs_4_.4, s32[384,384]{1,0:T(8,128)} %refs_5_.5), custom_call_target="tpu_custom_call" | custom-call | tf_op jit(solution)/shard_map/pallas_call | solution.py:344
  9.4 0.0 copy-start.7
  9.4 0.2 collective-permute-start.4
  9.6 1.9 %collective-permute-start.5 = (f32[296,128]{1,0:T(8,128)}, f32[296,128]{1,0:T(8,128)S(1)}, u32[]{:S(2)}, u32[]{:S(2)}) collective-permute-start(f32[296,128]{1,0:T(8,128)} %get-tuple-element.23), channel_id=1, source_target_pairs={{0,16},{8,24},{16,0},{24,8},{1,17},{9,25},{17,1},{25,9},{2,18},{10... | collective-permute-start | bytes 454664 | tf_op jit(solution)/shard_map/ppermute | solution.py:833
  11.5 0.0 collective-permute-done.refs_1_.refs_2_
  11.5 0.0 collective-permute-start.6
  11.5 0.0 collective-permute-done.1.refs_2_.refs_3_
  11.5 2.5 %collective-permute-done.2.refs_3_.refs_4_ = f32[296,128]{1,0:T(8,128)S(1)} collective-permute-done((f32[296,128]{1,0:T(8,128)}, f32[296,128]{1,0:T(8,128)S(1)}, u32[]{:S(2)}, u32[]{:S(2)}) %collective-permute-start.2) | collective-permute-done | bytes 151584 | tf_op jit(solution)/shard_map/ppermute | solution.py:833
  14.0 0.0 copy-done.1
  14.0 3.4 %collective-permute-start.3 = (f32[4,8,128]{2,1,0:T(8,128)S(1)}, f32[4,8,128]{2,1,0:T(8,128)S(1)}, u32[]{:S(2)}, u32[]{:S(2)}) collective-permute-start(f32[4,8,128]{2,1,0:T(8,128)S(1)} %shard_map.150.refs_6_.refs_5_), channel_id=1, source_target_pairs={{0,1},{1,2},{2,3},{3,4},{4,5},{5,6},{6,7},{8,9},{9,10},{10,11},{11... | collective-permute-start | bytes 49160 | tf_op jit(solution)/shard_map/ppermute | solution.py:178
  17.4 0.0 copy-done
  17.4 0.0 copy-done.10
  17.4 1.8 %shard_map.153 = (f32[32,8,1152]{2,1,0:T(8,128)}, f32[32,8,128]{2,1,0:T(8,128)S(1)}, f32[8,128]{1,0:T(8,128)S(1)}) custom-call(s32[1]{0:T(128)} %bitcast.refs_0_, f32[296,128]{1,0:T(8,128)S(1)} %copy-done.1, f32[296,128]{1,0:T(8,128)S(1)} %collective-permute-done.refs_1_.refs_2_, f32[296,128]{1,0:T(8,128)S(1)} %collective-permute-done.1.refs_2_.refs_3_, ...), custom_call_target="tpu_custom_call" | custom-call | tf_op jit(solution)/shard_map/pallas_call | solution.py:678
  19.2 0.0 collective-permute-done.4.refs_2_
  19.2 0.0 collective-permute-done.5.refs_3_
  19.3 1.0 %collective-permute-done.6.refs_4_ = f32[296,128]{1,0:T(8,128)S(1)} collective-permute-done((f32[296,128]{1,0:T(8,128)}, f32[296,128]{1,0:T(8,128)S(1)}, u32[]{:S(2)}, u32[]{:S(2)}) %collective-permute-start.6) | collective-permute-done | bytes 151584 | tf_op jit(solution)/shard_map/ppermute | solution.py:833
  20.3 0.0 collective-permute-done.3.refs_7_.refs_6_
  20.3 0.0 copy-done.7
  20.3 2.2 %shard_map.154 = f32[32,8,1152]{2,1,0:T(8,128)} custom-call(s32[1]{0:T(128)} %bitcast.refs_0_, f32[296,128]{1,0:T(8,128)S(1)} %copy-done.7, f32[296,128]{1,0:T(8,128)S(1)} %collective-permute-done.4.refs_2_, f32[296,128]{1,0:T(8,128)S(1)} %collective-permute-done.5.refs_3_, ...), custom_call_target="tpu_custom_call", output_to_operand_aliasing={{}: (9, {})} | custom-call | tf_op jit(solution)/shard_map/pallas_call | solution.py:678
  22.5 0.0 copy-done.8
  22.5 0.0 copy-done.11
  22.6 0.0 copy-start.3
  22.6 0.0 copy-start.4
  22.6 0.0 copy-start.5
  22.6 0.0 copy-start.6
  22.6 0.0 copy-start.9
  22.6 5.8 %all-to-all-start = ((f32[32,8,1152]{2,1,0:T(8,128)}), f32[32,8,1152]{2,1,0:T(8,128)S(1)}, u32[]{:S(2)}, u32[]{:S(2)}) async-start(f32[32,8,1152]{2,1,0:T(8,128)} %shard_map.154), calls=%async_computation | async-start | bytes 2359296 | tf_op jit(solution)/shard_map/all_to_all | solution.py:172
  28.4 29.0 %all-to-all-done.refs_1_ = f32[32,8,1152]{2,1,0:T(8,128)S(1)} async-done(((f32[32,8,1152]{2,1,0:T(8,128)}), f32[32,8,1152]{2,1,0:T(8,128)S(1)}, u32[]{:S(2)}, u32[]{:S(2)}) %all-to-all-start) | async-done | bytes 1179680 | tf_op jit(solution)/shard_map/all_to_all | solution.py:172
  57.4 0.0 copy-done.3
  57.4 0.0 copy-done.4
  57.4 0.0 copy-done.5
  57.4 0.0 copy-done.6
  57.4 2.7 %shard_map.155 = f32[32,4,1152]{2,1,0:T(4,128)S(1)} custom-call(s32[1]{0:T(128)} %bitcast.1.refs_0_, f32[32,8,1152]{2,1,0:T(8,128)S(1)} %all-to-all-done.refs_1_, bf16[2,256,256]{2,1,0:T(8,128)(2,1)S(1)} %copy-done.3, bf16[2,192,192]{2,1,0:T(8,128)(2,1)S(1)} %copy-done.5, bf16[2,192,192]{2,1,0:T(8,128)(2,1)S(1)} %copy-done.6, ...), custom_call_target="tpu_custom_call" | custom-call | tf_op jit(solution)/shard_map/pallas_call | solution.py:307
  60.1 0.0 copy-start.2
  60.2 20.2 %all_to_all.10.refs_1_ = f32[32,4,1152]{2,1,0:T(4,128)S(1)} all-to-all(f32[32,4,1152]{2,1,0:T(4,128)S(1)} %shard_map.155), channel_id=1, replica_groups=mesh['gx'=4,'gy'=8] {'gy','gx'}, dimensions={0} | all-to-all | bytes 1179648 | tf_op jit(solution)/shard_map/all_to_all | solution.py:172
  80.4 0.8 shard_map.156
  81.2 0.1 collective-permute-start.7
  81.3 1.4 %collective-permute-start.8 = (f32[3,96,128]{2,1,0:T(8,128)S(1)}, f32[3,96,128]{2,1,0:T(8,128)S(1)}, u32[]{:S(2)}, u32[]{:S(2)}) collective-permute-start(f32[3,96,128]{2,1,0:T(8,128)S(1)} %get-tuple-element.30), channel_id=1, source_target_pairs={{0,16},{8,24},{16,0},{24,8},{1,17},{9,25},{17,1},{25,9},{2,18},{10... | collective-permute-start | bytes 442376 | tf_op jit(solution)/shard_map/ppermute | solution.py:833
  82.7 0.5 collective-permute-start.9
  83.1 3.7 %shard_map.151 = f32[384,384]{1,0:T(8,128)} custom-call(s32[1]{0:T(128)} %bitcast.refs_0_, f32[384,384]{1,0:T(8,128)} %refs_1_.5, f32[384,384]{1,0:T(8,128)} %refs_2_.7, f32[384,384]{1,0:T(8,128)} %refs_3_.7, f32[384,384]{1,0:T(8,128)} %refs_4_.4, s32[384,384]{1,0:T(8,128)} %refs_5_.5, f32[4,8,128]{2,1,0:T(8,128)} %copy-done.8, f32[4,8,128]{2,1,0:T(8,128)} %copy-done.11), custom_call_target="tpu_custom_call" | custom-call | tf_op jit(solution)/shard_map/pallas_call | solution.py:344
  86.9 0.0 collective-permute-done.7.refs_2_
  86.9 1.2 %collective-permute-done.8.refs_3_ = f32[3,96,128]{2,1,0:T(8,128)S(1)} collective-permute-done((f32[3,96,128]{2,1,0:T(8,128)S(1)}, f32[3,96,128]{2,1,0:T(8,128)S(1)}, u32[]{:S(2)}, u32[]{:S(2)}) %collective-permute-start.8) | collective-permute-done | bytes 147488 | tf_op jit(solution)/shard_map/ppermute | solution.py:833
  88.1 2.1 %collective-permute-done.9.refs_4_ = f32[3,96,128]{2,1,0:T(8,128)S(1)} collective-permute-done((f32[3,96,128]{2,1,0:T(8,128)S(1)}, f32[3,96,128]{2,1,0:T(8,128)S(1)}, u32[]{:S(2)}, u32[]{:S(2)}) %collective-permute-start.9) | collective-permute-done | bytes 147488 | tf_op jit(solution)/shard_map/ppermute | solution.py:833
  90.1 1.0 %shard_map.157 = f32[384,384]{1,0:T(8,128)} custom-call(s32[1]{0:T(128)} %bitcast.refs_0_, f32[3,96,128]{2,1,0:T(8,128)S(1)} %get-tuple-element.28.refs_1_, f32[3,96,128]{2,1,0:T(8,128)S(1)} %collective-permute-done.7.refs_2_, f32[3,96,128]{2,1,0:T(8,128)S(1)} %collective-permute-done.8.refs_3_, f32[3,96,128]{2,1,0:T(8,128)S(1)} %collective-permute-done.9.refs_4_), custom_call_target="tpu_custom_call" | custom-call | tf_op jit(solution)/shard_map/pallas_call | solution.py:827
  (8 shorter events, 0.0 us)
Async XLA Ops:
  2.9 8.5 %collective-permute-start = (f32[296,128]{1,0:T(8,128)}, f32[296,128]{1,0:T(8,128)S(1)}, u32[]{:S(2)}, u32[]{:S(2)}) collective-permute-start(f32[296,128]{1,0:T(8,128)} %get-tuple-element.18), channel_id=1, source_target_pairs={{0,8},{8,0},{16,24},{24,16},{1,9},{9,1},{17,25},{25,17},{2,10},{10... | collective-permute-start | bytes 454664 | tf_op jit(solution)/shard_map/ppermute | solution.py:833
  3.5 8.0 %collective-permute-start.1 = (f32[296,128]{1,0:T(8,128)}, f32[296,128]{1,0:T(8,128)S(1)}, u32[]{:S(2)}, u32[]{:S(2)}) collective-permute-start(f32[296,128]{1,0:T(8,128)} %get-tuple-element.19), channel_id=1, source_target_pairs={{0,16},{8,24},{16,0},{24,8},{1,17},{9,25},{17,1},{25,9},{2,18},{10... | collective-permute-start | bytes 454664 | tf_op jit(solution)/shard_map/ppermute | solution.py:833
  6.1 7.9 %copy-start.1 = (f32[296,128]{1,0:T(8,128)S(1)}, f32[296,128]{1,0:T(8,128)}, u32[]{:S(2)}) copy-start(f32[296,128]{1,0:T(8,128)} %get-tuple-element.17.refs_0_.refs_1_) | copy-start | bytes 454660
  6.1 11.3 %copy-start = (bf16[2,2,256,256]{3,2,1,0:T(8,128)(2,1)S(1)}, bf16[2,2,256,256]{3,2,1,0:T(8,128)(2,1)}, u32[]{:S(2)}) copy-start(bf16[2,2,256,256]{3,2,1,0:T(8,128)(2,1)} %constant.27.clone.refs_6_.refs_11_) | copy-start | bytes 1572868
  6.1 11.3 %copy-start.10 = (f32[2,6,128]{2,1,0:T(8,128)S(1)}, f32[2,6,128]{2,1,0:T(8,128)}, u32[]{:S(2)}) copy-start(f32[2,6,128]{2,1,0:T(8,128)} %constant.26.clone.refs_5_.refs_10_.refs_2_) | copy-start | bytes 18436
  6.1 7.9 %collective-permute-start.2 = (f32[296,128]{1,0:T(8,128)}, f32[296,128]{1,0:T(8,128)S(1)}, u32[]{:S(2)}, u32[]{:S(2)}) collective-permute-start(f32[296,128]{1,0:T(8,128)} %get-tuple-element.20), channel_id=1, source_target_pairs={{0,24},{8,16},{16,8},{24,0},{1,25},{9,17},{17,9},{25,1},{2,26},{10... | collective-permute-start | bytes 454664 | tf_op jit(solution)/shard_map/ppermute | solution.py:833
  9.4 10.9 %copy-start.7 = (f32[296,128]{1,0:T(8,128)S(1)}, f32[296,128]{1,0:T(8,128)}, u32[]{:S(2)}) copy-start(f32[296,128]{1,0:T(8,128)} %get-tuple-element.21.refs_1_) | copy-start | bytes 454660
  9.4 9.8 %collective-permute-start.4 = (f32[296,128]{1,0:T(8,128)}, f32[296,128]{1,0:T(8,128)S(1)}, u32[]{:S(2)}, u32[]{:S(2)}) collective-permute-start(f32[296,128]{1,0:T(8,128)} %get-tuple-element.22), channel_id=1, source_target_pairs={{0,8},{8,0},{16,24},{24,16},{1,9},{9,1},{17,25},{25,17},{2,10},{10... | collective-permute-start | bytes 454664 | tf_op jit(solution)/shard_map/ppermute | solution.py:833
  9.6 9.7 %collective-permute-start.5 = (f32[296,128]{1,0:T(8,128)}, f32[296,128]{1,0:T(8,128)S(1)}, u32[]{:S(2)}, u32[]{:S(2)}) collective-permute-start(f32[296,128]{1,0:T(8,128)} %get-tuple-element.23), channel_id=1, source_target_pairs={{0,16},{8,24},{16,0},{24,8},{1,17},{9,25},{17,1},{25,9},{2,18},{10... | collective-permute-start | bytes 454664 | tf_op jit(solution)/shard_map/ppermute | solution.py:833
  11.5 8.8 %collective-permute-start.6 = (f32[296,128]{1,0:T(8,128)}, f32[296,128]{1,0:T(8,128)S(1)}, u32[]{:S(2)}, u32[]{:S(2)}) collective-permute-start(f32[296,128]{1,0:T(8,128)} %get-tuple-element.24), channel_id=1, source_target_pairs={{0,24},{8,16},{16,8},{24,0},{1,25},{9,17},{17,9},{25,1},{2,26},{10... | collective-permute-start | bytes 454664 | tf_op jit(solution)/shard_map/ppermute | solution.py:833
  14.0 8.6 %copy-start.8 = (f32[4,8,128]{2,1,0:T(8,128)}, f32[4,8,128]{2,1,0:T(8,128)S(1)}, u32[]{:S(2)}) copy-start(f32[4,8,128]{2,1,0:T(8,128)S(1)} %shard_map.150.refs_6_.refs_5_) | copy-start | bytes 49156
  14.0 6.3 %collective-permute-start.3 = (f32[4,8,128]{2,1,0:T(8,128)S(1)}, f32[4,8,128]{2,1,0:T(8,128)S(1)}, u32[]{:S(2)}, u32[]{:S(2)}) collective-permute-start(f32[4,8,128]{2,1,0:T(8,128)S(1)} %shard_map.150.refs_6_.refs_5_), channel_id=1, source_target_pairs={{0,1},{1,2},{2,3},{3,4},{4,5},{5,6},{6,7},{8,9},{9,10},{10,11},{11... | collective-permute-start | bytes 49160 | tf_op jit(solution)/shard_map/ppermute | solution.py:178
  20.3 2.3 %copy-start.11 = (f32[4,8,128]{2,1,0:T(8,128)}, f32[4,8,128]{2,1,0:T(8,128)S(1)}, u32[]{:S(2)}) copy-start(f32[4,8,128]{2,1,0:T(8,128)S(1)} %collective-permute-done.3.refs_7_.refs_6_) | copy-start | bytes 49156
  22.6 34.8 %copy-start.3 = (bf16[2,256,256]{2,1,0:T(8,128)(2,1)S(1)}, bf16[2,256,256]{2,1,0:T(8,128)(2,1)}, u32[]{:S(2)}) copy-start(bf16[2,256,256]{2,1,0:T(8,128)(2,1)} %constant.28.clone.refs_2_) | copy-start | bytes 786436
  22.6 34.8 %copy-start.4 = (bf16[2,256,256]{2,1,0:T(8,128)(2,1)S(1)}, bf16[2,256,256]{2,1,0:T(8,128)(2,1)}, u32[]{:S(2)}) copy-start(bf16[2,256,256]{2,1,0:T(8,128)(2,1)} %constant.31.clone.refs_5_) | copy-start | bytes 786436
  22.6 34.8 %copy-start.5 = (bf16[2,192,192]{2,1,0:T(8,128)(2,1)S(1)}, bf16[2,192,192]{2,1,0:T(8,128)(2,1)}, u32[]{:S(2)}) copy-start(bf16[2,192,192]{2,1,0:T(8,128)(2,1)} %constant.29.clone.refs_3_) | copy-start | bytes 442372
  22.6 34.8 %copy-start.6 = (bf16[2,192,192]{2,1,0:T(8,128)(2,1)S(1)}, bf16[2,192,192]{2,1,0:T(8,128)(2,1)}, u32[]{:S(2)}) copy-start(bf16[2,192,192]{2,1,0:T(8,128)(2,1)} %constant.30.clone.refs_4_) | copy-start | bytes 442372
  22.6 34.8 %copy-start.9 = (f32[2,96,128]{2,1,0:T(8,128)S(1)}, f32[2,96,128]{2,1,0:T(8,128)}, u32[]{:S(2)}) copy-start(f32[2,96,128]{2,1,0:T(8,128)} %constant.32.clone.refs_6_) | copy-start | bytes 294916
  22.6 34.8 %all-to-all-start = ((f32[32,8,1152]{2,1,0:T(8,128)}), f32[32,8,1152]{2,1,0:T(8,128)S(1)}, u32[]{:S(2)}, u32[]{:S(2)}) async-start(f32[32,8,1152]{2,1,0:T(8,128)} %shard_map.154), calls=%async_computation | async-start | bytes 2359296 | tf_op jit(solution)/shard_map/all_to_all | solution.py:172
  60.1 20.2 %copy-start.2 = (bf16[2,2,256,256]{3,2,1,0:T(8,128)(2,1)S(1)}, bf16[2,2,256,256]{3,2,1,0:T(8,128)(2,1)}, u32[]{:S(2)}) copy-start(bf16[2,2,256,256]{3,2,1,0:T(8,128)(2,1)} %constant.33.clone.refs_3_) | copy-start | bytes 1572868
  81.2 5.7 %collective-permute-start.7 = (f32[3,96,128]{2,1,0:T(8,128)S(1)}, f32[3,96,128]{2,1,0:T(8,128)S(1)}, u32[]{:S(2)}, u32[]{:S(2)}) collective-permute-start(f32[3,96,128]{2,1,0:T(8,128)S(1)} %get-tuple-element.29), channel_id=1, source_target_pairs={{0,8},{8,0},{16,24},{24,16},{1,9},{9,1},{17,25},{25,17},{2,10},{10... | collective-permute-start | bytes 442376 | tf_op jit(solution)/shard_map/ppermute | solution.py:833
  81.3 6.8 %collective-permute-start.8 = (f32[3,96,128]{2,1,0:T(8,128)S(1)}, f32[3,96,128]{2,1,0:T(8,128)S(1)}, u32[]{:S(2)}, u32[]{:S(2)}) collective-permute-start(f32[3,96,128]{2,1,0:T(8,128)S(1)} %get-tuple-element.30), channel_id=1, source_target_pairs={{0,16},{8,24},{16,0},{24,8},{1,17},{9,25},{17,1},{25,9},{2,18},{10... | collective-permute-start | bytes 442376 | tf_op jit(solution)/shard_map/ppermute | solution.py:833
  82.7 7.5 %collective-permute-start.9 = (f32[3,96,128]{2,1,0:T(8,128)S(1)}, f32[3,96,128]{2,1,0:T(8,128)S(1)}, u32[]{:S(2)}, u32[]{:S(2)}) collective-permute-start(f32[3,96,128]{2,1,0:T(8,128)S(1)} %get-tuple-element.31), channel_id=1, source_target_pairs={{0,24},{8,16},{16,8},{24,0},{1,25},{9,17},{17,9},{25,1},{2,26},{10... | collective-permute-start | bytes 442376 | tf_op jit(solution)/shard_map/ppermute | solution.py:833

commit v4 on v3

--- a/solution.py
+++ b/solution.py
@@ -281,16 +281,24 @@
 
 def table_halves(table):
     high = table.astype(jnp.bfloat16)
-    return np.stack([high, (table - high.astype(np.float32)).astype(jnp.bfloat16)])
-
-
-def product(left, right, turned=False):
+    return np.concatenate([high, (table - high.astype(np.float32)).astype(jnp.bfloat16)], 0)
+
+
+def dot(left, right, turned=False):
     dims = (((1,), (1 if turned else 0,)), ((), ()))
-
-    def one(a, b):
-        return lax.dot_general(a, b, dims, preferred_element_type=jnp.float32)
-
-    return one(left[0], right[0]) + (one(left[0], right[1]) + one(left[1], right[0]))
+    return lax.dot_general(left, right, dims, preferred_element_type=jnp.float32)
+
+
+def table_times(table, data, turned=False):
+    rows = table.shape[0] // 2
+    both = dot(table, data[0], turned)
+    return both[:rows] + (both[rows:] + dot(table[:rows], data[1], turned))
+
+
+def times_table(data, table):
+    rows, inner = data[0].shape[0], table.shape[0] // 2
+    both = dot(jnp.concatenate(data, 0), table[:inner])
+    return both[:rows] + (both[rows:] + dot(data[0], table[inner:]))
 
 
 def call(body, outs, scratch, scalars, *operands):
@@ -344,7 +352,7 @@
     return run(*scalars, *inputs, *faces)
 
 
-def uplift_kernel(plan, own_ref, uplift_hbm, flux_x_hbm, flux_y_hbm, *refs):
+def uplift_kernel(plan, own_ref, _, uplift_hbm, flux_x_hbm, flux_y_hbm, *refs):
     own = own_ref[0]
     out_refs = refs[: plan.gx]
     field_ref, turned_ref, tail_ref, last_x_ref, last_y_ref, sems, out_sems = refs[plan.gx :]
@@ -384,12 +392,12 @@
         copy.wait()
 
 
-def send_uplift(plan, own, bed_uplift, flux_x, flux_y):
+def send_uplift(plan, own, across_y, bed_uplift, flux_x, flux_y):
     rows, cols = bed_uplift.shape
     run = pl.pallas_call(
         lambda *refs: uplift_kernel(plan, *refs),
         out_shape=[real_array(plan.piece_rows, lanes)] * plan.gx,
-        in_specs=[pl.BlockSpec(memory_space=pltpu.SMEM)] + [pl.BlockSpec(memory_space=pl.ANY)] * 3,
+        in_specs=[pl.BlockSpec(memory_space=pltpu.SMEM)] * 2 + [pl.BlockSpec(memory_space=pl.ANY)] * 3,
         out_specs=[pl.BlockSpec(memory_space=pl.ANY)] * plan.gx,
         scratch_shapes=[
             pltpu.VMEM((rows, cols), jnp.float32),
@@ -401,7 +409,7 @@
             pltpu.SemaphoreType.DMA((plan.here + 1, plan.gx)),
         ],
     )
-    return run(own, bed_uplift, flux_x, flux_y)
+    return run(own, across_y, bed_uplift, flux_x, flux_y)
 
 
 def fetch_fields(plan, sources, mask_ref, floats_ref, sems):
@@ -584,8 +592,6 @@
         if edge[0] < edge[1]:
             high_ref[edge[0] : edge[1], :] = jnp.zeros((edge[1] - edge[0], 2 * lanes), jnp.bfloat16)
             low_ref[edge[0] : edge[1], :] = jnp.zeros((edge[1] - edge[0], 2 * lanes), jnp.bfloat16)
-    general = (table_ref[0, 0], table_ref[0, 1])
-    special = (table_ref[1, 0], table_ref[1, 1])
     before = (lead - skip) // lanes
     blocks = high_ref.shape[0] // lanes
     sent = []
@@ -596,18 +602,18 @@
         sent[-1].start()
 
     held = -(-(skip + cols) // lanes) if lead else 0
+    end = skip + cols
+    special = -(-end // lanes) * lanes
+    first = table_times(table_ref[1], (high_ref[:special, :], low_ref[:special, :]), True)
     for block in range(blocks):
         start = block * lanes
-        rows = slice(start, start + lanes)
-        data = (high_ref[rows, :], low_ref[rows, :])
-        end = skip + cols
-        lane = lax.broadcasted_iota(jnp.int32, (2 * lanes, lanes), 1)
-        if start + lanes <= end:
-            out = product(special, data, True)
-        else:
-            out = product(general, data, True)
-            if start < end:
-                out = jnp.where(lane < end - start, product(special, data, True), out)
+        if block % 2 == 0:
+            rows = slice(start, min(start + 2 * lanes, blocks * lanes))
+            pair = table_times(table_ref[0], (high_ref[rows, :], low_ref[rows, :]), True)
+        out = pair[:, (block % 2) * lanes : (block % 2 + 1) * lanes]
+        if start < end:
+            lane = lax.broadcasted_iota(jnp.int32, (2 * lanes, lanes), 1)
+            out = jnp.where(lane < end - start, first[:, start : start + lanes], out)
         out = out.reshape(plan.devices, plan.rows, lanes)
         if start < skip:
             lane = lax.broadcasted_iota(jnp.int32, out.shape, 2)
@@ -678,17 +684,17 @@
     return run(own, *operands, *tables)
 
 
-def middle_kernel(plan, position_ref, in_ref, t1_ref, t2_ref, t2i_ref, t1i_ref, twiddle_ref, out_ref, high_ref, low_ref, back_high, back_low, turn_ref):
-    position = position_ref[0]
+def middle_kernel(plan, own_ref, across_ref, in_ref, t1_ref, t2_ref, t2i_ref, t1i_ref, twiddle_ref, out_ref, high_ref, low_ref, back_high, back_low, turn_ref, mixed_ref):
+    position = across_ref[0] * plan.gx + own_ref[0]
     cols, groups, deep, count = plan.cols, plan.groups, plan.deep, plan.devices
     width, size = lanes, 2 * lanes
     for start in range(0, 2 * groups * cols, lanes):
         block = in_ref[:, :, start : start + lanes].reshape(size, lanes).T
         high_ref[start : start + lanes, :], low_ref[start : start + lanes, :] = halves(block)
-    t1 = (t1_ref[0], t1_ref[1])
-    t2 = (t2_ref[0], t2_ref[1])
-    t2i = (t2i_ref[0], t2i_ref[1])
-    t1i = (t1i_ref[0], t1i_ref[1])
+    step = 2 * groups * cols // 4
+    for start in range(0, 2 * groups * cols, step):
+        rows = slice(start, start + step)
+        mixed_ref[rows, :] = times_table((high_ref[rows, :], low_ref[rows, :]), t1_ref[...])
     cos, sin = twiddle_ref[0], twiddle_ref[1]
     lane = lax.broadcasted_iota(jnp.int32, (1, width), 1)
     q, t = lane % deep, lane // deep
@@ -697,19 +703,13 @@
     m = position * deep + q
     special = jnp.broadcast_to((position == 0) & (q == 0), (cols, width))
     results = []
-    mixed = []
     for g in range(groups):
-        if g % 2 == 0:
-            mixed = []
-            for field in range(2):
-                rows = slice((field * groups + g) * cols, (field * groups + min(g + 2, groups)) * cols)
-                mixed.append(product((high_ref[rows, :], low_ref[rows, :]), t1))
         sides = []
         for field in range(2):
-            part = mixed[field][(g % 2) * cols : (g % 2 + 1) * cols]
+            part = mixed_ref[(field * groups + g) * cols : (field * groups + g + 1) * cols, :]
             re, im = part[:, :width], part[:, width:]
             sides.append(jnp.concatenate([re * cos + im * sin, im * cos - re * sin], 0))
-        spectra = product(t2, halves(jnp.concatenate(sides, 1)))
+        spectra = table_times(t2_ref[...], halves(jnp.concatenate(sides, 1)))
         ur, vr = spectra[:cols, :width], spectra[:cols, width:]
         ui, vi = spectra[cols:, :width], spectra[cols:, width:]
         half = lanes // 2
@@ -728,22 +728,21 @@
     results.append(extra)
     for g in range(0, groups + 1, 2):
         pair = results[g : g + 2]
-        back = product(t2i, halves(jnp.concatenate(pair, 1)))
+        back = table_times(t2i_ref[...], halves(jnp.concatenate(pair, 1)))
         for k in range(len(pair)):
             re, im = back[:cols, k * width : (k + 1) * width], back[cols:, k * width : (k + 1) * width]
             turned = jnp.concatenate([re * cos - im * sin, im * cos + re * sin], 1)
             place = slice((g + k) * cols, (g + k + 1) * cols)
             back_high[place, :], back_low[place, :] = halves(turned)
-    last = slice(groups * cols, (groups + 1) * cols)
-    extra = product((back_high[last, :], back_low[last, :]), t1i)
+    total = (groups + 1) * cols
+    cuts = [total * k // 2 // 16 * 16 for k in range(2)] + [total]
+    for start, stop in zip(cuts, cuts[1:]):
+        rows = slice(start, stop)
+        turn_ref[rows, :] = times_table((back_high[rows, :], back_low[rows, :]), t1i_ref[...])
     place = lax.broadcasted_iota(jnp.int32, (cols, size), 1)
     moved = (position == 0) & (place % plan.rows == deep)
-    for g in range(groups):
-        rows = slice(g * cols, (g + 1) * cols)
-        lines = product((back_high[rows, :], back_low[rows, :]), t1i)
-        if g == 0:
-            lines = jnp.where(moved, pltpu.roll(extra, deep, 1), lines)
-        turn_ref[rows, :] = lines
+    extra = turn_ref[groups * cols : (groups + 1) * cols, :]
+    turn_ref[:cols, :] = jnp.where(moved, pltpu.roll(extra, deep, 1), turn_ref[:cols, :])
     for start in range(0, groups * cols, lanes):
         block = turn_ref[start : start + lanes, :].T.reshape(count, plan.rows, lanes)
         keep = min(lanes, groups * cols - start)
@@ -768,10 +767,8 @@
         imag = pltpu.roll(real, keep, 2) if keep < lanes else in_ref[:, :, 2 * start + lanes : 2 * start + 2 * lanes]
         block = jnp.concatenate([real, imag], 1).reshape(size, lanes)
         turn_ref[start : start + keep, :] = block.T[:keep]
-    for g in range(groups):
-        rows = slice(g * cols, (g + 1) * cols)
-        kind = 1 if g == 0 else 0
-        mid_ref[rows, :] = product(halves(turn_ref[rows, :]), (table_ref[kind, 0], table_ref[kind, 1]))
+    mid_ref[:cols, :] = times_table(halves(turn_ref[:cols, :]), table_ref[1])
+    mid_ref[cols:, :] = times_table(halves(turn_ref[cols:, :]), table_ref[0])
     step_rows = 16
 
     def chunk(index, carry):
@@ -842,10 +839,9 @@
     line = vmem((plan.radix, cols, lanes), f32)
 
     def local(thickness, bed_uplift, flux_x, flux_y, mass_balance, ice_mask):
-        own = lax.axis_index("gx").reshape(1)
-        position = (lax.axis_index("gy") * plan.gx + lax.axis_index("gx")).reshape(1)
+        own, across_y = lax.axis_index("gx").reshape(1), lax.axis_index("gy").reshape(1)
         fields = (thickness, flux_x, flux_y, mass_balance, ice_mask)
-        uplift = send_uplift(plan, own, bed_uplift, flux_x, flux_y)
+        uplift = send_uplift(plan, own, across_y, bed_uplift, flux_x, flux_y)
         lines_u = swap_gx(plan, uplift)
         load = make_load(plan, own, fields)
         lines_v = swap_gx(plan, load)
@@ -863,8 +859,8 @@
         (middle,) = call(
             lambda *refs: middle_kernel(plan, *refs),
             [real_array(plan.devices, plan.deep, 2 * half)],
-            [vmem((2 * half, size), bf16)] * 2 + [vmem((half + cols, size), bf16)] * 2 + [vmem((half + cols, size), f32)],
-            [position],
+            [vmem((2 * half, size), bf16)] * 2 + [vmem((half + cols, size), bf16)] * 2 + [vmem((half + cols, size), f32), vmem((2 * half, size), f32)],
+            [own, across_y],
             *([received] + tables + [plan.line_twiddle()]),
         )
         back = exchange_all(middle)

time: 91.5 us -> 90.5 us (0.989)
  blocking collectives: 20.2 us -> 54.8 us
  waiting for transfers between devices: 35.8 us -> 7.1 us
  starting transfers between devices: 16.3 us -> 10.6 us
  Pallas kernels: 17.8 us -> 16.7 us
    all_to_all x1 -> x2, blocking collectives: 20.2 us -> 54.8 us  [exchange_all(): lax.all_to_all(value, ('gy', 'gx'), split_axis=0, concat_axis=0, tiled=True)]
    all_to_all x1 -> x0, waiting for transfers between devices: 29 us -> none  [exchange_all(): lax.all_to_all(value, ('gy', 'gx'), split_axis=0, concat_axis=0, tiled=True)]
    all_to_all x1 -> x0, starting transfers between devices: 5.76 us -> none  [exchange_all(): lax.all_to_all(value, ('gy', 'gx'), split_axis=0, concat_axis=0, tiled=True)]
  transfers between devices with their start and end apart: 11 -> 10, of which waited for: 5 -> 4; matrix products, arithmetic and copies ran while one was open for 0% -> 0% of each run, Pallas kernels for 10% -> 9%
where the time goes in v4:
time: 90.5 us; the launch traced here: 90.1 us
  blocking collectives  54.8 us (61%)
  Pallas kernels  16.7 us (18%)
  starting transfers between devices  10.6 us (12%)
  waiting for transfers between devices  7.1 us (8%)
    all_to_all x2, blocking collectives, exchange_all(): lax.all_to_all(value, ('gy', 'gx'), split_axis=0, concat_axis=0, tiled=True)  54.8 us
    ppermute x9, starting transfers between devices, swap_gx(): lax.ppermute(pieces[step], 'gx', [(k, k ^ step) for k in range(plan.gx)])  7.16 us
    ppermute x9, waiting for transfers between devices, swap_gx(): lax.ppermute(pieces[step], 'gx', [(k, k ^ step) for k in range(plan.gx)])  7.1 us
    pallas_call x2, Pallas kernels, kernel_call(): return run(*scalars, *inputs, *faces)  6.95 us
    pallas_call x2, Pallas kernels, make_forward(): return run(own, *operands, *tables)  3.46 us
    ppermute x1, starting transfers between devices, passed_along(): lax.ppermute(value, axis, [(source, source + steps) for source in range(l...  3.42 us
    pallas_call x3, Pallas kernels, call(): return run(*scalars, *operands)  2.98 us
    pallas_call x1, Pallas kernels, send_uplift(): return run(own, across_y, bed_uplift, flux_x, flux_y)  2.31 us
  transfers between devices with their start and end apart: 10, of which 4 were waited for; matrix products, arithmetic and copies ran while one was open for 0% of the time, Pallas kernels for 9%

profile of v4, /device:TPU:0, one launch (start us, length us, event | category | flops | bytes accessed | tf_op | source)
XLA Modules:
  0.0 90.1 jit_solution(4581142318899945760)
XLA Ops:
  0.6 2.3 %shard_map.149 = (f32[296,128]{1,0:T(8,128)}, f32[296,128]{1,0:T(8,128)}, f32[296,128]{1,0:T(8,128)}, f32[296,128]{1,0:T(8,128)}) custom-call(s32[1]{0:T(128)} %bitcast.refs_0_, s32[1]{0:T(128)} %bitcast.1.refs_1_, f32[384,384]{1,0:T(8,128)} %refs_2_.4, f32[384,384]{1,0:T(8,128)} %refs_2_.6, f32[384,384]{1,0:T(8,128)} %refs_3_.7), custom_call_target="tpu_custom_call" | custom-call | tf_op jit(solution)/shard_map/pallas_call | solution.py:412
  3.0 0.6 collective-permute-start
  3.5 2.6 %collective-permute-start.1 = (f32[296,128]{1,0:T(8,128)}, f32[296,128]{1,0:T(8,128)S(1)}, u32[]{:S(2)}, u32[]{:S(2)}) collective-permute-start(f32[296,128]{1,0:T(8,128)} %get-tuple-element.19), channel_id=1, source_target_pairs={{0,16},{8,24},{16,0},{24,8},{1,17},{9,25},{17,1},{25,9},{2,18},{10... | collective-permute-start | bytes 454664 | tf_op jit(solution)/shard_map/ppermute | solution.py:830
  6.1 0.1 collective-permute-start.2
  6.2 3.2 %shard_map.152 = (f32[296,128]{1,0:T(8,128)}, f32[296,128]{1,0:T(8,128)}, f32[296,128]{1,0:T(8,128)}, f32[296,128]{1,0:T(8,128)}) custom-call(s32[1]{0:T(128)} %bitcast.refs_0_, f32[384,384]{1,0:T(8,128)} %refs_1_.3, f32[384,384]{1,0:T(8,128)} %refs_2_.6, f32[384,384]{1,0:T(8,128)} %refs_3_.7, f32[384,384]{1,0:T(8,128)} %refs_4_.6, s32[384,384]{1,0:T(8,128)} %refs_5_.5), custom_call_target="tpu_custom_call" | custom-call | tf_op jit(solution)/shard_map/pallas_call | solution.py:352
  9.4 0.0 copy-start.7
  9.4 0.2 collective-permute-start.4
  9.6 1.9 %collective-permute-start.5 = (f32[296,128]{1,0:T(8,128)}, f32[296,128]{1,0:T(8,128)S(1)}, u32[]{:S(2)}, u32[]{:S(2)}) collective-permute-start(f32[296,128]{1,0:T(8,128)} %get-tuple-element.23), channel_id=1, source_target_pairs={{0,16},{8,24},{16,0},{24,8},{1,17},{9,25},{17,1},{25,9},{2,18},{10... | collective-permute-start | bytes 454664 | tf_op jit(solution)/shard_map/ppermute | solution.py:830
  11.4 0.0 collective-permute-done.refs_1_.refs_2_
  11.5 0.0 collective-permute-start.6
  11.5 0.0 collective-permute-done.1.refs_2_.refs_3_
  11.5 2.5 %collective-permute-done.2.refs_3_.refs_4_ = f32[296,128]{1,0:T(8,128)S(1)} collective-permute-done((f32[296,128]{1,0:T(8,128)}, f32[296,128]{1,0:T(8,128)S(1)}, u32[]{:S(2)}, u32[]{:S(2)}) %collective-permute-start.2) | collective-permute-done | bytes 151584 | tf_op jit(solution)/shard_map/ppermute | solution.py:830
  14.0 0.0 copy-done.1
  14.0 3.4 %collective-permute-start.3 = (f32[4,8,128]{2,1,0:T(8,128)S(1)}, f32[4,8,128]{2,1,0:T(8,128)S(1)}, u32[]{:S(2)}, u32[]{:S(2)}) collective-permute-start(f32[4,8,128]{2,1,0:T(8,128)S(1)} %shard_map.150.refs_6_.refs_5_), channel_id=1, source_target_pairs={{0,1},{1,2},{2,3},{3,4},{4,5},{5,6},{6,7},{8,9},{9,10},{10,11},{11... | collective-permute-start | bytes 49160 | tf_op jit(solution)/shard_map/ppermute | solution.py:178
  17.4 0.0 copy-done
  17.4 0.0 copy-done.10
  17.4 1.5 %shard_map.153 = (f32[32,8,1152]{2,1,0:T(8,128)S(1)}, f32[32,8,128]{2,1,0:T(8,128)S(1)}, f32[8,128]{1,0:T(8,128)S(1)}) custom-call(s32[1]{0:T(128)} %bitcast.refs_0_, f32[296,128]{1,0:T(8,128)S(1)} %copy-done.1, f32[296,128]{1,0:T(8,128)S(1)} %collective-permute-done.refs_1_.refs_2_, f32[296,128]{1,0:T(8,128)S(1)} %collective-permute-done.1.refs_2_.refs_3_, ...), custom_call_target="tpu_custom_call" | custom-call | tf_op jit(solution)/shard_map/pallas_call | solution.py:684
  19.0 0.0 collective-permute-done.4.refs_2_
  19.0 0.0 collective-permute-done.5.refs_3_
  19.0 1.3 %collective-permute-done.6.refs_4_ = f32[296,128]{1,0:T(8,128)S(1)} collective-permute-done((f32[296,128]{1,0:T(8,128)}, f32[296,128]{1,0:T(8,128)S(1)}, u32[]{:S(2)}, u32[]{:S(2)}) %collective-permute-start.6) | collective-permute-done | bytes 151584 | tf_op jit(solution)/shard_map/ppermute | solution.py:830
  20.3 0.0 collective-permute-done.3.refs_7_.refs_6_
  20.3 0.0 copy-done.7
  20.3 1.9 %shard_map.154 = f32[32,8,1152]{2,1,0:T(8,128)S(1)} custom-call(s32[1]{0:T(128)} %bitcast.refs_0_, f32[296,128]{1,0:T(8,128)S(1)} %copy-done.7, f32[296,128]{1,0:T(8,128)S(1)} %collective-permute-done.4.refs_2_, f32[296,128]{1,0:T(8,128)S(1)} %collective-permute-done.5.refs_3_, ...), custom_call_target="tpu_custom_call", output_to_operand_aliasing={{}: (9, {})} | custom-call | tf_op jit(solution)/shard_map/pallas_call | solution.py:684
  22.2 0.0 copy-done.8
  22.2 0.0 copy-done.11
  22.2 0.0 copy-start.3
  22.3 0.0 copy-start.4
  22.3 0.0 copy-start.5
  22.3 0.0 copy-start.6
  22.3 0.0 copy-start.9
  22.3 36.2 %all_to_all.10.refs_2_ = f32[32,8,1152]{2,1,0:T(8,128)S(1)} all-to-all(f32[32,8,1152]{2,1,0:T(8,128)S(1)} %shard_map.154), channel_id=1, replica_groups=mesh['gx'=4,'gy'=8] {'gy','gx'}, dimensions={0} | all-to-all | bytes 2359296 | tf_op jit(solution)/shard_map/all_to_all | solution.py:172
  58.5 0.0 copy-done.3
  58.5 0.0 copy-done.4
  58.5 0.0 copy-done.5
  58.5 0.0 copy-done.6
  58.5 0.0 copy-done.9
  58.5 2.2 %shard_map.155 = f32[32,4,1152]{2,1,0:T(4,128)S(1)} custom-call(s32[1]{0:T(128)} %bitcast.refs_0_, s32[1]{0:T(128)} %bitcast.1.refs_1_, f32[32,8,1152]{2,1,0:T(8,128)S(1)} %all_to_all.10.refs_2_, bf16[512,256]{1,0:T(8,128)(2,1)S(1)} %copy-done.3, bf16[384,192]{1,0:T(8,128)(2,1)S(1)} %copy-done.5, bf16[384,192]{1,0:T(8,128)(2,1)S(1)} %copy-done.6, ...), custom_call_target="tpu_custom_call" | custom-call | tf_op jit(solution)/shard_map/pallas_call | solution.py:315
  60.8 18.7 %all_to_all.11.refs_1_ = f32[32,4,1152]{2,1,0:T(4,128)S(1)} all-to-all(f32[32,4,1152]{2,1,0:T(4,128)S(1)} %shard_map.155), channel_id=1, replica_groups=mesh['gx'=4,'gy'=8] {'gy','gx'}, dimensions={0} | all-to-all | bytes 1179648 | tf_op jit(solution)/shard_map/all_to_all | solution.py:172
  79.4 0.0 copy-done.2
  79.4 0.8 shard_map.156
  80.2 0.1 collective-permute-start.7
  80.3 1.4 %collective-permute-start.8 = (f32[3,96,128]{2,1,0:T(8,128)S(1)}, f32[3,96,128]{2,1,0:T(8,128)S(1)}, u32[]{:S(2)}, u32[]{:S(2)}) collective-permute-start(f32[3,96,128]{2,1,0:T(8,128)S(1)} %get-tuple-element.30), channel_id=1, source_target_pairs={{0,16},{8,24},{16,0},{24,8},{1,17},{9,25},{17,1},{25,9},{2,18},{10... | collective-permute-start | bytes 442376 | tf_op jit(solution)/shard_map/ppermute | solution.py:830
  81.6 0.5 collective-permute-start.9
  82.1 3.7 %shard_map.151 = f32[384,384]{1,0:T(8,128)} custom-call(s32[1]{0:T(128)} %bitcast.refs_0_, f32[384,384]{1,0:T(8,128)} %refs_1_.3, f32[384,384]{1,0:T(8,128)} %refs_2_.6, f32[384,384]{1,0:T(8,128)} %refs_3_.7, f32[384,384]{1,0:T(8,128)} %refs_4_.6, s32[384,384]{1,0:T(8,128)} %refs_5_.5, f32[4,8,128]{2,1,0:T(8,128)} %copy-done.8, f32[4,8,128]{2,1,0:T(8,128)} %copy-done.11), custom_call_target="tpu_custom_call" | custom-call | tf_op jit(solution)/shard_map/pallas_call | solution.py:352
  85.8 0.0 collective-permute-done.7.refs_2_
  85.8 1.2 %collective-permute-done.8.refs_3_ = f32[3,96,128]{2,1,0:T(8,128)S(1)} collective-permute-done((f32[3,96,128]{2,1,0:T(8,128)S(1)}, f32[3,96,128]{2,1,0:T(8,128)S(1)}, u32[]{:S(2)}, u32[]{:S(2)}) %collective-permute-start.8) | collective-permute-done | bytes 147488 | tf_op jit(solution)/shard_map/ppermute | solution.py:830
  87.0 2.1 %collective-permute-done.9.refs_4_ = f32[3,96,128]{2,1,0:T(8,128)S(1)} collective-permute-done((f32[3,96,128]{2,1,0:T(8,128)S(1)}, f32[3,96,128]{2,1,0:T(8,128)S(1)}, u32[]{:S(2)}, u32[]{:S(2)}) %collective-permute-start.9) | collective-permute-done | bytes 147488 | tf_op jit(solution)/shard_map/ppermute | solution.py:830
  89.1 1.0 %shard_map.157 = f32[384,384]{1,0:T(8,128)} custom-call(s32[1]{0:T(128)} %bitcast.refs_0_, f32[3,96,128]{2,1,0:T(8,128)S(1)} %get-tuple-element.28.refs_1_, f32[3,96,128]{2,1,0:T(8,128)S(1)} %collective-permute-done.7.refs_2_, f32[3,96,128]{2,1,0:T(8,128)S(1)} %collective-permute-done.8.refs_3_, f32[3,96,128]{2,1,0:T(8,128)S(1)} %collective-permute-done.9.refs_4_), custom_call_target="tpu_custom_call" | custom-call | tf_op jit(solution)/shard_map/pallas_call | solution.py:824
  (7 shorter events, 0.0 us)
Async XLA Ops:
  3.0 8.5 %collective-permute-start = (f32[296,128]{1,0:T(8,128)}, f32[296,128]{1,0:T(8,128)S(1)}, u32[]{:S(2)}, u32[]{:S(2)}) collective-permute-start(f32[296,128]{1,0:T(8,128)} %get-tuple-element.18), channel_id=1, source_target_pairs={{0,8},{8,0},{16,24},{24,16},{1,9},{9,1},{17,25},{25,17},{2,10},{10... | collective-permute-start | bytes 454664 | tf_op jit(solution)/shard_map/ppermute | solution.py:830
  3.5 7.9 %collective-permute-start.1 = (f32[296,128]{1,0:T(8,128)}, f32[296,128]{1,0:T(8,128)S(1)}, u32[]{:S(2)}, u32[]{:S(2)}) collective-permute-start(f32[296,128]{1,0:T(8,128)} %get-tuple-element.19), channel_id=1, source_target_pairs={{0,16},{8,24},{16,0},{24,8},{1,17},{9,25},{17,1},{25,9},{2,18},{10... | collective-permute-start | bytes 454664 | tf_op jit(solution)/shard_map/ppermute | solution.py:830
  6.1 7.9 %copy-start.1 = (f32[296,128]{1,0:T(8,128)S(1)}, f32[296,128]{1,0:T(8,128)}, u32[]{:S(2)}) copy-start(f32[296,128]{1,0:T(8,128)} %get-tuple-element.17.refs_0_.refs_1_) | copy-start | bytes 454660
  6.1 11.3 %copy-start = (bf16[2,512,256]{2,1,0:T(8,128)(2,1)S(1)}, bf16[2,512,256]{2,1,0:T(8,128)(2,1)}, u32[]{:S(2)}) copy-start(bf16[2,512,256]{2,1,0:T(8,128)(2,1)} %constant.25.clone.refs_6_.refs_11_) | copy-start | bytes 1572868
  6.1 11.3 %copy-start.10 = (f32[2,6,128]{2,1,0:T(8,128)S(1)}, f32[2,6,128]{2,1,0:T(8,128)}, u32[]{:S(2)}) copy-start(f32[2,6,128]{2,1,0:T(8,128)} %constant.24.clone.refs_5_.refs_10_.refs_2_) | copy-start | bytes 18436
  6.1 7.9 %collective-permute-start.2 = (f32[296,128]{1,0:T(8,128)}, f32[296,128]{1,0:T(8,128)S(1)}, u32[]{:S(2)}, u32[]{:S(2)}) collective-permute-start(f32[296,128]{1,0:T(8,128)} %get-tuple-element.20), channel_id=1, source_target_pairs={{0,24},{8,16},{16,8},{24,0},{1,25},{9,17},{17,9},{25,1},{2,26},{10... | collective-permute-start | bytes 454664 | tf_op jit(solution)/shard_map/ppermute | solution.py:830
  9.4 10.9 %copy-start.7 = (f32[296,128]{1,0:T(8,128)S(1)}, f32[296,128]{1,0:T(8,128)}, u32[]{:S(2)}) copy-start(f32[296,128]{1,0:T(8,128)} %get-tuple-element.21.refs_1_) | copy-start | bytes 454660
  9.4 9.5 %collective-permute-start.4 = (f32[296,128]{1,0:T(8,128)}, f32[296,128]{1,0:T(8,128)S(1)}, u32[]{:S(2)}, u32[]{:S(2)}) collective-permute-start(f32[296,128]{1,0:T(8,128)} %get-tuple-element.22), channel_id=1, source_target_pairs={{0,8},{8,0},{16,24},{24,16},{1,9},{9,1},{17,25},{25,17},{2,10},{10... | collective-permute-start | bytes 454664 | tf_op jit(solution)/shard_map/ppermute | solution.py:830
  9.6 9.4 %collective-permute-start.5 = (f32[296,128]{1,0:T(8,128)}, f32[296,128]{1,0:T(8,128)S(1)}, u32[]{:S(2)}, u32[]{:S(2)}) collective-permute-start(f32[296,128]{1,0:T(8,128)} %get-tuple-element.23), channel_id=1, source_target_pairs={{0,16},{8,24},{16,0},{24,8},{1,17},{9,25},{17,1},{25,9},{2,18},{10... | collective-permute-start | bytes 454664 | tf_op jit(solution)/shard_map/ppermute | solution.py:830
  11.5 8.8 %collective-permute-start.6 = (f32[296,128]{1,0:T(8,128)}, f32[296,128]{1,0:T(8,128)S(1)}, u32[]{:S(2)}, u32[]{:S(2)}) collective-permute-start(f32[296,128]{1,0:T(8,128)} %get-tuple-element.24), channel_id=1, source_target_pairs={{0,24},{8,16},{16,8},{24,0},{1,25},{9,17},{17,9},{25,1},{2,26},{10... | collective-permute-start | bytes 454664 | tf_op jit(solution)/shard_map/ppermute | solution.py:830
  14.0 8.3 %copy-start.8 = (f32[4,8,128]{2,1,0:T(8,128)}, f32[4,8,128]{2,1,0:T(8,128)S(1)}, u32[]{:S(2)}) copy-start(f32[4,8,128]{2,1,0:T(8,128)S(1)} %shard_map.150.refs_6_.refs_5_) | copy-start | bytes 49156
  14.0 6.3 %collective-permute-start.3 = (f32[4,8,128]{2,1,0:T(8,128)S(1)}, f32[4,8,128]{2,1,0:T(8,128)S(1)}, u32[]{:S(2)}, u32[]{:S(2)}) collective-permute-start(f32[4,8,128]{2,1,0:T(8,128)S(1)} %shard_map.150.refs_6_.refs_5_), channel_id=1, source_target_pairs={{0,1},{1,2},{2,3},{3,4},{4,5},{5,6},{6,7},{8,9},{9,10},{10,11},{11... | collective-permute-start | bytes 49160 | tf_op jit(solution)/shard_map/ppermute | solution.py:178
  20.3 2.0 %copy-start.11 = (f32[4,8,128]{2,1,0:T(8,128)}, f32[4,8,128]{2,1,0:T(8,128)S(1)}, u32[]{:S(2)}) copy-start(f32[4,8,128]{2,1,0:T(8,128)S(1)} %collective-permute-done.3.refs_7_.refs_6_) | copy-start | bytes 49156
  22.2 36.3 %copy-start.3 = (bf16[512,256]{1,0:T(8,128)(2,1)S(1)}, bf16[512,256]{1,0:T(8,128)(2,1)}, u32[]{:S(2)}) copy-start(bf16[512,256]{1,0:T(8,128)(2,1)} %constant.26.clone.refs_3_) | copy-start | bytes 786436
  22.3 36.2 %copy-start.4 = (bf16[512,256]{1,0:T(8,128)(2,1)S(1)}, bf16[512,256]{1,0:T(8,128)(2,1)}, u32[]{:S(2)}) copy-start(bf16[512,256]{1,0:T(8,128)(2,1)} %constant.29.clone.refs_6_) | copy-start | bytes 786436
  22.3 36.2 %copy-start.5 = (bf16[384,192]{1,0:T(8,128)(2,1)S(1)}, bf16[384,192]{1,0:T(8,128)(2,1)}, u32[]{:S(2)}) copy-start(bf16[384,192]{1,0:T(8,128)(2,1)} %constant.27.clone.refs_4_) | copy-start | bytes 442372
  22.3 36.2 %copy-start.6 = (bf16[384,192]{1,0:T(8,128)(2,1)S(1)}, bf16[384,192]{1,0:T(8,128)(2,1)}, u32[]{:S(2)}) copy-start(bf16[384,192]{1,0:T(8,128)(2,1)} %constant.28.clone.refs_5_) | copy-start | bytes 442372
  22.3 36.2 %copy-start.9 = (f32[2,96,128]{2,1,0:T(8,128)S(1)}, f32[2,96,128]{2,1,0:T(8,128)}, u32[]{:S(2)}) copy-start(f32[2,96,128]{2,1,0:T(8,128)} %constant.30.clone.refs_7_) | copy-start | bytes 294916
  60.7 18.7 %copy-start.2 = (bf16[2,512,256]{2,1,0:T(8,128)(2,1)S(1)}, bf16[2,512,256]{2,1,0:T(8,128)(2,1)}, u32[]{:S(2)}) copy-start(bf16[2,512,256]{2,1,0:T(8,128)(2,1)} %constant.31.clone.refs_3_) | copy-start | bytes 1572868
  80.2 5.7 %collective-permute-start.7 = (f32[3,96,128]{2,1,0:T(8,128)S(1)}, f32[3,96,128]{2,1,0:T(8,128)S(1)}, u32[]{:S(2)}, u32[]{:S(2)}) collective-permute-start(f32[3,96,128]{2,1,0:T(8,128)S(1)} %get-tuple-element.29), channel_id=1, source_target_pairs={{0,8},{8,0},{16,24},{24,16},{1,9},{9,1},{17,25},{25,17},{2,10},{10... | collective-permute-start | bytes 442376 | tf_op jit(solution)/shard_map/ppermute | solution.py:830
  80.3 6.8 %collective-permute-start.8 = (f32[3,96,128]{2,1,0:T(8,128)S(1)}, f32[3,96,128]{2,1,0:T(8,128)S(1)}, u32[]{:S(2)}, u32[]{:S(2)}) collective-permute-start(f32[3,96,128]{2,1,0:T(8,128)S(1)} %get-tuple-element.30), channel_id=1, source_target_pairs={{0,16},{8,24},{16,0},{24,8},{1,17},{9,25},{17,1},{25,9},{2,18},{10... | collective-permute-start | bytes 442376 | tf_op jit(solution)/shard_map/ppermute | solution.py:830
  81.6 7.5 %collective-permute-start.9 = (f32[3,96,128]{2,1,0:T(8,128)S(1)}, f32[3,96,128]{2,1,0:T(8,128)S(1)}, u32[]{:S(2)}, u32[]{:S(2)}) collective-permute-start(f32[3,96,128]{2,1,0:T(8,128)S(1)} %get-tuple-element.31), channel_id=1, source_target_pairs={{0,24},{8,16},{16,8},{24,0},{1,25},{9,17},{17,9},{25,1},{2,26},{10... | collective-permute-start | bytes 442376 | tf_op jit(solution)/shard_map/ppermute | solution.py:830

commit v5 on v4

--- a/solution.py
+++ b/solution.py
@@ -558,9 +558,9 @@
     tail = slice(here * cols, here * cols + plan.tail)
     if lead:
         uplift_tails, side_ref, edge_ref, head_ref, _, twiddle_ref, table_ref, *refs = refs
-        out_hbm, line_ref, high_ref, low_ref, block_ref, sems = refs
+        out_ref, line_ref, high_ref, low_ref = refs
     else:
-        twiddle_ref, table_ref, out_hbm, edge_ref, head_ref, line_ref, high_ref, low_ref, block_ref, sems = refs
+        twiddle_ref, table_ref, out_ref, edge_ref, head_ref, line_ref, high_ref, low_ref = refs
     step_rows = 16
     total = groups * cols
     for step in range(plan.gx):
@@ -582,9 +582,9 @@
                 first = real[g] * cos + imag[g - 1] * sin
                 second = imag[g - 1] * cos - real[g] * sin
             high, low = halves(jnp.concatenate([first, second], 1))
-            place = pl.ds(skip + g * cols + row, step_rows)
-            high_ref[place, :] = high
-            low_ref[place, :] = low
+            target = pl.ds(skip + g * cols + row, step_rows)
+            high_ref[target, :] = high
+            low_ref[target, :] = low
         return carry
 
     lax.fori_loop(0, cols // step_rows, chunk, 0)
@@ -594,12 +594,9 @@
             low_ref[edge[0] : edge[1], :] = jnp.zeros((edge[1] - edge[0], 2 * lanes), jnp.bfloat16)
     before = (lead - skip) // lanes
     blocks = high_ref.shape[0] // lanes
-    sent = []
-
-    def send(block):
-        lane = pl.ds((before + block) * lanes, lanes)
-        sent.append(pltpu.make_async_copy(block_ref.at[block], out_hbm.at[:, :, lane], sems.at[block]))
-        sent[-1].start()
+
+    def place(block):
+        return slice((before + block) * lanes, (before + block + 1) * lanes)
 
     held = -(-(skip + cols) // lanes) if lead else 0
     end = skip + cols
@@ -621,11 +618,11 @@
         if not lead and (block + 1) * lanes > total:
             edge_ref[...] = out
             continue
-        block_ref[block] = out
+        out_ref[:, :, place(block)] = out
         if not lead and block == 0:
             head_ref[...] = out[0]
         if block + 1 == held:
-            two = jnp.concatenate([block_ref[k, 0] for k in range(held)], 1)
+            two = jnp.concatenate([out_ref[0, :, place(k)] for k in range(held)], 1)
             width = held * lanes
             row = lax.broadcasted_iota(jnp.int32, two.shape, 0)
             lane = lax.broadcasted_iota(jnp.int32, two.shape, 1)
@@ -635,19 +632,11 @@
             swapped = pltpu.roll(two, plan.deep, 0)
             to_left = pltpu.roll(swapped, width - skip, 1) if skip else swapped
             take = (row[:, :lanes] == plan.deep) & (lane[:, :lanes] < cols)
-            head_out = block_ref.at[blocks, 0]
-            head_out[...] = jnp.where(take, to_left[:, :lanes], head)
+            out_ref[0, :, :lanes] = jnp.where(take, to_left[:, :lanes], head)
             take = (row == 0) & (lane >= skip) & (lane < skip + cols)
             fixed = jnp.where(take, to_right, two)
             for k in range(held):
-                block_ref[k, 0] = fixed[:, k * lanes : (k + 1) * lanes]
-                send(k)
-            sent.append(pltpu.make_async_copy(head_out, out_hbm.at[0, :, pl.ds(0, lanes)], sems.at[blocks]))
-            sent[-1].start()
-        elif block >= held:
-            send(block)
-    for copy in sent:
-        copy.wait()
+                out_ref[0, :, place(k)] = fixed[:, k * lanes : (k + 1) * lanes]
 
 
 def make_forward(plan, own, pieces, tables, before=None):
@@ -655,33 +644,29 @@
     lead = half if before else 0
     skip = lead % lanes
     blocks = -(-(skip + half) // lanes)
-    any_space, whole = pl.BlockSpec(memory_space=pl.ANY), pl.BlockSpec(memory_space=pltpu.VMEM)
-    outs, out_specs, operands, alias = [real_array(plan.devices, plan.rows, 2 * half)], [any_space], list(pieces), {}
-    in_specs = [pl.BlockSpec(memory_space=pltpu.SMEM)] + [whole] * len(pieces)
+    whole = pl.BlockSpec(memory_space=pltpu.VMEM)
+    outs, operands, alias = [real_array(plan.devices, plan.rows, 2 * half)], list(pieces), {}
     if before:
         tails, side, spectrum, edge, head = before
         operands += [tails, side, edge, head, spectrum]
-        in_specs += [whole] * 4 + [any_space]
         alias = {len(operands): 0}
     else:
         outs += [real_array(plan.devices, plan.rows, lanes), real_array(plan.rows, lanes)]
-        out_specs += [whole] * 2
+    operands += tables
     run = pl.pallas_call(
         lambda *refs: forward_kernel(plan, lead, *refs),
         out_shape=outs,
-        in_specs=in_specs + [whole] * 2,
-        out_specs=out_specs,
+        in_specs=[pl.BlockSpec(memory_space=pltpu.SMEM)] + [whole] * len(operands),
+        out_specs=[whole] * len(outs),
         scratch_shapes=[
             pltpu.VMEM((plan.radix, plan.cols, lanes), jnp.float32),
             pltpu.VMEM((blocks * lanes, 2 * lanes), jnp.bfloat16),
             pltpu.VMEM((blocks * lanes, 2 * lanes), jnp.bfloat16),
-            pltpu.VMEM((blocks + 1, plan.devices, plan.rows, lanes), jnp.float32),
-            pltpu.SemaphoreType.DMA((blocks + 1,)),
         ],
         input_output_aliases=alias,
         compiler_params=pltpu.CompilerParams(vmem_limit_bytes=16 << 20),
     )
-    return run(own, *operands, *tables)
+    return run(own, *operands)
 
 
 def middle_kernel(plan, own_ref, across_ref, in_ref, t1_ref, t2_ref, t2i_ref, t1i_ref, twiddle_ref, out_ref, high_ref, low_ref, back_high, back_low, turn_ref, mixed_ref):

time: 90.5 us -> 89.8 us (level)
  Pallas kernels: 16.7 us -> 15.3 us
    pallas_call x2, Pallas kernels: 3.46 us -> 2.13 us  [make_forward(): return run(own, *operands)]
where the time goes in v5:
time: 89.8 us; the launch traced here: 89.4 us
  blocking collectives  54.9 us (61%)
  Pallas kernels  15.3 us (17%)
  starting transfers between devices  10.6 us (12%)
  waiting for transfers between devices  7.75 us (9%)
    all_to_all x2, blocking collectives, exchange_all(): lax.all_to_all(value, ('gy', 'gx'), split_axis=0, concat_axis=0, tiled=True)  54.9 us
    ppermute x9, waiting for transfers between devices, swap_gx(): lax.ppermute(pieces[step], 'gx', [(k, k ^ step) for k in range(plan.gx)])  7.75 us
    ppermute x9, starting transfers between devices, swap_gx(): lax.ppermute(pieces[step], 'gx', [(k, k ^ step) for k in range(plan.gx)])  7.16 us
    pallas_call x2, Pallas kernels, kernel_call(): return run(*scalars, *inputs, *faces)  6.95 us
    ppermute x1, starting transfers between devices, passed_along(): lax.ppermute(value, axis, [(source, source + steps) for source in range(l...  3.42 us
    pallas_call x3, Pallas kernels, call(): return run(*scalars, *operands)  2.98 us
    pallas_call x1, Pallas kernels, send_uplift(): return run(own, across_y, bed_uplift, flux_x, flux_y)  2.31 us
    pallas_call x2, Pallas kernels, make_forward(): return run(own, *operands)  2.13 us
  transfers between devices with their start and end apart: 10, of which 4 were waited for; matrix products, arithmetic and copies ran while one was open for 0% of the time, Pallas kernels for 9%

profile of v5, /device:TPU:0, one launch (start us, length us, event | category | flops | bytes accessed | tf_op | source)
XLA Modules:
  0.0 89.4 jit_solution(2095534588087836833)
XLA Ops:
  0.6 2.3 %shard_map.149 = (f32[296,128]{1,0:T(8,128)}, f32[296,128]{1,0:T(8,128)}, f32[296,128]{1,0:T(8,128)}, f32[296,128]{1,0:T(8,128)}) custom-call(s32[1]{0:T(128)} %bitcast.refs_0_, s32[1]{0:T(128)} %bitcast.1.refs_1_, f32[384,384]{1,0:T(8,128)} %refs_2_.4, f32[384,384]{1,0:T(8,128)} %refs_2_.6, f32[384,384]{1,0:T(8,128)} %refs_3_.7), custom_call_target="tpu_custom_call" | custom-call | tf_op jit(solution)/shard_map/pallas_call | solution.py:412
  3.0 0.6 collective-permute-start
  3.5 2.6 %collective-permute-start.1 = (f32[296,128]{1,0:T(8,128)}, f32[296,128]{1,0:T(8,128)S(1)}, u32[]{:S(2)}, u32[]{:S(2)}) collective-permute-start(f32[296,128]{1,0:T(8,128)} %get-tuple-element.19), channel_id=1, source_target_pairs={{0,16},{8,24},{16,0},{24,8},{1,17},{9,25},{17,1},{25,9},{2,18},{10... | collective-permute-start | bytes 454664 | tf_op jit(solution)/shard_map/ppermute | solution.py:815
  6.1 0.1 collective-permute-start.2
  6.2 3.2 %shard_map.152 = (f32[296,128]{1,0:T(8,128)}, f32[296,128]{1,0:T(8,128)}, f32[296,128]{1,0:T(8,128)}, f32[296,128]{1,0:T(8,128)}) custom-call(s32[1]{0:T(128)} %bitcast.refs_0_, f32[384,384]{1,0:T(8,128)} %refs_1_.3, f32[384,384]{1,0:T(8,128)} %refs_2_.6, f32[384,384]{1,0:T(8,128)} %refs_3_.7, f32[384,384]{1,0:T(8,128)} %refs_4_.6, s32[384,384]{1,0:T(8,128)} %refs_5_.5), custom_call_target="tpu_custom_call" | custom-call | tf_op jit(solution)/shard_map/pallas_call | solution.py:352
  9.4 0.0 copy-start.7
  9.4 0.2 collective-permute-start.4
  9.6 1.9 %collective-permute-start.5 = (f32[296,128]{1,0:T(8,128)}, f32[296,128]{1,0:T(8,128)S(1)}, u32[]{:S(2)}, u32[]{:S(2)}) collective-permute-start(f32[296,128]{1,0:T(8,128)} %get-tuple-element.23), channel_id=1, source_target_pairs={{0,16},{8,24},{16,0},{24,8},{1,17},{9,25},{17,1},{25,9},{2,18},{10... | collective-permute-start | bytes 454664 | tf_op jit(solution)/shard_map/ppermute | solution.py:815
  11.4 0.0 collective-permute-done.refs_1_.refs_2_
  11.5 0.0 collective-permute-start.6
  11.5 0.0 collective-permute-done.1.refs_2_.refs_3_
  11.5 2.5 %collective-permute-done.2.refs_3_.refs_4_ = f32[296,128]{1,0:T(8,128)S(1)} collective-permute-done((f32[296,128]{1,0:T(8,128)}, f32[296,128]{1,0:T(8,128)S(1)}, u32[]{:S(2)}, u32[]{:S(2)}) %collective-permute-start.2) | collective-permute-done | bytes 151584 | tf_op jit(solution)/shard_map/ppermute | solution.py:815
  14.0 0.0 copy-done.1
  14.0 3.4 %collective-permute-start.3 = (f32[4,8,128]{2,1,0:T(8,128)S(1)}, f32[4,8,128]{2,1,0:T(8,128)S(1)}, u32[]{:S(2)}, u32[]{:S(2)}) collective-permute-start(f32[4,8,128]{2,1,0:T(8,128)S(1)} %shard_map.150.refs_6_.refs_5_), channel_id=1, source_target_pairs={{0,1},{1,2},{2,3},{3,4},{4,5},{5,6},{6,7},{8,9},{9,10},{10,11},{11... | collective-permute-start | bytes 49160 | tf_op jit(solution)/shard_map/ppermute | solution.py:178
  17.4 0.0 copy-done
  17.4 0.0 copy-done.10
  17.4 0.9 shard_map.153
  18.3 0.0 collective-permute-done.4.refs_2_
  18.3 0.0 collective-permute-done.5.refs_3_
  18.3 2.0 %collective-permute-done.6.refs_4_ = f32[296,128]{1,0:T(8,128)S(1)} collective-permute-done((f32[296,128]{1,0:T(8,128)}, f32[296,128]{1,0:T(8,128)S(1)}, u32[]{:S(2)}, u32[]{:S(2)}) %collective-permute-start.6) | collective-permute-done | bytes 151584 | tf_op jit(solution)/shard_map/ppermute | solution.py:815
  20.3 0.0 collective-permute-done.3.refs_7_.refs_6_
  20.3 0.0 copy-done.7
  20.3 1.2 %shard_map.154 = f32[32,8,1152]{2,1,0:T(8,128)S(1)} custom-call(s32[1]{0:T(128)} %bitcast.refs_0_, f32[296,128]{1,0:T(8,128)S(1)} %copy-done.7, f32[296,128]{1,0:T(8,128)S(1)} %collective-permute-done.4.refs_2_, f32[296,128]{1,0:T(8,128)S(1)} %collective-permute-done.5.refs_3_, ...), custom_call_target="tpu_custom_call", output_to_operand_aliasing={{}: (9, {})} | custom-call | tf_op jit(solution)/shard_map/pallas_call | solution.py:669
  21.5 0.0 copy-done.8
  21.6 0.0 copy-done.11
  21.6 0.0 copy-start.3
  21.6 0.0 copy-start.4
  21.6 0.0 copy-start.5
  21.6 0.0 copy-start.6
  21.6 0.0 copy-start.9
  21.6 36.2 %all_to_all.10.refs_2_ = f32[32,8,1152]{2,1,0:T(8,128)S(1)} all-to-all(f32[32,8,1152]{2,1,0:T(8,128)S(1)} %shard_map.154), channel_id=1, replica_groups=mesh['gx'=4,'gy'=8] {'gy','gx'}, dimensions={0} | all-to-all | bytes 2359296 | tf_op jit(solution)/shard_map/all_to_all | solution.py:172
  57.8 0.0 copy-done.3
  57.8 0.0 copy-done.4
  57.8 0.0 copy-done.5
  57.8 0.0 copy-done.6
  57.8 0.0 copy-done.9
  57.9 2.2 %shard_map.155 = f32[32,4,1152]{2,1,0:T(4,128)S(1)} custom-call(s32[1]{0:T(128)} %bitcast.refs_0_, s32[1]{0:T(128)} %bitcast.1.refs_1_, f32[32,8,1152]{2,1,0:T(8,128)S(1)} %all_to_all.10.refs_2_, bf16[512,256]{1,0:T(8,128)(2,1)S(1)} %copy-done.3, bf16[384,192]{1,0:T(8,128)(2,1)S(1)} %copy-done.5, bf16[384,192]{1,0:T(8,128)(2,1)S(1)} %copy-done.6, ...), custom_call_target="tpu_custom_call" | custom-call | tf_op jit(solution)/shard_map/pallas_call | solution.py:315
  60.1 18.7 %all_to_all.11.refs_1_ = f32[32,4,1152]{2,1,0:T(4,128)S(1)} all-to-all(f32[32,4,1152]{2,1,0:T(4,128)S(1)} %shard_map.155), channel_id=1, replica_groups=mesh['gx'=4,'gy'=8] {'gy','gx'}, dimensions={0} | all-to-all | bytes 1179648 | tf_op jit(solution)/shard_map/all_to_all | solution.py:172
  78.7 0.0 copy-done.2
  78.7 0.8 shard_map.156
  79.5 0.1 collective-permute-start.7
  79.6 1.4 %collective-permute-start.8 = (f32[3,96,128]{2,1,0:T(8,128)S(1)}, f32[3,96,128]{2,1,0:T(8,128)S(1)}, u32[]{:S(2)}, u32[]{:S(2)}) collective-permute-start(f32[3,96,128]{2,1,0:T(8,128)S(1)} %get-tuple-element.30), channel_id=1, source_target_pairs={{0,16},{8,24},{16,0},{24,8},{1,17},{9,25},{17,1},{25,9},{2,18},{10... | collective-permute-start | bytes 442376 | tf_op jit(solution)/shard_map/ppermute | solution.py:815
  81.0 0.5 collective-permute-start.9
  81.4 3.7 %shard_map.151 = f32[384,384]{1,0:T(8,128)} custom-call(s32[1]{0:T(128)} %bitcast.refs_0_, f32[384,384]{1,0:T(8,128)} %refs_1_.3, f32[384,384]{1,0:T(8,128)} %refs_2_.6, f32[384,384]{1,0:T(8,128)} %refs_3_.7, f32[384,384]{1,0:T(8,128)} %refs_4_.6, s32[384,384]{1,0:T(8,128)} %refs_5_.5, f32[4,8,128]{2,1,0:T(8,128)} %copy-done.8, f32[4,8,128]{2,1,0:T(8,128)} %copy-done.11), custom_call_target="tpu_custom_call" | custom-call | tf_op jit(solution)/shard_map/pallas_call | solution.py:352
  85.2 0.0 collective-permute-done.7.refs_2_
  85.2 1.2 %collective-permute-done.8.refs_3_ = f32[3,96,128]{2,1,0:T(8,128)S(1)} collective-permute-done((f32[3,96,128]{2,1,0:T(8,128)S(1)}, f32[3,96,128]{2,1,0:T(8,128)S(1)}, u32[]{:S(2)}, u32[]{:S(2)}) %collective-permute-start.8) | collective-permute-done | bytes 147488 | tf_op jit(solution)/shard_map/ppermute | solution.py:815
  86.4 2.1 %collective-permute-done.9.refs_4_ = f32[3,96,128]{2,1,0:T(8,128)S(1)} collective-permute-done((f32[3,96,128]{2,1,0:T(8,128)S(1)}, f32[3,96,128]{2,1,0:T(8,128)S(1)}, u32[]{:S(2)}, u32[]{:S(2)}) %collective-permute-start.9) | collective-permute-done | bytes 147488 | tf_op jit(solution)/shard_map/ppermute | solution.py:815
  88.5 1.0 %shard_map.157 = f32[384,384]{1,0:T(8,128)} custom-call(s32[1]{0:T(128)} %bitcast.refs_0_, f32[3,96,128]{2,1,0:T(8,128)S(1)} %get-tuple-element.28.refs_1_, f32[3,96,128]{2,1,0:T(8,128)S(1)} %collective-permute-done.7.refs_2_, f32[3,96,128]{2,1,0:T(8,128)S(1)} %collective-permute-done.8.refs_3_, f32[3,96,128]{2,1,0:T(8,128)S(1)} %collective-permute-done.9.refs_4_), custom_call_target="tpu_custom_call" | custom-call | tf_op jit(solution)/shard_map/pallas_call | solution.py:809
  (7 shorter events, 0.0 us)
Async XLA Ops:
  3.0 8.5 %collective-permute-start = (f32[296,128]{1,0:T(8,128)}, f32[296,128]{1,0:T(8,128)S(1)}, u32[]{:S(2)}, u32[]{:S(2)}) collective-permute-start(f32[296,128]{1,0:T(8,128)} %get-tuple-element.18), channel_id=1, source_target_pairs={{0,8},{8,0},{16,24},{24,16},{1,9},{9,1},{17,25},{25,17},{2,10},{10... | collective-permute-start | bytes 454664 | tf_op jit(solution)/shard_map/ppermute | solution.py:815
  3.5 7.9 %collective-permute-start.1 = (f32[296,128]{1,0:T(8,128)}, f32[296,128]{1,0:T(8,128)S(1)}, u32[]{:S(2)}, u32[]{:S(2)}) collective-permute-start(f32[296,128]{1,0:T(8,128)} %get-tuple-element.19), channel_id=1, source_target_pairs={{0,16},{8,24},{16,0},{24,8},{1,17},{9,25},{17,1},{25,9},{2,18},{10... | collective-permute-start | bytes 454664 | tf_op jit(solution)/shard_map/ppermute | solution.py:815
  6.1 7.9 %copy-start.1 = (f32[296,128]{1,0:T(8,128)S(1)}, f32[296,128]{1,0:T(8,128)}, u32[]{:S(2)}) copy-start(f32[296,128]{1,0:T(8,128)} %get-tuple-element.17.refs_0_.refs_1_) | copy-start | bytes 454660
  6.1 11.3 %copy-start = (bf16[2,512,256]{2,1,0:T(8,128)(2,1)S(1)}, bf16[2,512,256]{2,1,0:T(8,128)(2,1)}, u32[]{:S(2)}) copy-start(bf16[2,512,256]{2,1,0:T(8,128)(2,1)} %constant.25.clone.refs_6_.refs_11_) | copy-start | bytes 1572868
  6.1 11.3 %copy-start.10 = (f32[2,6,128]{2,1,0:T(8,128)S(1)}, f32[2,6,128]{2,1,0:T(8,128)}, u32[]{:S(2)}) copy-start(f32[2,6,128]{2,1,0:T(8,128)} %constant.24.clone.refs_5_.refs_10_.refs_2_) | copy-start | bytes 18436
  6.1 7.9 %collective-permute-start.2 = (f32[296,128]{1,0:T(8,128)}, f32[296,128]{1,0:T(8,128)S(1)}, u32[]{:S(2)}, u32[]{:S(2)}) collective-permute-start(f32[296,128]{1,0:T(8,128)} %get-tuple-element.20), channel_id=1, source_target_pairs={{0,24},{8,16},{16,8},{24,0},{1,25},{9,17},{17,9},{25,1},{2,26},{10... | collective-permute-start | bytes 454664 | tf_op jit(solution)/shard_map/ppermute | solution.py:815
  9.4 10.9 %copy-start.7 = (f32[296,128]{1,0:T(8,128)S(1)}, f32[296,128]{1,0:T(8,128)}, u32[]{:S(2)}) copy-start(f32[296,128]{1,0:T(8,128)} %get-tuple-element.21.refs_1_) | copy-start | bytes 454660
  9.4 8.9 %collective-permute-start.4 = (f32[296,128]{1,0:T(8,128)}, f32[296,128]{1,0:T(8,128)S(1)}, u32[]{:S(2)}, u32[]{:S(2)}) collective-permute-start(f32[296,128]{1,0:T(8,128)} %get-tuple-element.22), channel_id=1, source_target_pairs={{0,8},{8,0},{16,24},{24,16},{1,9},{9,1},{17,25},{25,17},{2,10},{10... | collective-permute-start | bytes 454664 | tf_op jit(solution)/shard_map/ppermute | solution.py:815
  9.6 8.7 %collective-permute-start.5 = (f32[296,128]{1,0:T(8,128)}, f32[296,128]{1,0:T(8,128)S(1)}, u32[]{:S(2)}, u32[]{:S(2)}) collective-permute-start(f32[296,128]{1,0:T(8,128)} %get-tuple-element.23), channel_id=1, source_target_pairs={{0,16},{8,24},{16,0},{24,8},{1,17},{9,25},{17,1},{25,9},{2,18},{10... | collective-permute-start | bytes 454664 | tf_op jit(solution)/shard_map/ppermute | solution.py:815
  11.5 8.8 %collective-permute-start.6 = (f32[296,128]{1,0:T(8,128)}, f32[296,128]{1,0:T(8,128)S(1)}, u32[]{:S(2)}, u32[]{:S(2)}) collective-permute-start(f32[296,128]{1,0:T(8,128)} %get-tuple-element.24), channel_id=1, source_target_pairs={{0,24},{8,16},{16,8},{24,0},{1,25},{9,17},{17,9},{25,1},{2,26},{10... | collective-permute-start | bytes 454664 | tf_op jit(solution)/shard_map/ppermute | solution.py:815
  14.0 7.6 %copy-start.8 = (f32[4,8,128]{2,1,0:T(8,128)}, f32[4,8,128]{2,1,0:T(8,128)S(1)}, u32[]{:S(2)}) copy-start(f32[4,8,128]{2,1,0:T(8,128)S(1)} %shard_map.150.refs_6_.refs_5_) | copy-start | bytes 49156
  14.0 6.3 %collective-permute-start.3 = (f32[4,8,128]{2,1,0:T(8,128)S(1)}, f32[4,8,128]{2,1,0:T(8,128)S(1)}, u32[]{:S(2)}, u32[]{:S(2)}) collective-permute-start(f32[4,8,128]{2,1,0:T(8,128)S(1)} %shard_map.150.refs_6_.refs_5_), channel_id=1, source_target_pairs={{0,1},{1,2},{2,3},{3,4},{4,5},{5,6},{6,7},{8,9},{9,10},{10,11},{11... | collective-permute-start | bytes 49160 | tf_op jit(solution)/shard_map/ppermute | solution.py:178
  20.3 1.3 %copy-start.11 = (f32[4,8,128]{2,1,0:T(8,128)}, f32[4,8,128]{2,1,0:T(8,128)S(1)}, u32[]{:S(2)}) copy-start(f32[4,8,128]{2,1,0:T(8,128)S(1)} %collective-permute-done.3.refs_7_.refs_6_) | copy-start | bytes 49156
  21.6 36.3 %copy-start.3 = (bf16[512,256]{1,0:T(8,128)(2,1)S(1)}, bf16[512,256]{1,0:T(8,128)(2,1)}, u32[]{:S(2)}) copy-start(bf16[512,256]{1,0:T(8,128)(2,1)} %constant.26.clone.refs_3_) | copy-start | bytes 786436
  21.6 36.3 %copy-start.4 = (bf16[512,256]{1,0:T(8,128)(2,1)S(1)}, bf16[512,256]{1,0:T(8,128)(2,1)}, u32[]{:S(2)}) copy-start(bf16[512,256]{1,0:T(8,128)(2,1)} %constant.29.clone.refs_6_) | copy-start | bytes 786436
  21.6 36.2 %copy-start.5 = (bf16[384,192]{1,0:T(8,128)(2,1)S(1)}, bf16[384,192]{1,0:T(8,128)(2,1)}, u32[]{:S(2)}) copy-start(bf16[384,192]{1,0:T(8,128)(2,1)} %constant.27.clone.refs_4_) | copy-start | bytes 442372
  21.6 36.2 %copy-start.6 = (bf16[384,192]{1,0:T(8,128)(2,1)S(1)}, bf16[384,192]{1,0:T(8,128)(2,1)}, u32[]{:S(2)}) copy-start(bf16[384,192]{1,0:T(8,128)(2,1)} %constant.28.clone.refs_5_) | copy-start | bytes 442372
  21.6 36.2 %copy-start.9 = (f32[2,96,128]{2,1,0:T(8,128)S(1)}, f32[2,96,128]{2,1,0:T(8,128)}, u32[]{:S(2)}) copy-start(f32[2,96,128]{2,1,0:T(8,128)} %constant.30.clone.refs_7_) | copy-start | bytes 294916
  60.1 18.7 %copy-start.2 = (bf16[2,512,256]{2,1,0:T(8,128)(2,1)S(1)}, bf16[2,512,256]{2,1,0:T(8,128)(2,1)}, u32[]{:S(2)}) copy-start(bf16[2,512,256]{2,1,0:T(8,128)(2,1)} %constant.31.clone.refs_3_) | copy-start | bytes 1572868
  79.5 5.7 %collective-permute-start.7 = (f32[3,96,128]{2,1,0:T(8,128)S(1)}, f32[3,96,128]{2,1,0:T(8,128)S(1)}, u32[]{:S(2)}, u32[]{:S(2)}) collective-permute-start(f32[3,96,128]{2,1,0:T(8,128)S(1)} %get-tuple-element.29), channel_id=1, source_target_pairs={{0,8},{8,0},{16,24},{24,16},{1,9},{9,1},{17,25},{25,17},{2,10},{10... | collective-permute-start | bytes 442376 | tf_op jit(solution)/shard_map/ppermute | solution.py:815
  79.6 6.8 %collective-permute-start.8 = (f32[3,96,128]{2,1,0:T(8,128)S(1)}, f32[3,96,128]{2,1,0:T(8,128)S(1)}, u32[]{:S(2)}, u32[]{:S(2)}) collective-permute-start(f32[3,96,128]{2,1,0:T(8,128)S(1)} %get-tuple-element.30), channel_id=1, source_target_pairs={{0,16},{8,24},{16,0},{24,8},{1,17},{9,25},{17,1},{25,9},{2,18},{10... | collective-permute-start | bytes 442376 | tf_op jit(solution)/shard_map/ppermute | solution.py:815
  81.0 7.5 %collective-permute-start.9 = (f32[3,96,128]{2,1,0:T(8,128)S(1)}, f32[3,96,128]{2,1,0:T(8,128)S(1)}, u32[]{:S(2)}, u32[]{:S(2)}) collective-permute-start(f32[3,96,128]{2,1,0:T(8,128)S(1)} %get-tuple-element.31), channel_id=1, source_target_pairs={{0,24},{8,16},{16,8},{24,0},{1,25},{9,17},{17,9},{25,1},{2,26},{10... | collective-permute-start | bytes 442376 | tf_op jit(solution)/shard_map/ppermute | solution.py:815
